TPU v7x, 32 devices: a whole 2x2x4 slice. The times are simulated.
32 devices in a mesh: mat: 8 (over z, core), pts: 4 (over y, x).
Axes of the slice: x: 2, y: 2, z: 4, core: 2. Of those that a mesh axis runs over, the one named last changes fastest.
Arguments:
- dens_blocks: bfloat16 [8, 2048, 2048], P(None, 'pts', 'mat'), may hold values from -0.00390625 to 0.00390625
- basis_values: bfloat16 [8, 6144, 1536], P('mat', 'pts'), may hold values from -6 to 6
- kernel: float32 [8, 6144], P('mat', 'pts'), may hold values from 0.3 to 3
- perturbation: float32 [8, 6144], P('mat', 'pts'), may hold values from -6 to 6
- quad_weight: float32 [8, 6144], P('mat', 'pts'), may hold values from 0.002 to 0.02
- point_count: int32 [8, 4], P('mat', 'pts'), may hold values from 192 to 1536, as said below
- active_blocks: int32 [8, 4, 12], P('mat', 'pts'), may hold values from 0 to 15, as said below
- block_pattern: int32 [8, 16, 16], replicated, may hold values 0 or 1
Outputs:
- h_response: float32 [8, 2048, 2048], P(None, 'pts', 'mat')
- n_response: float32 [8, 6144], P('mat', 'pts')
Inputs may be any that keep to these rules, and one draw needn't show every extreme that they name: `point_count`: each cluster has at least one shard with exactly 1536 points in use; the others hold 192 or more. `active_blocks`: the 12 entries of one shard are distinct block numbers of its cluster, in no particular order.
All inputs are finite; a program needn't handle non-finite values.
Results may differ from a plain program's by a relative error of at most 0.011.
Values may be sent and summed in bfloat16 or wider, within the bound.
No kernel may reach another device: no remote copies, remote signals or barrier semaphores. Data moves between devices by JAX's collectives and lax.ppermute only.
A program may use at most 128 MiB of HBM per device.

v0:
```python
import functools

import jax
import jax.numpy as jnp
from jax import lax
from jax.experimental import pallas as pl
from jax.experimental.pallas import tpu as pltpu
from jax.sharding import PartitionSpec as P


BLOCK = 128
VM = pl.BlockSpec(memory_space=pltpu.VMEM)
ANY = pl.BlockSpec(memory_space=pl.ANY)
HEAD = 3
GRANT = pltpu.CompilerParams(vmem_limit_bytes=20 << 20)


def cost(flops, moved):
    return pl.CostEstimate(flops=int(flops), bytes_accessed=int(moved), transcendentals=0)


def lanes(block):
    return pl.ds(pl.multiple_of(block * BLOCK, BLOCK), BLOCK)


def rows_at(block):
    return pl.ds(pl.multiple_of(block * BLOCK, BLOCK), BLOCK)


def active_rows(dims, meta, o, column):
    _, n_pts, act, nact = dims
    out = []
    for r in range(act // n_pts):
        found = jnp.int32(0)
        for j in range(nact):
            found += (meta[HEAD + o * nact + j] == column * (act // n_pts) + r).astype(jnp.int32)
        out.append(found)
    return out


def ranked_row(flags, rank, from_end):
    row, passed = jnp.int32(-1), jnp.int32(0)
    order = range(len(flags) - 1, -1, -1) if from_end else range(len(flags))
    for r in order:
        row = jnp.where((flags[r] != 0) & (passed == rank), r, row)
        passed += flags[r]
    return row


def list_slots(dims, meta, table, o, column, row, lower, positions):
    _, n_pts, act, nact = dims
    each = act // n_pts
    base, filled = o * (nact + 1), jnp.int32(0)
    for j in range(nact + 1):
        table[base + j] = 0
    for j in range(nact):
        block = meta[HEAD + (0 if positions else o) * nact + j]
        local = block - column * each
        kept = (local < 0) | (local >= each) | ((local <= row) if lower else (local >= row))
        table[base + filled] = j if positions else block
        filled += kept.astype(jnp.int32)


def slots_in(dims, k):
    return dims[3] - dims[2] // dims[1] + 1 + k


def slots_out(dims, k):
    return dims[3] - k


def pack_kernel(dims, k, meta, *refs):
    n_mat, n_pts, act, nact = dims
    each = act // n_pts
    arrived, earlier = refs[:n_mat], refs[n_mat : n_mat + k]
    stage, packed, table = refs[n_mat + k], refs[n_mat + k + 1 : -1], refs[-1]
    width = arrived[0].shape[1]
    me_pts = meta[1]
    pattern_at = HEAD + n_pts * nact + (me_pts * each + k) * act
    for d in range(n_mat):
        m = meta[0] ^ d
        for c in range(width // BLOCK):
            b = m * (width // BLOCK) + c
            value = arrived[d][:, c * BLOCK : (c + 1) * BLOCK]
            stage[:, lanes(b)] = jnp.where(meta[pattern_at + b] != 0, value, jnp.zeros_like(value))
    for r in range(k):
        mine, other = me_pts * each + r, me_pts * each + k
        pair = stage[:, lanes(mine)].astype(jnp.float32) + earlier[r][:, lanes(other)].astype(jnp.float32).T
        stage[:, lanes(mine)] = pair.astype(jnp.bfloat16)
    for o in range(n_pts):
        flags = active_rows(dims, meta, o, me_pts)
        row = jnp.maximum(ranked_row(flags, each - 1 - k, True), 0)
        list_slots(dims, meta, table, o, me_pts, row, True, False)
        for r in range(k + 1):
            source = stage if r == k else earlier[r]

            @pl.when(row == r)
            def _(source=source, o=o):
                for slot in range(slots_in(dims, k)):
                    b = table[o * (nact + 1) + slot]
                    packed[o][:, slot * BLOCK : (slot + 1) * BLOCK] = source[:, lanes(b)]


def pack(dims, k, meta, arrived, earlier):
    n_mat, n_pts, act, nact = dims
    shapes = [jax.ShapeDtypeStruct((BLOCK, act * BLOCK), jnp.bfloat16)]
    shapes += [jax.ShapeDtypeStruct((BLOCK, slots_in(dims, k) * BLOCK), jnp.bfloat16)] * n_pts
    out = pl.pallas_call(
        functools.partial(pack_kernel, dims, k),
        out_shape=shapes,
        in_specs=[pl.BlockSpec(memory_space=pltpu.SMEM)] + [VM] * (n_mat + k),
        out_specs=[VM] * len(shapes),
        scratch_shapes=[pltpu.SMEM((n_pts * (nact + 1),), jnp.int32)],
        compiler_params=GRANT,
        cost_estimate=cost(0, 2 * BLOCK * BLOCK * (act + n_pts * nact)),
    )(meta, *arrived, *earlier)
    return out[0], out[1:]


def transpose_kernel(given, out):
    out[...] = given[...].T


def transposed(basis):
    points, orbitals = basis.shape
    tile = 256
    return pl.pallas_call(
        transpose_kernel,
        out_shape=jax.ShapeDtypeStruct((orbitals, points), basis.dtype),
        grid=(points // tile,),
        in_specs=[pl.BlockSpec((tile, orbitals), lambda i: (i, 0))],
        out_specs=pl.BlockSpec((orbitals, tile), lambda i: (0, i)),
        compiler_params=GRANT,
        cost_estimate=cost(0, 4 * points * orbitals),
        name="flip",
    )(basis)


def invert(dims, meta, place):
    _, _, act, nact = dims
    for a in range(act):
        place[a] = -1
    for i in range(nact):
        place[meta[HEAD + i]] = i


def density_kernel(dims, k, tile, last, meta, *refs):
    _, n_pts, act, nact = dims
    each = act // n_pts
    parts, flipped, before, after, place, table, left = refs[:n_pts], *refs[n_pts:]
    invert(dims, meta, place)
    points = flipped.shape[1]
    rows = []
    left[...] = jnp.zeros_like(left)
    for o in range(n_pts):
        column = meta[1] ^ o
        row = ranked_row(active_rows(dims, meta, 0, column), each - 1 - k, True)
        list_slots(dims, meta, table, o, column, jnp.maximum(row, 0), True, True)
        rows.append((jnp.maximum(place[column * each + jnp.maximum(row, 0)], 0), row >= 0))
        for slot in range(slots_in(dims, k)):
            j = table[o * (nact + 1) + slot]
            left[o * BLOCK : (o + 1) * BLOCK, lanes(j)] = parts[o][:, slot * BLOCK : (slot + 1) * BLOCK]

    @pl.loop(0, points // tile)
    def _(t):
        at = pl.ds(pl.multiple_of(t * tile, tile), tile)
        inner = jnp.dot(left[...], flipped[:, at], preferred_element_type=jnp.float32)
        total = before[:, at]
        for o, (spot, valid) in enumerate(rows):
            own = flipped[rows_at(spot), at].astype(jnp.float32)
            share = jnp.sum(inner[o * BLOCK : (o + 1) * BLOCK] * own, axis=0, keepdims=True)
            total = total + jnp.where(valid, share, jnp.zeros_like(share))
        if last:
            point = t * tile + lax.broadcasted_iota(jnp.int32, total.shape, 1)
            total = jnp.where(point < meta[2], total, jnp.zeros_like(total))
        after[:, at] = total


def density(dims, k, last, meta, parts, flipped, before):
    _, n_pts, act, nact = dims
    orbitals, points = flipped.shape
    return pl.pallas_call(
        functools.partial(density_kernel, dims, k, 256, last),
        out_shape=jax.ShapeDtypeStruct((1, points), jnp.float32),
        in_specs=[pl.BlockSpec(memory_space=pltpu.SMEM)] + [VM] * (n_pts + 2),
        out_specs=VM,
        scratch_shapes=[
            pltpu.SMEM((act,), jnp.int32),
            pltpu.SMEM((n_pts * (nact + 1),), jnp.int32),
            pltpu.VMEM((n_pts * BLOCK, orbitals), jnp.bfloat16),
        ],
        compiler_params=GRANT,
        cost_estimate=cost(2 * n_pts * BLOCK * orbitals * points, 2 * orbitals * points),
    )(meta, *parts, flipped, before)


def response_kernel(dims, k, tile, meta, *refs):
    _, n_pts, act, nact = dims
    each = act // n_pts
    flipped, basis, n, kern, pert, weight = refs[:6]
    out, (place, table, left, right) = refs[6 : 6 + n_pts], refs[6 + n_pts :]
    invert(dims, meta, place)
    points = flipped.shape[1]
    inside = lax.broadcasted_iota(jnp.int32, (1, points), 1) < meta[2]
    scaling = jnp.where(inside, weight[...] * (pert[...] - kern[...] * n[...]), 0.0)
    for o in range(n_pts):
        column = meta[1] ^ o
        row = ranked_row(active_rows(dims, meta, 0, column), k, False)
        list_slots(dims, meta, table, o, column, jnp.maximum(row, 0), False, True)
        spot = jnp.maximum(place[column * each + jnp.maximum(row, 0)], 0)
        own = flipped[rows_at(spot), :].astype(jnp.float32)
        left[o * BLOCK : (o + 1) * BLOCK, :] = jnp.where(row >= 0, own * scaling, 0.0).astype(jnp.bfloat16)

    @pl.loop(0, basis.shape[1] // tile)
    def _(t):
        at = pl.ds(pl.multiple_of(t * tile, tile), tile)
        right[:, at] = jnp.dot(left[...], basis[:, at], preferred_element_type=jnp.float32).astype(jnp.bfloat16)

    for o in range(n_pts):
        for slot in range(slots_out(dims, k)):
            j = table[o * (nact + 1) + slot]
            out[o][:, slot * BLOCK : (slot + 1) * BLOCK] = right[o * BLOCK : (o + 1) * BLOCK, lanes(j)]


def response(dims, k, meta, flipped, basis, n, kern, pert, weight):
    _, n_pts, act, nact = dims
    orbitals, points = flipped.shape
    return pl.pallas_call(
        functools.partial(response_kernel, dims, k, 256),
        out_shape=[jax.ShapeDtypeStruct((BLOCK, slots_out(dims, k) * BLOCK), jnp.bfloat16)] * n_pts,
        in_specs=[pl.BlockSpec(memory_space=pltpu.SMEM)] + [VM] * 6,
        out_specs=[VM] * n_pts,
        scratch_shapes=[
            pltpu.SMEM((act,), jnp.int32),
            pltpu.SMEM((n_pts * (nact + 1),), jnp.int32),
            pltpu.VMEM((n_pts * BLOCK, points), jnp.bfloat16),
            pltpu.VMEM((n_pts * BLOCK, orbitals), jnp.bfloat16),
        ],
        compiler_params=GRANT,
        cost_estimate=cost(2 * n_pts * BLOCK * orbitals * points, 4 * orbitals * points),
    )(meta, flipped, basis, n, kern, pert, weight)


def combine_kernel(dims, k, meta, *refs):
    n_mat, n_pts, act, nact = dims
    each = act // n_pts
    strips, before = refs[: (k + 1) * n_pts], refs[(k + 1) * n_pts : (k + 1) * n_pts + k]
    out, (inner, total, table, held, sem) = refs[(k + 1) * n_pts + k : -5], refs[-5:]
    me_pts = meta[1]
    first = me_pts * each
    ranks = []
    for o in range(n_pts):
        flags = active_rows(dims, meta, o, me_pts)
        ranks.append(jnp.where(flags[k] != 0, sum(flags[:k], jnp.int32(0)), -1))
        for i in range(k + 1):

            @pl.when(ranks[o] == i)
            def _(o=o, i=i):
                filled = slots_out(dims, i) * BLOCK
                pltpu.make_async_copy(strips[i * n_pts + o], held.at[o, :, :filled], sem.at[o]).start()

        list_slots(dims, meta, table, o, me_pts, jnp.int32(k), False, False)
    total[...] = jnp.zeros_like(total)
    for o in range(n_pts):
        for i in range(k + 1):

            @pl.when(ranks[o] == i)
            def _(o=o, i=i):
                filled = slots_out(dims, i) * BLOCK
                pltpu.make_async_copy(strips[i * n_pts + o], held.at[o, :, :filled], sem.at[o]).wait()
                for slot in range(slots_out(dims, i)):
                    b = table[o * (nact + 1) + slot]
                    part = held[o, :, slot * BLOCK : (slot + 1) * BLOCK].astype(jnp.float32)
                    total[:, lanes(b)] += part

    for r in range(k):
        total[:, lanes(first + r)] = before[r][:, k * BLOCK : (k + 1) * BLOCK].T
    for r in range(each):
        inner[:, r * BLOCK : (r + 1) * BLOCK] = total[:, lanes(first + r)]
    width = act // n_mat
    pattern_at = HEAD + n_pts * nact + (first + k) * act
    for d in range(n_mat):
        for c in range(width):
            b = (meta[0] ^ d) * width + c
            value = total[:, lanes(b)]
            value = jnp.where(meta[pattern_at + b] != 0, value, jnp.zeros_like(value))
            out[d][:, c * BLOCK : (c + 1) * BLOCK] = value.astype(jnp.bfloat16)


def combine(dims, k, meta, strips, before):
    n_mat, n_pts, act, nact = dims
    shapes = [jax.ShapeDtypeStruct((BLOCK, act // n_mat * BLOCK), jnp.bfloat16)] * n_mat
    shapes += [jax.ShapeDtypeStruct((BLOCK, act // n_pts * BLOCK), jnp.float32)]
    given = sum(strips, [])
    out = pl.pallas_call(
        functools.partial(combine_kernel, dims, k),
        out_shape=shapes,
        in_specs=[pl.BlockSpec(memory_space=pltpu.SMEM)] + [ANY] * len(given) + [VM] * k,
        out_specs=[VM] * len(shapes),
        scratch_shapes=[
            pltpu.VMEM((BLOCK, act * BLOCK), jnp.float32),
            pltpu.SMEM((n_pts * (nact + 1),), jnp.int32),
            pltpu.VMEM((n_pts, BLOCK, nact * BLOCK), jnp.bfloat16),
            pltpu.SemaphoreType.DMA((n_pts,)),
        ],
        compiler_params=GRANT,
        cost_estimate=cost(0, 2 * BLOCK * BLOCK * (act + n_pts * nact)),
    )(meta, *given, *before)
    return out[:-1], out[-1]


def widen_kernel(n_mat, meta, *refs):
    out = refs[-1]
    for d in range(n_mat):
        out[meta[0] ^ d] = refs[d][...].astype(jnp.float32)


def widen(dims, start, rows, all_rows, meta, given, held):
    n_mat, _, act, _ = dims
    width = act // n_mat * BLOCK
    more = [] if held is None else [held]
    return pl.pallas_call(
        functools.partial(widen_kernel, n_mat),
        out_shape=jax.ShapeDtypeStruct((n_mat, all_rows, width), jnp.float32),
        grid_spec=pltpu.PrefetchScalarGridSpec(
            num_scalar_prefetch=1,
            grid=(1,),
            in_specs=[pl.BlockSpec((rows, width), lambda i, meta: (0, 0))] * n_mat + [ANY] * len(more),
            out_specs=pl.BlockSpec((n_mat, rows, width), lambda i, meta: (0, start // rows, 0)),
        ),
        input_output_aliases={} if held is None else {1 + n_mat: 0},
        compiler_params=GRANT,
        cost_estimate=cost(0, 6 * rows * n_mat * width),
    )(meta, *given, *more)


def body(dens_blocks, basis_values, kernel, perturbation, quad_weight, point_count, active_blocks, block_pattern):
    n_mat, n_pts = lax.axis_size("mat"), lax.axis_size("pts")
    act, nact = block_pattern.shape[1], active_blocks.shape[2]
    dims = (n_mat, n_pts, act, nact)
    row_blocks = act // n_pts
    me_mat, me_pts = lax.axis_index("mat"), lax.axis_index("pts")

    def to_peer(value, o):
        return lax.ppermute(value, "pts", [(i, i ^ o) for i in range(n_pts)])

    points = basis_values.shape[1]
    basis = basis_values[0]
    own_active = active_blocks[0, 0]

    def across(values):
        out = [values[0]] + [None] * (n_mat - 1)
        for d in range(n_mat - 1, 0, -1):
            out[d] = lax.ppermute(values[d], "mat", [(i, i ^ d) for i in range(n_mat)])
        return out

    arrived = []
    for k in range(row_blocks):
        cut = [
            lax.dynamic_slice(dens_blocks, (me_mat ^ d, k * BLOCK, 0), (1, BLOCK, dens_blocks.shape[2]))[0]
            for d in range(n_mat)
        ]
        arrived.append(across(cut))

    peers = [own_active] + [to_peer(own_active, o) for o in range(1, n_pts)]
    pattern = lax.dynamic_index_in_dim(block_pattern, me_mat, 0, keepdims=False).reshape(-1)
    head = jnp.stack([me_mat, me_pts, point_count[0, 0]]).astype(jnp.int32)
    meta = jnp.concatenate([head] + peers + [pattern])

    flipped = transposed(basis)

    parts, stages = [], []
    for k in range(row_blocks):
        held, packed = pack(dims, k, meta, arrived[k], stages)
        stages.append(held)
        parts.append([packed[0]] + [to_peer(packed[o], o) for o in range(1, n_pts)])

    n = jnp.zeros((1, points), jnp.float32)
    for k in range(row_blocks):
        n = density(dims, k, k == row_blocks - 1, meta, parts[k], flipped, n)

    strips = []
    for k in range(row_blocks):
        sent = response(dims, k, meta, flipped, basis, n, kernel, perturbation, quad_weight)
        strips.append([sent[0]] + [to_peer(sent[o], o) for o in range(1, n_pts)])

    inner, result = [], None
    for k in range(row_blocks):
        cut, pairs = combine(dims, k, meta, strips[: k + 1], inner)
        inner.append(pairs)
        back = across(cut)
        result = widen(dims, k * BLOCK, BLOCK, dens_blocks.shape[1], meta, back, result)
    return result, n


def solution(mesh):
    placed = (
        P(None, "pts", "mat"),
        P("mat", "pts", None),
        P("mat", "pts"),
        P("mat", "pts"),
        P("mat", "pts"),
        P("mat", "pts"),
        P("mat", "pts", None),
        P(),
    )

    return jax.shard_map(
        body,
        mesh=mesh,
        in_specs=placed,
        out_specs=(P(None, "pts", "mat"), P("mat", "pts")),
        check_vma=False,
    )
```

profile of v0, /device:TPU:0, one launch (start us, length us, event | category | flops | bytes accessed | tf_op | source)
XLA Modules:
  0.0 256.2 jit_solution(18380450801680809510)
XLA Ops:
  2.5 4.6 %collective-permute-start.30 = (bf16[128,256]{1,0:T(8,128)(2,1)S(1)}, bf16[128,256]{1,0:T(8,128)(2,1)S(1)}, u32[]{:S(2)}, u32[]{:S(2)}) collective-permute-start(bf16[128,256]{1,0:T(8,128)(2,1)S(1)} %get-tuple-element.142), channel_id=1, source_target_pairs={{0,28},{4,24},{8,20},{12,16},{16,12},{20,8},{24,4},{28,0},{1,29},{... | collective-permute-start | bytes 196616 | tf_op jit(solution)/shard_map/ppermute | solution.py:354
  7.1 2.4 collective-permute-start.2
  11.6 3.2 %collective-permute-start.27 = (bf16[128,256]{1,0:T(8,128)(2,1)S(1)}, bf16[128,256]{1,0:T(8,128)(2,1)S(1)}, u32[]{:S(2)}, u32[]{:S(2)}) collective-permute-start(bf16[128,256]{1,0:T(8,128)(2,1)S(1)} %get-tuple-element.144), channel_id=1, source_target_pairs={{0,16},{4,20},{8,24},{12,28},{16,0},{20,4},{24,8},{28,12},{1,17},{... | collective-permute-start | bytes 196616 | tf_op jit(solution)/shard_map/ppermute | solution.py:354
  20.2 2.7 %collective-permute-start.20 = (bf16[128,256]{1,0:T(8,128)(2,1)S(1)}, bf16[128,256]{1,0:T(8,128)(2,1)S(1)}, u32[]{:S(2)}, u32[]{:S(2)}) collective-permute-start(bf16[128,256]{1,0:T(8,128)(2,1)S(1)} %get-tuple-element.152), channel_id=1, source_target_pairs={{0,16},{4,20},{8,24},{12,28},{16,0},{20,4},{24,8},{28,12},{1,17},{... | collective-permute-start | bytes 196616 | tf_op jit(solution)/shard_map/ppermute | solution.py:354
  26.3 5.5 %collective-permute-start.14 = (bf16[128,256]{1,0:T(8,128)(2,1)S(1)}, bf16[128,256]{1,0:T(8,128)(2,1)S(1)}, u32[]{:S(2)}, u32[]{:S(2)}) collective-permute-start(bf16[128,256]{1,0:T(8,128)(2,1)S(1)} %get-tuple-element.159), channel_id=1, source_target_pairs={{0,20},{4,16},{8,28},{12,24},{16,4},{20,0},{24,12},{28,8},{1,21},{... | collective-permute-start | bytes 196616 | tf_op jit(solution)/shard_map/ppermute | solution.py:354
  34.8 2.8 %collective-permute-start.11 = (bf16[128,256]{1,0:T(8,128)(2,1)S(1)}, bf16[128,256]{1,0:T(8,128)(2,1)S(1)}, u32[]{:S(2)}, u32[]{:S(2)}) collective-permute-start(bf16[128,256]{1,0:T(8,128)(2,1)S(1)} %get-tuple-element.162), channel_id=1, source_target_pairs={{0,8},{4,12},{8,0},{12,4},{16,24},{20,28},{24,16},{28,20},{1,9},{5... | collective-permute-start | bytes 196616 | tf_op jit(solution)/shard_map/ppermute | solution.py:354
  42.7 2.4 collective-permute-start.9
  62.4 4.2 %collective-permute-done.29.refs_6_ = bf16[128,256]{1,0:T(8,128)(2,1)S(1)} collective-permute-done((bf16[128,256]{1,0:T(8,128)(2,1)S(1)}, bf16[128,256]{1,0:T(8,128)(2,1)S(1)}, u32[]{:S(2)}, u32[]{:S(2)}) %collective-permute-start.29) | collective-permute-done | bytes 65568 | tf_op jit(solution)/shard_map/ppermute | solution.py:354
  71.8 2.3 copy-done.1
  76.1 2.7 %shard_map.98 = (bf16[128,2048]{1,0:T(8,128)(2,1)}, bf16[128,1536]{1,0:T(8,128)(2,1)S(1)}, bf16[128,1536]{1,0:T(8,128)(2,1)S(1)}, bf16[128,1536]{1,0:T(8,128)(2,1)S(1)}, bf16[128,1536]{1,0:T(8,128)(2,1)S(1)}) custom-call(s32[307]{0:T(512)S(1)} %concatenate.3.meta, bf16[128,256]{1,0:T(8,128)(2,1)S(1)} %get-tuple-element.172.refs_0_, ...), custom_call_target="tpu_custom_call" | custom-call | bytes 2097152 | tf_op jit(solution)/shard_map/pallas_call | solution.py:108
  81.9 4.7 %shard_map.99.refs_5_ = f32[1,1536]{1,0:T(1,128)S(1)} custom-call(s32[307]{0:T(512)S(1)} %concatenate.3.meta, bf16[128,1152]{1,0:T(8,128)(2,1)S(1)} %get-tuple-element.87.refs_0_, bf16[128,1152]{1,0:T(8,128)(2,1)S(1)} %collective-permute-done.40.refs_1_, bf16[128,1152]{1,0:T(8,128)(2,1)S(1)} %collective-permute-done.41.refs_2_, ...), custom_call_target="tpu_custom_call" | custom-call | flops 2415919104 | bytes 4718592 | tf_op jit(solution)/shard_map/pallas_call | solution.py:182
  87.1 2.8 %collective-permute-done.39.refs_3_ = bf16[128,1280]{1,0:T(8,128)(2,1)S(1)} collective-permute-done((bf16[128,1280]{1,0:T(8,128)(2,1)S(1)}, bf16[128,1280]{1,0:T(8,128)(2,1)S(1)}, u32[]{:S(2)}, u32[]{:S(2)}) %collective-permute-start.39) | collective-permute-done | bytes 327712 | tf_op jit(solution)/shard_map/ppermute | solution.py:345
  93.5 4.8 %shard_map.100.refs_5_ = f32[1,1536]{1,0:T(1,128)S(1)} custom-call(s32[307]{0:T(512)S(1)} %concatenate.3.meta, bf16[128,1280]{1,0:T(8,128)(2,1)S(1)} %get-tuple-element.83.refs_0_, bf16[128,1280]{1,0:T(8,128)(2,1)S(1)} %collective-permute-done.37.refs_1_, bf16[128,1280]{1,0:T(8,128)(2,1)S(1)} %collective-permute-done.38.refs_2_, ...), custom_call_target="tpu_custom_call" | custom-call | flops 2415919104 | bytes 4718592 | tf_op jit(solution)/shard_map/pallas_call | solution.py:182
  98.2 6.1 %collective-permute-done.35.refs_2_ = bf16[128,1408]{1,0:T(8,128)(2,1)S(1)} collective-permute-done((bf16[128,1408]{1,0:T(8,128)(2,1)S(1)}, bf16[128,1408]{1,0:T(8,128)(2,1)S(1)}, u32[]{:S(2)}, u32[]{:S(2)}) %collective-permute-start.35) | collective-permute-done | bytes 360480 | tf_op jit(solution)/shard_map/ppermute | solution.py:345
  104.3 4.8 %shard_map.101.refs_5_ = f32[1,1536]{1,0:T(1,128)S(1)} custom-call(s32[307]{0:T(512)S(1)} %concatenate.3.meta, bf16[128,1408]{1,0:T(8,128)(2,1)S(1)} %get-tuple-element.79.refs_0_, bf16[128,1408]{1,0:T(8,128)(2,1)S(1)} %collective-permute-done.34.refs_1_, bf16[128,1408]{1,0:T(8,128)(2,1)S(1)} %collective-permute-done.35.refs_2_, ...), custom_call_target="tpu_custom_call" | custom-call | flops 2415919104 | bytes 4718592 | tf_op jit(solution)/shard_map/pallas_call | solution.py:182
  109.1 11.6 %collective-permute-done.32.refs_2_ = bf16[128,1536]{1,0:T(8,128)(2,1)S(1)} collective-permute-done((bf16[128,1536]{1,0:T(8,128)(2,1)S(1)}, bf16[128,1536]{1,0:T(8,128)(2,1)S(1)}, u32[]{:S(2)}, u32[]{:S(2)}) %collective-permute-start.32) | collective-permute-done | bytes 393248 | tf_op jit(solution)/shard_map/ppermute | solution.py:345
  120.7 5.4 %shard_map.102.refs_2_ = f32[1,1536]{1,0:T(1,128)} custom-call(s32[307]{0:T(512)S(1)} %concatenate.3.meta, bf16[128,1536]{1,0:T(8,128)(2,1)S(1)} %get-tuple-element.75.refs_0_, bf16[128,1536]{1,0:T(8,128)(2,1)S(1)} %collective-permute-done.31.refs_1_, bf16[128,1536]{1,0:T(8,128)(2,1)S(1)} %collective-permute-done.32.refs_2_, ...), custom_call_target="tpu_custom_call" | custom-call | flops 2415919104 | bytes 4718592 | tf_op jit(solution)/shard_map/pallas_call | solution.py:182
  126.9 4.8 %shard_map.106 = (bf16[128,1152]{1,0:T(8,128)(2,1)S(1)}, bf16[128,1152]{1,0:T(8,128)(2,1)S(1)}, bf16[128,1152]{1,0:T(8,128)(2,1)S(1)}, bf16[128,1152]{1,0:T(8,128)(2,1)S(1)}) custom-call(s32[307]{0:T(512)S(1)} %concatenate.3.meta, bf16[1536,1536]{1,0:T(8,128)(2,1)S(1)} %flip.1.refs_4_.refs_0_, bf16[1536,1536]{1,0:T(8,128)(2,1)S(1)} %bitcast.73, ...), custom_call_target="tpu_custom_call" | custom-call | flops 2415919104 | bytes 9437184 | tf_op jit(solution)/shard_map/pallas_call | solution.py:228
  133.5 4.9 %shard_map.103 = (bf16[128,1536]{1,0:T(8,128)(2,1)S(1)}, bf16[128,1536]{1,0:T(8,128)(2,1)S(1)}, bf16[128,1536]{1,0:T(8,128)(2,1)S(1)}, bf16[128,1536]{1,0:T(8,128)(2,1)S(1)}) custom-call(s32[307]{0:T(512)S(1)} %concatenate.3.meta, bf16[1536,1536]{1,0:T(8,128)(2,1)S(1)} %flip.1.refs_4_.refs_0_, bf16[1536,1536]{1,0:T(8,128)(2,1)S(1)} %bitcast.74, ...), custom_call_target="tpu_custom_call" | custom-call | flops 2415919104 | bytes 9437184 | tf_op jit(solution)/shard_map/pallas_call | solution.py:228
  139.6 4.8 %shard_map.105 = (bf16[128,1280]{1,0:T(8,128)(2,1)S(1)}, bf16[128,1280]{1,0:T(8,128)(2,1)S(1)}, bf16[128,1280]{1,0:T(8,128)(2,1)S(1)}, bf16[128,1280]{1,0:T(8,128)(2,1)S(1)}) custom-call(s32[307]{0:T(512)S(1)} %concatenate.3.meta, bf16[1536,1536]{1,0:T(8,128)(2,1)S(1)} %flip.1.refs_4_.refs_0_, bf16[1536,1536]{1,0:T(8,128)(2,1)S(1)} %bitcast.75, ...), custom_call_target="tpu_custom_call" | custom-call | flops 2415919104 | bytes 9437184 | tf_op jit(solution)/shard_map/pallas_call | solution.py:228
  147.9 2.3 collective-permute-start.54
  150.2 4.8 %shard_map.104 = (bf16[128,1408]{1,0:T(8,128)(2,1)S(1)}, bf16[128,1408]{1,0:T(8,128)(2,1)S(1)}, bf16[128,1408]{1,0:T(8,128)(2,1)S(1)}, bf16[128,1408]{1,0:T(8,128)(2,1)S(1)}) custom-call(s32[307]{0:T(512)S(1)} %concatenate.3.meta, bf16[1536,1536]{1,0:T(8,128)(2,1)S(1)} %flip.1.refs_4_.refs_0_, bf16[1536,1536]{1,0:T(8,128)(2,1)S(1)} %bitcast.76, ...), custom_call_target="tpu_custom_call" | custom-call | flops 2415919104 | bytes 9437184 | tf_op jit(solution)/shard_map/pallas_call | solution.py:228
  155.1 16.8 %collective-permute-done.54.refs_15_ = bf16[128,1152]{1,0:T(8,128)(2,1)S(1)} collective-permute-done((bf16[128,1152]{1,0:T(8,128)(2,1)S(1)}, bf16[128,1152]{1,0:T(8,128)(2,1)S(1)}, u32[]{:S(2)}, u32[]{:S(2)}) %collective-permute-start.54) | collective-permute-done | bytes 294944 | tf_op jit(solution)/shard_map/ppermute | solution.py:345
  179.2 4.0 %collective-permute-done.46.refs_5_ = bf16[128,1408]{1,0:T(8,128)(2,1)S(1)} collective-permute-done((bf16[128,1408]{1,0:T(8,128)(2,1)S(1)}, bf16[128,1408]{1,0:T(8,128)(2,1)S(1)}, u32[]{:S(2)}, u32[]{:S(2)}) %collective-permute-start.46) | collective-permute-done | bytes 360480 | tf_op jit(solution)/shard_map/ppermute | solution.py:345
  183.2 15.1 %collective-permute-done.47.refs_6_ = bf16[128,1408]{1,0:T(8,128)(2,1)S(1)} collective-permute-done((bf16[128,1408]{1,0:T(8,128)(2,1)S(1)}, bf16[128,1408]{1,0:T(8,128)(2,1)S(1)}, u32[]{:S(2)}, u32[]{:S(2)}) %collective-permute-start.47) | collective-permute-done | bytes 360480 | tf_op jit(solution)/shard_map/ppermute | solution.py:345
  206.4 2.9 %collective-permute-start.82 = (bf16[128,256]{1,0:T(8,128)(2,1)S(1)}, bf16[128,256]{1,0:T(8,128)(2,1)S(1)}, u32[]{:S(2)}, u32[]{:S(2)}) collective-permute-start(bf16[128,256]{1,0:T(8,128)(2,1)S(1)} %get-tuple-element.141), channel_id=1, source_target_pairs={{0,28},{4,24},{8,20},{12,16},{16,12},{20,8},{24,4},{28,0},{1,29},{... | collective-permute-start | bytes 196616 | tf_op jit(solution)/shard_map/ppermute | solution.py:354
  209.3 4.7 %collective-permute-done.79.refs_4_ = bf16[128,256]{1,0:T(8,128)(2,1)S(1)} collective-permute-done((bf16[128,256]{1,0:T(8,128)(2,1)S(1)}, bf16[128,256]{1,0:T(8,128)(2,1)S(1)}, u32[]{:S(2)}, u32[]{:S(2)}) %collective-permute-start.79) | collective-permute-done | bytes 65568 | tf_op jit(solution)/shard_map/ppermute | solution.py:354
  222.5 2.5 shard_map.110
  228.7 2.5 collective-permute-done.75.refs_7_
  233.1 2.4 collective-permute-start.67
  237.5 4.8 %collective-permute-done.65.refs_4_ = bf16[128,256]{1,0:T(8,128)(2,1)S(1)} collective-permute-done((bf16[128,256]{1,0:T(8,128)(2,1)S(1)}, bf16[128,256]{1,0:T(8,128)(2,1)S(1)}, u32[]{:S(2)}, u32[]{:S(2)}) %collective-permute-start.65) | collective-permute-done | bytes 65568 | tf_op jit(solution)/shard_map/ppermute | solution.py:354
  245.7 2.7 %collective-permute-start.61 = (bf16[128,256]{1,0:T(8,128)(2,1)S(1)}, bf16[128,256]{1,0:T(8,128)(2,1)S(1)}, u32[]{:S(2)}, u32[]{:S(2)}) collective-permute-start(bf16[128,256]{1,0:T(8,128)(2,1)S(1)} %get-tuple-element.117), channel_id=1, source_target_pairs={{0,28},{4,24},{8,20},{12,16},{16,12},{20,8},{24,4},{28,0},{1,29},{... | collective-permute-start | bytes 196616 | tf_op jit(solution)/shard_map/ppermute | solution.py:354
  (179 shorter events, 101.7 us)
Async XLA Ops:
  2.5 12.6 %collective-permute-start.30 = (bf16[128,256]{1,0:T(8,128)(2,1)S(1)}, bf16[128,256]{1,0:T(8,128)(2,1)S(1)}, u32[]{:S(2)}, u32[]{:S(2)}) collective-permute-start(bf16[128,256]{1,0:T(8,128)(2,1)S(1)} %get-tuple-element.142), channel_id=1, source_target_pairs={{0,28},{4,24},{8,20},{12,16},{16,12},{20,8},{24,4},{28,0},{1,29},{... | collective-permute-start | bytes 196616 | tf_op jit(solution)/shard_map/ppermute | solution.py:354
  20.1 11.7 %collective-permute-start.21 = (bf16[128,256]{1,0:T(8,128)(2,1)S(1)}, bf16[128,256]{1,0:T(8,128)(2,1)S(1)}, u32[]{:S(2)}, u32[]{:S(2)}) collective-permute-start(bf16[128,256]{1,0:T(8,128)(2,1)S(1)} %get-tuple-element.151), channel_id=1, source_target_pairs={{0,20},{4,16},{8,28},{12,24},{16,4},{20,0},{24,12},{28,8},{1,21},{... | collective-permute-start | bytes 196616 | tf_op jit(solution)/shard_map/ppermute | solution.py:354
  20.2 14.6 %collective-permute-start.20 = (bf16[128,256]{1,0:T(8,128)(2,1)S(1)}, bf16[128,256]{1,0:T(8,128)(2,1)S(1)}, u32[]{:S(2)}, u32[]{:S(2)}) collective-permute-start(bf16[128,256]{1,0:T(8,128)(2,1)S(1)} %get-tuple-element.152), channel_id=1, source_target_pairs={{0,16},{4,20},{8,24},{12,28},{16,0},{20,4},{24,8},{28,12},{1,17},{... | collective-permute-start | bytes 196616 | tf_op jit(solution)/shard_map/ppermute | solution.py:354
  22.8 12.0 %collective-permute-start.16 = (bf16[128,256]{1,0:T(8,128)(2,1)S(1)}, bf16[128,256]{1,0:T(8,128)(2,1)S(1)}, u32[]{:S(2)}, u32[]{:S(2)}) collective-permute-start(bf16[128,256]{1,0:T(8,128)(2,1)S(1)} %get-tuple-element.157), channel_id=1, source_target_pairs={{0,28},{4,24},{8,20},{12,16},{16,12},{20,8},{24,4},{28,0},{1,29},{... | collective-permute-start | bytes 196616 | tf_op jit(solution)/shard_map/ppermute | solution.py:354
  24.6 13.0 %collective-permute-start.15 = (bf16[128,256]{1,0:T(8,128)(2,1)S(1)}, bf16[128,256]{1,0:T(8,128)(2,1)S(1)}, u32[]{:S(2)}, u32[]{:S(2)}) collective-permute-start(bf16[128,256]{1,0:T(8,128)(2,1)S(1)} %get-tuple-element.158), channel_id=1, source_target_pairs={{0,24},{4,28},{8,16},{12,20},{16,8},{20,12},{24,0},{28,4},{1,25},{... | collective-permute-start | bytes 196616 | tf_op jit(solution)/shard_map/ppermute | solution.py:354
  26.3 13.7 %collective-permute-start.14 = (bf16[128,256]{1,0:T(8,128)(2,1)S(1)}, bf16[128,256]{1,0:T(8,128)(2,1)S(1)}, u32[]{:S(2)}, u32[]{:S(2)}) collective-permute-start(bf16[128,256]{1,0:T(8,128)(2,1)S(1)} %get-tuple-element.159), channel_id=1, source_target_pairs={{0,20},{4,16},{8,28},{12,24},{16,4},{20,0},{24,12},{28,8},{1,21},{... | collective-permute-start | bytes 196616 | tf_op jit(solution)/shard_map/ppermute | solution.py:354
  49.1 20.9 %collective-permute-start.40 = (bf16[128,1152]{1,0:T(8,128)(2,1)S(1)}, bf16[128,1152]{1,0:T(8,128)(2,1)S(1)}, u32[]{:S(2)}, u32[]{:S(2)}) collective-permute-start(bf16[128,1152]{1,0:T(8,128)(2,1)S(1)} %get-tuple-element.88), channel_id=1, source_target_pairs={{0,1},{1,0},{2,3},{3,2},{4,5},{5,4},{6,7},{7,6},{8,9},{9,8},{10,11... | collective-permute-start | bytes 884744 | tf_op jit(solution)/shard_map/ppermute | solution.py:345
  50.6 19.9 %collective-permute-start.41 = (bf16[128,1152]{1,0:T(8,128)(2,1)S(1)}, bf16[128,1152]{1,0:T(8,128)(2,1)S(1)}, u32[]{:S(2)}, u32[]{:S(2)}) collective-permute-start(bf16[128,1152]{1,0:T(8,128)(2,1)S(1)} %get-tuple-element.89), channel_id=1, source_target_pairs={{0,2},{1,3},{2,0},{3,1},{4,6},{5,7},{6,4},{7,5},{8,10},{9,11},{10,... | collective-permute-start | bytes 884744 | tf_op jit(solution)/shard_map/ppermute | solution.py:345
  58.1 21.8 %collective-permute-start.37 = (bf16[128,1280]{1,0:T(8,128)(2,1)S(1)}, bf16[128,1280]{1,0:T(8,128)(2,1)S(1)}, u32[]{:S(2)}, u32[]{:S(2)}) collective-permute-start(bf16[128,1280]{1,0:T(8,128)(2,1)S(1)} %get-tuple-element.84), channel_id=1, source_target_pairs={{0,1},{1,0},{2,3},{3,2},{4,5},{5,4},{6,7},{7,6},{8,9},{9,8},{10,11... | collective-permute-start | bytes 983048 | tf_op jit(solution)/shard_map/ppermute | solution.py:345
  59.2 19.6 %collective-permute-start.42 = (bf16[128,1152]{1,0:T(8,128)(2,1)S(1)}, bf16[128,1152]{1,0:T(8,128)(2,1)S(1)}, u32[]{:S(2)}, u32[]{:S(2)}) collective-permute-start(bf16[128,1152]{1,0:T(8,128)(2,1)S(1)} %get-tuple-element.90), channel_id=1, source_target_pairs={{0,3},{1,2},{2,1},{3,0},{4,7},{5,6},{6,5},{7,4},{8,11},{9,10},{10,... | collective-permute-start | bytes 884744 | tf_op jit(solution)/shard_map/ppermute | solution.py:345
  68.3 23.0 %collective-permute-start.34 = (bf16[128,1408]{1,0:T(8,128)(2,1)S(1)}, bf16[128,1408]{1,0:T(8,128)(2,1)S(1)}, u32[]{:S(2)}, u32[]{:S(2)}) collective-permute-start(bf16[128,1408]{1,0:T(8,128)(2,1)S(1)} %get-tuple-element.80), channel_id=1, source_target_pairs={{0,1},{1,0},{2,3},{3,2},{4,5},{5,4},{6,7},{7,6},{8,9},{9,8},{10,11... | collective-permute-start | bytes 1081352 | tf_op jit(solution)/shard_map/ppermute | solution.py:345
  70.0 16.6 %collective-permute-start.38 = (bf16[128,1280]{1,0:T(8,128)(2,1)S(1)}, bf16[128,1280]{1,0:T(8,128)(2,1)S(1)}, u32[]{:S(2)}, u32[]{:S(2)}) collective-permute-start(bf16[128,1280]{1,0:T(8,128)(2,1)S(1)} %get-tuple-element.85), channel_id=1, source_target_pairs={{0,2},{1,3},{2,0},{3,1},{4,6},{5,7},{6,4},{7,5},{8,10},{9,11},{10,... | collective-permute-start | bytes 983048 | tf_op jit(solution)/shard_map/ppermute | solution.py:345
  70.4 19.5 %collective-permute-start.39 = (bf16[128,1280]{1,0:T(8,128)(2,1)S(1)}, bf16[128,1280]{1,0:T(8,128)(2,1)S(1)}, u32[]{:S(2)}, u32[]{:S(2)}) collective-permute-start(bf16[128,1280]{1,0:T(8,128)(2,1)S(1)} %get-tuple-element.86), channel_id=1, source_target_pairs={{0,3},{1,2},{2,1},{3,0},{4,7},{5,6},{6,5},{7,4},{8,11},{9,10},{10,... | collective-permute-start | bytes 983048 | tf_op jit(solution)/shard_map/ppermute | solution.py:345
  78.8 25.5 %collective-permute-start.35 = (bf16[128,1408]{1,0:T(8,128)(2,1)S(1)}, bf16[128,1408]{1,0:T(8,128)(2,1)S(1)}, u32[]{:S(2)}, u32[]{:S(2)}) collective-permute-start(bf16[128,1408]{1,0:T(8,128)(2,1)S(1)} %get-tuple-element.81), channel_id=1, source_target_pairs={{0,2},{1,3},{2,0},{3,1},{4,6},{5,7},{6,4},{7,5},{8,10},{9,11},{10,... | collective-permute-start | bytes 1081352 | tf_op jit(solution)/shard_map/ppermute | solution.py:345
  79.9 24.4 %collective-permute-start.36 = (bf16[128,1408]{1,0:T(8,128)(2,1)S(1)}, bf16[128,1408]{1,0:T(8,128)(2,1)S(1)}, u32[]{:S(2)}, u32[]{:S(2)}) collective-permute-start(bf16[128,1408]{1,0:T(8,128)(2,1)S(1)} %get-tuple-element.82), channel_id=1, source_target_pairs={{0,3},{1,2},{2,1},{3,0},{4,7},{5,6},{6,5},{7,4},{8,11},{9,10},{10,... | collective-permute-start | bytes 1081352 | tf_op jit(solution)/shard_map/ppermute | solution.py:345
  86.6 22.5 %collective-permute-start.31 = (bf16[128,1536]{1,0:T(8,128)(2,1)S(1)}, bf16[128,1536]{1,0:T(8,128)(2,1)S(1)}, u32[]{:S(2)}, u32[]{:S(2)}) collective-permute-start(bf16[128,1536]{1,0:T(8,128)(2,1)S(1)} %get-tuple-element.76), channel_id=1, source_target_pairs={{0,1},{1,0},{2,3},{3,2},{4,5},{5,4},{6,7},{7,6},{8,9},{9,8},{10,11... | collective-permute-start | bytes 1179656 | tf_op jit(solution)/shard_map/ppermute | solution.py:345
  89.9 30.8 %collective-permute-start.32 = (bf16[128,1536]{1,0:T(8,128)(2,1)S(1)}, bf16[128,1536]{1,0:T(8,128)(2,1)S(1)}, u32[]{:S(2)}, u32[]{:S(2)}) collective-permute-start(bf16[128,1536]{1,0:T(8,128)(2,1)S(1)} %get-tuple-element.77), channel_id=1, source_target_pairs={{0,2},{1,3},{2,0},{3,1},{4,6},{5,7},{6,4},{7,5},{8,10},{9,11},{10,... | collective-permute-start | bytes 1179656 | tf_op jit(solution)/shard_map/ppermute | solution.py:345
  91.3 29.4 %collective-permute-start.33 = (bf16[128,1536]{1,0:T(8,128)(2,1)S(1)}, bf16[128,1536]{1,0:T(8,128)(2,1)S(1)}, u32[]{:S(2)}, u32[]{:S(2)}) collective-permute-start(bf16[128,1536]{1,0:T(8,128)(2,1)S(1)} %get-tuple-element.78), channel_id=1, source_target_pairs={{0,3},{1,2},{2,1},{3,0},{4,7},{5,6},{6,5},{7,4},{8,11},{9,10},{10,... | collective-permute-start | bytes 1179656 | tf_op jit(solution)/shard_map/ppermute | solution.py:345
  131.6 15.7 %collective-permute-start.52 = (bf16[128,1152]{1,0:T(8,128)(2,1)S(1)}, bf16[128,1152]{1,0:T(8,128)(2,1)S(1)}, u32[]{:S(2)}, u32[]{:S(2)}) collective-permute-start(bf16[128,1152]{1,0:T(8,128)(2,1)S(1)} %get-tuple-element.104), channel_id=1, source_target_pairs={{0,1},{1,0},{2,3},{3,2},{4,5},{5,4},{6,7},{7,6},{8,9},{9,8},{10,11... | collective-permute-start | bytes 884744 | tf_op jit(solution)/shard_map/ppermute | solution.py:345
  133.4 14.5 %collective-permute-start.53 = (bf16[128,1152]{1,0:T(8,128)(2,1)S(1)}, bf16[128,1152]{1,0:T(8,128)(2,1)S(1)}, u32[]{:S(2)}, u32[]{:S(2)}) collective-permute-start(bf16[128,1152]{1,0:T(8,128)(2,1)S(1)} %get-tuple-element.105), channel_id=1, source_target_pairs={{0,2},{1,3},{2,0},{3,1},{4,6},{5,7},{6,4},{7,5},{8,10},{9,11},{10,... | collective-permute-start | bytes 884744 | tf_op jit(solution)/shard_map/ppermute | solution.py:345
  138.3 35.5 %collective-permute-start.43 = (bf16[128,1536]{1,0:T(8,128)(2,1)S(1)}, bf16[128,1536]{1,0:T(8,128)(2,1)S(1)}, u32[]{:S(2)}, u32[]{:S(2)}) collective-permute-start(bf16[128,1536]{1,0:T(8,128)(2,1)S(1)} %get-tuple-element.92), channel_id=1, source_target_pairs={{0,1},{1,0},{2,3},{3,2},{4,5},{5,4},{6,7},{7,6},{8,9},{9,8},{10,11... | collective-permute-start | bytes 1179656 | tf_op jit(solution)/shard_map/ppermute | solution.py:345
  144.4 27.9 %collective-permute-start.49 = (bf16[128,1280]{1,0:T(8,128)(2,1)S(1)}, bf16[128,1280]{1,0:T(8,128)(2,1)S(1)}, u32[]{:S(2)}, u32[]{:S(2)}) collective-permute-start(bf16[128,1280]{1,0:T(8,128)(2,1)S(1)} %get-tuple-element.100), channel_id=1, source_target_pairs={{0,1},{1,0},{2,3},{3,2},{4,5},{5,4},{6,7},{7,6},{8,9},{9,8},{10,11... | collective-permute-start | bytes 983048 | tf_op jit(solution)/shard_map/ppermute | solution.py:345
  145.3 30.1 %collective-permute-start.44 = (bf16[128,1536]{1,0:T(8,128)(2,1)S(1)}, bf16[128,1536]{1,0:T(8,128)(2,1)S(1)}, u32[]{:S(2)}, u32[]{:S(2)}) collective-permute-start(bf16[128,1536]{1,0:T(8,128)(2,1)S(1)} %get-tuple-element.93), channel_id=1, source_target_pairs={{0,2},{1,3},{2,0},{3,1},{4,6},{5,7},{6,4},{7,5},{8,10},{9,11},{10,... | collective-permute-start | bytes 1179656 | tf_op jit(solution)/shard_map/ppermute | solution.py:345
  147.3 28.4 %collective-permute-start.45 = (bf16[128,1536]{1,0:T(8,128)(2,1)S(1)}, bf16[128,1536]{1,0:T(8,128)(2,1)S(1)}, u32[]{:S(2)}, u32[]{:S(2)}) collective-permute-start(bf16[128,1536]{1,0:T(8,128)(2,1)S(1)} %get-tuple-element.94), channel_id=1, source_target_pairs={{0,3},{1,2},{2,1},{3,0},{4,7},{5,6},{6,5},{7,4},{8,11},{9,10},{10,... | collective-permute-start | bytes 1179656 | tf_op jit(solution)/shard_map/ppermute | solution.py:345
  147.9 23.9 %collective-permute-start.54 = (bf16[128,1152]{1,0:T(8,128)(2,1)S(1)}, bf16[128,1152]{1,0:T(8,128)(2,1)S(1)}, u32[]{:S(2)}, u32[]{:S(2)}) collective-permute-start(bf16[128,1152]{1,0:T(8,128)(2,1)S(1)} %get-tuple-element.106), channel_id=1, source_target_pairs={{0,3},{1,2},{2,1},{3,0},{4,7},{5,6},{6,5},{7,4},{8,11},{9,10},{10,... | collective-permute-start | bytes 884744 | tf_op jit(solution)/shard_map/ppermute | solution.py:345
  172.2 26.0 %collective-permute-start.47 = (bf16[128,1408]{1,0:T(8,128)(2,1)S(1)}, bf16[128,1408]{1,0:T(8,128)(2,1)S(1)}, u32[]{:S(2)}, u32[]{:S(2)}) collective-permute-start(bf16[128,1408]{1,0:T(8,128)(2,1)S(1)} %get-tuple-element.97), channel_id=1, source_target_pairs={{0,2},{1,3},{2,0},{3,1},{4,6},{5,7},{6,4},{7,5},{8,10},{9,11},{10,... | collective-permute-start | bytes 1081352 | tf_op jit(solution)/shard_map/ppermute | solution.py:345
  173.8 25.5 %collective-permute-start.48 = (bf16[128,1408]{1,0:T(8,128)(2,1)S(1)}, bf16[128,1408]{1,0:T(8,128)(2,1)S(1)}, u32[]{:S(2)}, u32[]{:S(2)}) collective-permute-start(bf16[128,1408]{1,0:T(8,128)(2,1)S(1)} %get-tuple-element.98), channel_id=1, source_target_pairs={{0,3},{1,2},{2,1},{3,0},{4,7},{5,6},{6,5},{7,4},{8,11},{9,10},{10,... | collective-permute-start | bytes 1081352 | tf_op jit(solution)/shard_map/ppermute | solution.py:345
  175.4 27.7 %collective-permute-start.50 = (bf16[128,1280]{1,0:T(8,128)(2,1)S(1)}, bf16[128,1280]{1,0:T(8,128)(2,1)S(1)}, u32[]{:S(2)}, u32[]{:S(2)}) collective-permute-start(bf16[128,1280]{1,0:T(8,128)(2,1)S(1)} %get-tuple-element.101), channel_id=1, source_target_pairs={{0,2},{1,3},{2,0},{3,1},{4,6},{5,7},{6,4},{7,5},{8,10},{9,11},{10,... | collective-permute-start | bytes 983048 | tf_op jit(solution)/shard_map/ppermute | solution.py:345
  175.7 28.0 %collective-permute-start.51 = (bf16[128,1280]{1,0:T(8,128)(2,1)S(1)}, bf16[128,1280]{1,0:T(8,128)(2,1)S(1)}, u32[]{:S(2)}, u32[]{:S(2)}) collective-permute-start(bf16[128,1280]{1,0:T(8,128)(2,1)S(1)} %get-tuple-element.102), channel_id=1, source_target_pairs={{0,3},{1,2},{2,1},{3,0},{4,7},{5,6},{6,5},{7,4},{8,11},{9,10},{10,... | collective-permute-start | bytes 983048 | tf_op jit(solution)/shard_map/ppermute | solution.py:345
  183.2 22.1 %collective-permute-start.76 = (bf16[128,256]{1,0:T(8,128)(2,1)S(1)}, bf16[128,256]{1,0:T(8,128)(2,1)S(1)}, u32[]{:S(2)}, u32[]{:S(2)}) collective-permute-start(bf16[128,256]{1,0:T(8,128)(2,1)S(1)} %get-tuple-element.135), channel_id=1, source_target_pairs={{0,4},{4,0},{8,12},{12,8},{16,20},{20,16},{24,28},{28,24},{1,5},{5... | collective-permute-start | bytes 196616 | tf_op jit(solution)/shard_map/ppermute | solution.py:354
  214.7 12.0 %collective-permute-start.72 = (bf16[128,256]{1,0:T(8,128)(2,1)S(1)}, bf16[128,256]{1,0:T(8,128)(2,1)S(1)}, u32[]{:S(2)}, u32[]{:S(2)}) collective-permute-start(bf16[128,256]{1,0:T(8,128)(2,1)S(1)} %get-tuple-element.130), channel_id=1, source_target_pairs={{0,16},{4,20},{8,24},{12,28},{16,0},{20,4},{24,8},{28,12},{1,17},{... | collective-permute-start | bytes 196616 | tf_op jit(solution)/shard_map/ppermute | solution.py:354
  237.4 15.8 %collective-permute-start.57 = (bf16[128,256]{1,0:T(8,128)(2,1)S(1)}, bf16[128,256]{1,0:T(8,128)(2,1)S(1)}, u32[]{:S(2)}, u32[]{:S(2)}) collective-permute-start(bf16[128,256]{1,0:T(8,128)(2,1)S(1)} %get-tuple-element.113), channel_id=1, source_target_pairs={{0,12},{4,8},{8,4},{12,0},{16,28},{20,24},{24,20},{28,16},{1,13},{... | collective-permute-start | bytes 196616 | tf_op jit(solution)/shard_map/ppermute | solution.py:354
  (60 other events, 526.4 us)
where the time goes:
time: 257 us; the launch traced here: 256 us
  starting transfers between devices  101 us (39%)
  waiting for transfers between devices  85.6 us (33%)
  Pallas kernels  63.1 us (25%)
  local copies, waits for them, and re-layouts  5.02 us (2%)
    ppermute x56, starting transfers between devices, across(): out[d] = lax.ppermute(values[d], 'mat', [(i, i ^ d) for i in range(n_mat)])  67.4 us
    ppermute x27, waiting for transfers between devices, to_peer(): return lax.ppermute(value, 'pts', [(i, i ^ o) for i in range(n_pts)])  59.2 us
    ppermute x27, starting transfers between devices, to_peer(): return lax.ppermute(value, 'pts', [(i, i ^ o) for i in range(n_pts)])  33.5 us
    ppermute x56, waiting for transfers between devices, across(): out[d] = lax.ppermute(values[d], 'mat', [(i, i ^ d) for i in range(n_mat)])  26.4 us
    pallas_call x4, Pallas kernels, density(): pl.pallas_call(functools.partial(density_kernel, dims, k, 256, last), out...  19.7 us
    pallas_call x4, Pallas kernels, response(): pl.pallas_call(functools.partial(response_kernel, dims, k, 256), out_shap...  19.3 us
    pallas_call x4, Pallas kernels, combine(): pl.pallas_call(functools.partial(combine_kernel, dims, k), out_shape=shap...  8.55 us
    pallas_call x4, Pallas kernels, pack(): pl.pallas_call(functools.partial(pack_kernel, dims, k), out_shape=shapes,...  7.3 us
  transfers between devices with their start and end apart: 83, of which 22 were waited for; matrix products, arithmetic and copies ran while one was open for 0% of the time, Pallas kernels for 20%

commit v1 on v0

--- a/solution.py
+++ b/solution.py
@@ -47,14 +47,14 @@
     return row
 
 
-def list_slots(dims, meta, table, o, column, row, lower, positions):
+def list_slots(dims, meta, table, base, o, column, row, lower, positions):
     _, n_pts, act, nact = dims
     each = act // n_pts
-    base, filled = o * (nact + 1), jnp.int32(0)
+    filled = jnp.int32(0)
     for j in range(nact + 1):
         table[base + j] = 0
     for j in range(nact):
-        block = meta[HEAD + (0 if positions else o) * nact + j]
+        block = meta[HEAD + o * nact + j]
         local = block - column * each
         kept = (local < 0) | (local >= each) | ((local <= row) if lower else (local >= row))
         table[base + filled] = j if positions else block
@@ -90,7 +90,7 @@
     for o in range(n_pts):
         flags = active_rows(dims, meta, o, me_pts)
         row = jnp.maximum(ranked_row(flags, each - 1 - k, True), 0)
-        list_slots(dims, meta, table, o, me_pts, row, True, False)
+        list_slots(dims, meta, table, o * (nact + 1), o, me_pts, row, True, False)
         for r in range(k + 1):
             source = stage if r == k else earlier[r]
 
@@ -144,6 +144,11 @@
         place[meta[HEAD + i]] = i
 
 
+def tile_of(columns, cases):
+    half = columns // 2
+    return half if cases <= 4 and half % BLOCK == 0 else 2 * BLOCK
+
+
 def density_kernel(dims, k, tile, last, meta, *refs):
     _, n_pts, act, nact = dims
     each = act // n_pts
@@ -155,7 +160,7 @@
     for o in range(n_pts):
         column = meta[1] ^ o
         row = ranked_row(active_rows(dims, meta, 0, column), each - 1 - k, True)
-        list_slots(dims, meta, table, o, column, jnp.maximum(row, 0), True, True)
+        list_slots(dims, meta, table, o * (nact + 1), 0, column, jnp.maximum(row, 0), True, True)
         rows.append((jnp.maximum(place[column * each + jnp.maximum(row, 0)], 0), row >= 0))
         for slot in range(slots_in(dims, k)):
             j = table[o * (nact + 1) + slot]
@@ -180,7 +185,7 @@
     _, n_pts, act, nact = dims
     orbitals, points = flipped.shape
     return pl.pallas_call(
-        functools.partial(density_kernel, dims, k, 256, last),
+        functools.partial(density_kernel, dims, k, tile_of(points, n_pts), last),
         out_shape=jax.ShapeDtypeStruct((1, points), jnp.float32),
         in_specs=[pl.BlockSpec(memory_space=pltpu.SMEM)] + [VM] * (n_pts + 2),
         out_specs=VM,
@@ -194,51 +199,57 @@
     )(meta, *parts, flipped, before)
 
 
-def response_kernel(dims, k, tile, meta, *refs):
+def response_kernel(dims, ranks, tile, meta, *refs):
     _, n_pts, act, nact = dims
     each = act // n_pts
     flipped, basis, n, kern, pert, weight = refs[:6]
-    out, (place, table, left, right) = refs[6 : 6 + n_pts], refs[6 + n_pts :]
+    out, (place, table, left, right) = refs[6:-4], refs[-4:]
     invert(dims, meta, place)
     points = flipped.shape[1]
     inside = lax.broadcasted_iota(jnp.int32, (1, points), 1) < meta[2]
     scaling = jnp.where(inside, weight[...] * (pert[...] - kern[...] * n[...]), 0.0)
-    for o in range(n_pts):
+    cases = [(k, o) for k in ranks for o in range(n_pts)]
+    for at, (k, o) in enumerate(cases):
         column = meta[1] ^ o
         row = ranked_row(active_rows(dims, meta, 0, column), k, False)
-        list_slots(dims, meta, table, o, column, jnp.maximum(row, 0), False, True)
+        list_slots(dims, meta, table, at * (nact + 1), 0, column, jnp.maximum(row, 0), False, True)
         spot = jnp.maximum(place[column * each + jnp.maximum(row, 0)], 0)
         own = flipped[rows_at(spot), :].astype(jnp.float32)
-        left[o * BLOCK : (o + 1) * BLOCK, :] = jnp.where(row >= 0, own * scaling, 0.0).astype(jnp.bfloat16)
+        left[at * BLOCK : (at + 1) * BLOCK, :] = jnp.where(row >= 0, own * scaling, 0.0).astype(jnp.bfloat16)
 
     @pl.loop(0, basis.shape[1] // tile)
     def _(t):
-        at = pl.ds(pl.multiple_of(t * tile, tile), tile)
-        right[:, at] = jnp.dot(left[...], basis[:, at], preferred_element_type=jnp.float32).astype(jnp.bfloat16)
-
-    for o in range(n_pts):
+        cols = pl.ds(pl.multiple_of(t * tile, tile), tile)
+        right[:, cols] = jnp.dot(left[...], basis[:, cols], preferred_element_type=jnp.float32).astype(jnp.bfloat16)
+
+    for at, (k, o) in enumerate(cases):
         for slot in range(slots_out(dims, k)):
-            j = table[o * (nact + 1) + slot]
-            out[o][:, slot * BLOCK : (slot + 1) * BLOCK] = right[o * BLOCK : (o + 1) * BLOCK, lanes(j)]
-
-
-def response(dims, k, meta, flipped, basis, n, kern, pert, weight):
+            j = table[at * (nact + 1) + slot]
+            out[at][:, slot * BLOCK : (slot + 1) * BLOCK] = right[at * BLOCK : (at + 1) * BLOCK, lanes(j)]
+
+
+def response(dims, ranks, meta, flipped, basis, n, kern, pert, weight):
     _, n_pts, act, nact = dims
     orbitals, points = flipped.shape
-    return pl.pallas_call(
-        functools.partial(response_kernel, dims, k, 256),
-        out_shape=[jax.ShapeDtypeStruct((BLOCK, slots_out(dims, k) * BLOCK), jnp.bfloat16)] * n_pts,
+    cases = n_pts * len(ranks)
+    shapes = [
+        jax.ShapeDtypeStruct((BLOCK, slots_out(dims, k) * BLOCK), jnp.bfloat16) for k in ranks for _ in range(n_pts)
+    ]
+    out = pl.pallas_call(
+        functools.partial(response_kernel, dims, ranks, tile_of(orbitals, cases)),
+        out_shape=shapes,
         in_specs=[pl.BlockSpec(memory_space=pltpu.SMEM)] + [VM] * 6,
-        out_specs=[VM] * n_pts,
+        out_specs=[VM] * len(shapes),
         scratch_shapes=[
             pltpu.SMEM((act,), jnp.int32),
-            pltpu.SMEM((n_pts * (nact + 1),), jnp.int32),
-            pltpu.VMEM((n_pts * BLOCK, points), jnp.bfloat16),
-            pltpu.VMEM((n_pts * BLOCK, orbitals), jnp.bfloat16),
+            pltpu.SMEM((cases * (nact + 1),), jnp.int32),
+            pltpu.VMEM((cases * BLOCK, points), jnp.bfloat16),
+            pltpu.VMEM((cases * BLOCK, orbitals), jnp.bfloat16),
         ],
-        compiler_params=GRANT,
-        cost_estimate=cost(2 * n_pts * BLOCK * orbitals * points, 4 * orbitals * points),
+        compiler_params=pltpu.CompilerParams(vmem_limit_bytes=26 << 20),
+        cost_estimate=cost(2 * cases * BLOCK * orbitals * points, 4 * orbitals * points),
     )(meta, flipped, basis, n, kern, pert, weight)
+    return [out[at * n_pts : (at + 1) * n_pts] for at in range(len(ranks))]
 
 
 def combine_kernel(dims, k, meta, *refs):
@@ -259,7 +270,7 @@
                 filled = slots_out(dims, i) * BLOCK
                 pltpu.make_async_copy(strips[i * n_pts + o], held.at[o, :, :filled], sem.at[o]).start()
 
-        list_slots(dims, meta, table, o, me_pts, jnp.int32(k), False, False)
+        list_slots(dims, meta, table, o * (nact + 1), o, me_pts, jnp.int32(k), False, False)
     total[...] = jnp.zeros_like(total)
     for o in range(n_pts):
         for i in range(k + 1):
@@ -334,6 +345,10 @@
     )(meta, *given, *more)
 
 
+def emissions(row_blocks):
+    return [(0,)] + ([tuple(range(1, row_blocks))] if row_blocks > 1 else [])
+
+
 def body(dens_blocks, basis_values, kernel, perturbation, quad_weight, point_count, active_blocks, block_pattern):
     n_mat, n_pts = lax.axis_size("mat"), lax.axis_size("pts")
     act, nact = block_pattern.shape[1], active_blocks.shape[2]
@@ -380,9 +395,10 @@
         n = density(dims, k, k == row_blocks - 1, meta, parts[k], flipped, n)
 
     strips = []
-    for k in range(row_blocks):
-        sent = response(dims, k, meta, flipped, basis, n, kernel, perturbation, quad_weight)
-        strips.append([sent[0]] + [to_peer(sent[o], o) for o in range(1, n_pts)])
+    for ranks in emissions(row_blocks):
+        several = response(dims, ranks, meta, flipped, basis, n, kernel, perturbation, quad_weight)
+        for k, sent in zip(ranks, several):
+            strips.append([sent[0]] + [to_peer(sent[o], o) for o in range(1, n_pts)])
 
     inner, result = [], None
     for k in range(row_blocks):

time: 257 us -> 262 us (1.019)
  waiting for transfers between devices: 85.6 us -> 97.6 us
  Pallas kernels: 63.1 us -> 56.1 us
    ppermute x27, waiting for transfers between devices: 59.2 us -> 71.4 us  [to_peer(): return lax.ppermute(value, 'pts', [(i, i ^ o) for i in range(n_pts)])]
    pallas_call x8 -> x6, Pallas kernels: 38.9 us -> 32.2 us  [the longest x4 16.7 us: density(): pl.pallas_call(functools.partial(density_kernel, dims, k, tile_of(points,...]
  transfers between devices with their start and end apart: 83 -> 83, of which waited for: 22 -> 21; matrix products, arithmetic and copies ran while one was open for 0% -> 0% of each run, Pallas kernels for 20% -> 15%
where the time goes in v1:
time: 262 us; the launch traced here: 261 us
  starting transfers between devices  101 us (39%)
  waiting for transfers between devices  97.6 us (37%)
  Pallas kernels  56.1 us (21%)
  local copies, waits for them, and re-layouts  5.02 us (2%)
    ppermute x27, waiting for transfers between devices, to_peer(): return lax.ppermute(value, 'pts', [(i, i ^ o) for i in range(n_pts)])  71.4 us
    ppermute x56, starting transfers between devices, across(): out[d] = lax.ppermute(values[d], 'mat', [(i, i ^ d) for i in range(n_mat)])  67.5 us
    ppermute x27, starting transfers between devices, to_peer(): return lax.ppermute(value, 'pts', [(i, i ^ o) for i in range(n_pts)])  33.5 us
    ppermute x56, waiting for transfers between devices, across(): out[d] = lax.ppermute(values[d], 'mat', [(i, i ^ d) for i in range(n_mat)])  26.2 us
    pallas_call x4, Pallas kernels, density(): pl.pallas_call(functools.partial(density_kernel, dims, k, tile_of(points,...  16.7 us
    pallas_call x2, Pallas kernels, response(): pl.pallas_call(functools.partial(response_kernel, dims, ranks, tile_of(or...  15.4 us
    pallas_call x4, Pallas kernels, combine(): pl.pallas_call(functools.partial(combine_kernel, dims, k), out_shape=shap...  8.33 us
    pallas_call x4, Pallas kernels, pack(): pl.pallas_call(functools.partial(pack_kernel, dims, k), out_shape=shapes,...  7.3 us
  transfers between devices with their start and end apart: 83, of which 21 were waited for; matrix products, arithmetic and copies ran while one was open for 0% of the time, Pallas kernels for 15%

profile of v1, /device:TPU:0, one launch (start us, length us, event | category | flops | bytes accessed | tf_op | source)
XLA Modules:
  0.0 261.4 jit_solution(17268623472492060518)
XLA Ops:
  2.5 4.6 %collective-permute-start.30 = (bf16[128,256]{1,0:T(8,128)(2,1)S(1)}, bf16[128,256]{1,0:T(8,128)(2,1)S(1)}, u32[]{:S(2)}, u32[]{:S(2)}) collective-permute-start(bf16[128,256]{1,0:T(8,128)(2,1)S(1)} %get-tuple-element.142), channel_id=1, source_target_pairs={{0,28},{4,24},{8,20},{12,16},{16,12},{20,8},{24,4},{28,0},{1,29},{... | collective-permute-start | bytes 196616 | tf_op jit(solution)/shard_map/ppermute | solution.py:369
  7.1 2.4 collective-permute-start.2
  11.6 3.2 %collective-permute-start.27 = (bf16[128,256]{1,0:T(8,128)(2,1)S(1)}, bf16[128,256]{1,0:T(8,128)(2,1)S(1)}, u32[]{:S(2)}, u32[]{:S(2)}) collective-permute-start(bf16[128,256]{1,0:T(8,128)(2,1)S(1)} %get-tuple-element.144), channel_id=1, source_target_pairs={{0,16},{4,20},{8,24},{12,28},{16,0},{20,4},{24,8},{28,12},{1,17},{... | collective-permute-start | bytes 196616 | tf_op jit(solution)/shard_map/ppermute | solution.py:369
  20.2 2.7 %collective-permute-start.20 = (bf16[128,256]{1,0:T(8,128)(2,1)S(1)}, bf16[128,256]{1,0:T(8,128)(2,1)S(1)}, u32[]{:S(2)}, u32[]{:S(2)}) collective-permute-start(bf16[128,256]{1,0:T(8,128)(2,1)S(1)} %get-tuple-element.152), channel_id=1, source_target_pairs={{0,16},{4,20},{8,24},{12,28},{16,0},{20,4},{24,8},{28,12},{1,17},{... | collective-permute-start | bytes 196616 | tf_op jit(solution)/shard_map/ppermute | solution.py:369
  26.3 5.5 %collective-permute-start.14 = (bf16[128,256]{1,0:T(8,128)(2,1)S(1)}, bf16[128,256]{1,0:T(8,128)(2,1)S(1)}, u32[]{:S(2)}, u32[]{:S(2)}) collective-permute-start(bf16[128,256]{1,0:T(8,128)(2,1)S(1)} %get-tuple-element.159), channel_id=1, source_target_pairs={{0,20},{4,16},{8,28},{12,24},{16,4},{20,0},{24,12},{28,8},{1,21},{... | collective-permute-start | bytes 196616 | tf_op jit(solution)/shard_map/ppermute | solution.py:369
  34.8 2.8 %collective-permute-start.11 = (bf16[128,256]{1,0:T(8,128)(2,1)S(1)}, bf16[128,256]{1,0:T(8,128)(2,1)S(1)}, u32[]{:S(2)}, u32[]{:S(2)}) collective-permute-start(bf16[128,256]{1,0:T(8,128)(2,1)S(1)} %get-tuple-element.162), channel_id=1, source_target_pairs={{0,8},{4,12},{8,0},{12,4},{16,24},{20,28},{24,16},{28,20},{1,9},{5... | collective-permute-start | bytes 196616 | tf_op jit(solution)/shard_map/ppermute | solution.py:369
  42.7 2.4 collective-permute-start.9
  52.1 2.2 collective-permute-start.6
  62.4 4.2 %collective-permute-done.29.refs_6_ = bf16[128,256]{1,0:T(8,128)(2,1)S(1)} collective-permute-done((bf16[128,256]{1,0:T(8,128)(2,1)S(1)}, bf16[128,256]{1,0:T(8,128)(2,1)S(1)}, u32[]{:S(2)}, u32[]{:S(2)}) %collective-permute-start.29) | collective-permute-done | bytes 65568 | tf_op jit(solution)/shard_map/ppermute | solution.py:369
  71.8 2.3 copy-done.1
  76.1 2.7 %shard_map.98 = (bf16[128,2048]{1,0:T(8,128)(2,1)}, bf16[128,1536]{1,0:T(8,128)(2,1)S(1)}, bf16[128,1536]{1,0:T(8,128)(2,1)S(1)}, bf16[128,1536]{1,0:T(8,128)(2,1)S(1)}, bf16[128,1536]{1,0:T(8,128)(2,1)S(1)}) custom-call(s32[307]{0:T(512)S(1)} %concatenate.3.meta, bf16[128,256]{1,0:T(8,128)(2,1)S(1)} %get-tuple-element.172.refs_0_, ...), custom_call_target="tpu_custom_call" | custom-call | bytes 2097152 | tf_op jit(solution)/shard_map/pallas_call | solution.py:108
  81.9 4.0 %shard_map.99.refs_5_ = f32[1,1536]{1,0:T(1,128)S(1)} custom-call(s32[307]{0:T(512)S(1)} %concatenate.3.meta, bf16[128,1152]{1,0:T(8,128)(2,1)S(1)} %get-tuple-element.87.refs_0_, bf16[128,1152]{1,0:T(8,128)(2,1)S(1)} %collective-permute-done.40.refs_1_, bf16[128,1152]{1,0:T(8,128)(2,1)S(1)} %collective-permute-done.41.refs_2_, ...), custom_call_target="tpu_custom_call" | custom-call | flops 2415919104 | bytes 4718592 | tf_op jit(solution)/shard_map/pallas_call | solution.py:187
  86.3 3.6 %collective-permute-done.39.refs_3_ = bf16[128,1280]{1,0:T(8,128)(2,1)S(1)} collective-permute-done((bf16[128,1280]{1,0:T(8,128)(2,1)S(1)}, bf16[128,1280]{1,0:T(8,128)(2,1)S(1)}, u32[]{:S(2)}, u32[]{:S(2)}) %collective-permute-start.39) | collective-permute-done | bytes 327712 | tf_op jit(solution)/shard_map/ppermute | solution.py:360
  93.5 4.0 %shard_map.100.refs_5_ = f32[1,1536]{1,0:T(1,128)S(1)} custom-call(s32[307]{0:T(512)S(1)} %concatenate.3.meta, bf16[128,1280]{1,0:T(8,128)(2,1)S(1)} %get-tuple-element.83.refs_0_, bf16[128,1280]{1,0:T(8,128)(2,1)S(1)} %collective-permute-done.37.refs_1_, bf16[128,1280]{1,0:T(8,128)(2,1)S(1)} %collective-permute-done.38.refs_2_, ...), custom_call_target="tpu_custom_call" | custom-call | flops 2415919104 | bytes 4718592 | tf_op jit(solution)/shard_map/pallas_call | solution.py:187
  97.5 6.8 %collective-permute-done.35.refs_2_ = bf16[128,1408]{1,0:T(8,128)(2,1)S(1)} collective-permute-done((bf16[128,1408]{1,0:T(8,128)(2,1)S(1)}, bf16[128,1408]{1,0:T(8,128)(2,1)S(1)}, u32[]{:S(2)}, u32[]{:S(2)}) %collective-permute-start.35) | collective-permute-done | bytes 360480 | tf_op jit(solution)/shard_map/ppermute | solution.py:360
  104.3 4.0 %shard_map.101.refs_5_ = f32[1,1536]{1,0:T(1,128)S(1)} custom-call(s32[307]{0:T(512)S(1)} %concatenate.3.meta, bf16[128,1408]{1,0:T(8,128)(2,1)S(1)} %get-tuple-element.79.refs_0_, bf16[128,1408]{1,0:T(8,128)(2,1)S(1)} %collective-permute-done.34.refs_1_, bf16[128,1408]{1,0:T(8,128)(2,1)S(1)} %collective-permute-done.35.refs_2_, ...), custom_call_target="tpu_custom_call" | custom-call | flops 2415919104 | bytes 4718592 | tf_op jit(solution)/shard_map/pallas_call | solution.py:187
  108.4 12.3 %collective-permute-done.32.refs_2_ = bf16[128,1536]{1,0:T(8,128)(2,1)S(1)} collective-permute-done((bf16[128,1536]{1,0:T(8,128)(2,1)S(1)}, bf16[128,1536]{1,0:T(8,128)(2,1)S(1)}, u32[]{:S(2)}, u32[]{:S(2)}) %collective-permute-start.32) | collective-permute-done | bytes 393248 | tf_op jit(solution)/shard_map/ppermute | solution.py:360
  120.7 4.7 %shard_map.102.refs_2_ = f32[1,1536]{1,0:T(1,128)} custom-call(s32[307]{0:T(512)S(1)} %concatenate.3.meta, bf16[128,1536]{1,0:T(8,128)(2,1)S(1)} %get-tuple-element.75.refs_0_, bf16[128,1536]{1,0:T(8,128)(2,1)S(1)} %collective-permute-done.31.refs_1_, bf16[128,1536]{1,0:T(8,128)(2,1)S(1)} %collective-permute-done.32.refs_2_, ...), custom_call_target="tpu_custom_call" | custom-call | flops 2415919104 | bytes 4718592 | tf_op jit(solution)/shard_map/pallas_call | solution.py:187
  126.1 11.0 %shard_map.104 = (bf16[128,1408]{1,0:T(8,128)(2,1)S(1)}, bf16[128,1408]{1,0:T(8,128)(2,1)S(1)}, bf16[128,1408]{1,0:T(8,128)(2,1)S(1)}, bf16[128,1408]{1,0:T(8,12...) custom-call(s32[307]{0:T(512)S(1)} %concatenate.3.meta, ...), custom_call_target="tpu_custom_call" | custom-call | flops 7247757312 | bytes 9437184 | tf_op jit(solution)/shard_map/pallas_call | solution.py:238
  139.0 4.4 %shard_map.103 = (bf16[128,1536]{1,0:T(8,128)(2,1)S(1)}, bf16[128,1536]{1,0:T(8,128)(2,1)S(1)}, bf16[128,1536]{1,0:T(8,128)(2,1)S(1)}, bf16[128,1536]{1,0:T(8,128)(2,1)S(1)}) custom-call(s32[307]{0:T(512)S(1)} %concatenate.3.meta, bf16[1536,1536]{1,0:T(8,128)(2,1)S(1)} %flip.1.refs_4_.refs_0_, bf16[1536,1536]{1,0:T(8,128)(2,1)S(1)} %bitcast.74, ...), custom_call_target="tpu_custom_call" | custom-call | flops 2415919104 | bytes 9437184 | tf_op jit(solution)/shard_map/pallas_call | solution.py:238
  148.1 2.3 collective-permute-start.54
  150.4 26.5 %collective-permute-done.54.refs_15_ = bf16[128,1152]{1,0:T(8,128)(2,1)S(1)} collective-permute-done((bf16[128,1152]{1,0:T(8,128)(2,1)S(1)}, bf16[128,1152]{1,0:T(8,128)(2,1)S(1)}, u32[]{:S(2)}, u32[]{:S(2)}) %collective-permute-start.54) | collective-permute-done | bytes 294944 | tf_op jit(solution)/shard_map/ppermute | solution.py:360
  184.1 4.1 %collective-permute-done.46.refs_5_ = bf16[128,1408]{1,0:T(8,128)(2,1)S(1)} collective-permute-done((bf16[128,1408]{1,0:T(8,128)(2,1)S(1)}, bf16[128,1408]{1,0:T(8,128)(2,1)S(1)}, u32[]{:S(2)}, u32[]{:S(2)}) %collective-permute-start.46) | collective-permute-done | bytes 360480 | tf_op jit(solution)/shard_map/ppermute | solution.py:360
  188.2 15.1 %collective-permute-done.47.refs_6_ = bf16[128,1408]{1,0:T(8,128)(2,1)S(1)} collective-permute-done((bf16[128,1408]{1,0:T(8,128)(2,1)S(1)}, bf16[128,1408]{1,0:T(8,128)(2,1)S(1)}, u32[]{:S(2)}, u32[]{:S(2)}) %collective-permute-start.47) | collective-permute-done | bytes 360480 | tf_op jit(solution)/shard_map/ppermute | solution.py:360
  211.9 2.7 %collective-permute-start.82 = (bf16[128,256]{1,0:T(8,128)(2,1)S(1)}, bf16[128,256]{1,0:T(8,128)(2,1)S(1)}, u32[]{:S(2)}, u32[]{:S(2)}) collective-permute-start(bf16[128,256]{1,0:T(8,128)(2,1)S(1)} %get-tuple-element.141), channel_id=1, source_target_pairs={{0,28},{4,24},{8,20},{12,16},{16,12},{20,8},{24,4},{28,0},{1,29},{... | collective-permute-start | bytes 196616 | tf_op jit(solution)/shard_map/ppermute | solution.py:369
  214.6 3.9 %collective-permute-done.79.refs_4_ = bf16[128,256]{1,0:T(8,128)(2,1)S(1)} collective-permute-done((bf16[128,256]{1,0:T(8,128)(2,1)S(1)}, bf16[128,256]{1,0:T(8,128)(2,1)S(1)}, u32[]{:S(2)}, u32[]{:S(2)}) %collective-permute-start.79) | collective-permute-done | bytes 65568 | tf_op jit(solution)/shard_map/ppermute | solution.py:369
  219.9 2.3 collective-permute-start.72
  225.3 2.2 shard_map.107
  227.5 2.5 shard_map.108
  233.6 2.7 %collective-permute-done.75.refs_7_ = bf16[128,256]{1,0:T(8,128)(2,1)S(1)} collective-permute-done((bf16[128,256]{1,0:T(8,128)(2,1)S(1)}, bf16[128,256]{1,0:T(8,128)(2,1)S(1)}, u32[]{:S(2)}, u32[]{:S(2)}) %collective-permute-start.75) | collective-permute-done | bytes 65568 | tf_op jit(solution)/shard_map/ppermute | solution.py:369
  244.6 4.0 %collective-permute-done.66.refs_5_ = bf16[128,256]{1,0:T(8,128)(2,1)S(1)} collective-permute-done((bf16[128,256]{1,0:T(8,128)(2,1)S(1)}, bf16[128,256]{1,0:T(8,128)(2,1)S(1)}, u32[]{:S(2)}, u32[]{:S(2)}) %collective-permute-start.66) | collective-permute-done | bytes 65568 | tf_op jit(solution)/shard_map/ppermute | solution.py:369
  248.6 2.8 %collective-permute-start.60 = (bf16[128,256]{1,0:T(8,128)(2,1)S(1)}, bf16[128,256]{1,0:T(8,128)(2,1)S(1)}, u32[]{:S(2)}, u32[]{:S(2)}) collective-permute-start(bf16[128,256]{1,0:T(8,128)(2,1)S(1)} %get-tuple-element.116), channel_id=1, source_target_pairs={{0,24},{4,28},{8,16},{12,20},{16,8},{20,12},{24,0},{28,4},{1,25},{... | collective-permute-start | bytes 196616 | tf_op jit(solution)/shard_map/ppermute | solution.py:369
  (179 shorter events, 98.7 us)
Async XLA Ops:
  2.5 12.6 %collective-permute-start.30 = (bf16[128,256]{1,0:T(8,128)(2,1)S(1)}, bf16[128,256]{1,0:T(8,128)(2,1)S(1)}, u32[]{:S(2)}, u32[]{:S(2)}) collective-permute-start(bf16[128,256]{1,0:T(8,128)(2,1)S(1)} %get-tuple-element.142), channel_id=1, source_target_pairs={{0,28},{4,24},{8,20},{12,16},{16,12},{20,8},{24,4},{28,0},{1,29},{... | collective-permute-start | bytes 196616 | tf_op jit(solution)/shard_map/ppermute | solution.py:369
  20.1 11.7 %collective-permute-start.21 = (bf16[128,256]{1,0:T(8,128)(2,1)S(1)}, bf16[128,256]{1,0:T(8,128)(2,1)S(1)}, u32[]{:S(2)}, u32[]{:S(2)}) collective-permute-start(bf16[128,256]{1,0:T(8,128)(2,1)S(1)} %get-tuple-element.151), channel_id=1, source_target_pairs={{0,20},{4,16},{8,28},{12,24},{16,4},{20,0},{24,12},{28,8},{1,21},{... | collective-permute-start | bytes 196616 | tf_op jit(solution)/shard_map/ppermute | solution.py:369
  20.2 14.6 %collective-permute-start.20 = (bf16[128,256]{1,0:T(8,128)(2,1)S(1)}, bf16[128,256]{1,0:T(8,128)(2,1)S(1)}, u32[]{:S(2)}, u32[]{:S(2)}) collective-permute-start(bf16[128,256]{1,0:T(8,128)(2,1)S(1)} %get-tuple-element.152), channel_id=1, source_target_pairs={{0,16},{4,20},{8,24},{12,28},{16,0},{20,4},{24,8},{28,12},{1,17},{... | collective-permute-start | bytes 196616 | tf_op jit(solution)/shard_map/ppermute | solution.py:369
  22.8 12.0 %collective-permute-start.16 = (bf16[128,256]{1,0:T(8,128)(2,1)S(1)}, bf16[128,256]{1,0:T(8,128)(2,1)S(1)}, u32[]{:S(2)}, u32[]{:S(2)}) collective-permute-start(bf16[128,256]{1,0:T(8,128)(2,1)S(1)} %get-tuple-element.157), channel_id=1, source_target_pairs={{0,28},{4,24},{8,20},{12,16},{16,12},{20,8},{24,4},{28,0},{1,29},{... | collective-permute-start | bytes 196616 | tf_op jit(solution)/shard_map/ppermute | solution.py:369
  24.6 13.0 %collective-permute-start.15 = (bf16[128,256]{1,0:T(8,128)(2,1)S(1)}, bf16[128,256]{1,0:T(8,128)(2,1)S(1)}, u32[]{:S(2)}, u32[]{:S(2)}) collective-permute-start(bf16[128,256]{1,0:T(8,128)(2,1)S(1)} %get-tuple-element.158), channel_id=1, source_target_pairs={{0,24},{4,28},{8,16},{12,20},{16,8},{20,12},{24,0},{28,4},{1,25},{... | collective-permute-start | bytes 196616 | tf_op jit(solution)/shard_map/ppermute | solution.py:369
  26.3 13.7 %collective-permute-start.14 = (bf16[128,256]{1,0:T(8,128)(2,1)S(1)}, bf16[128,256]{1,0:T(8,128)(2,1)S(1)}, u32[]{:S(2)}, u32[]{:S(2)}) collective-permute-start(bf16[128,256]{1,0:T(8,128)(2,1)S(1)} %get-tuple-element.159), channel_id=1, source_target_pairs={{0,20},{4,16},{8,28},{12,24},{16,4},{20,0},{24,12},{28,8},{1,21},{... | collective-permute-start | bytes 196616 | tf_op jit(solution)/shard_map/ppermute | solution.py:369
  49.1 20.9 %collective-permute-start.40 = (bf16[128,1152]{1,0:T(8,128)(2,1)S(1)}, bf16[128,1152]{1,0:T(8,128)(2,1)S(1)}, u32[]{:S(2)}, u32[]{:S(2)}) collective-permute-start(bf16[128,1152]{1,0:T(8,128)(2,1)S(1)} %get-tuple-element.88), channel_id=1, source_target_pairs={{0,1},{1,0},{2,3},{3,2},{4,5},{5,4},{6,7},{7,6},{8,9},{9,8},{10,11... | collective-permute-start | bytes 884744 | tf_op jit(solution)/shard_map/ppermute | solution.py:360
  50.6 19.9 %collective-permute-start.41 = (bf16[128,1152]{1,0:T(8,128)(2,1)S(1)}, bf16[128,1152]{1,0:T(8,128)(2,1)S(1)}, u32[]{:S(2)}, u32[]{:S(2)}) collective-permute-start(bf16[128,1152]{1,0:T(8,128)(2,1)S(1)} %get-tuple-element.89), channel_id=1, source_target_pairs={{0,2},{1,3},{2,0},{3,1},{4,6},{5,7},{6,4},{7,5},{8,10},{9,11},{10,... | collective-permute-start | bytes 884744 | tf_op jit(solution)/shard_map/ppermute | solution.py:360
  58.1 21.8 %collective-permute-start.37 = (bf16[128,1280]{1,0:T(8,128)(2,1)S(1)}, bf16[128,1280]{1,0:T(8,128)(2,1)S(1)}, u32[]{:S(2)}, u32[]{:S(2)}) collective-permute-start(bf16[128,1280]{1,0:T(8,128)(2,1)S(1)} %get-tuple-element.84), channel_id=1, source_target_pairs={{0,1},{1,0},{2,3},{3,2},{4,5},{5,4},{6,7},{7,6},{8,9},{9,8},{10,11... | collective-permute-start | bytes 983048 | tf_op jit(solution)/shard_map/ppermute | solution.py:360
  59.2 19.6 %collective-permute-start.42 = (bf16[128,1152]{1,0:T(8,128)(2,1)S(1)}, bf16[128,1152]{1,0:T(8,128)(2,1)S(1)}, u32[]{:S(2)}, u32[]{:S(2)}) collective-permute-start(bf16[128,1152]{1,0:T(8,128)(2,1)S(1)} %get-tuple-element.90), channel_id=1, source_target_pairs={{0,3},{1,2},{2,1},{3,0},{4,7},{5,6},{6,5},{7,4},{8,11},{9,10},{10,... | collective-permute-start | bytes 884744 | tf_op jit(solution)/shard_map/ppermute | solution.py:360
  68.3 23.0 %collective-permute-start.34 = (bf16[128,1408]{1,0:T(8,128)(2,1)S(1)}, bf16[128,1408]{1,0:T(8,128)(2,1)S(1)}, u32[]{:S(2)}, u32[]{:S(2)}) collective-permute-start(bf16[128,1408]{1,0:T(8,128)(2,1)S(1)} %get-tuple-element.80), channel_id=1, source_target_pairs={{0,1},{1,0},{2,3},{3,2},{4,5},{5,4},{6,7},{7,6},{8,9},{9,8},{10,11... | collective-permute-start | bytes 1081352 | tf_op jit(solution)/shard_map/ppermute | solution.py:360
  70.0 15.9 %collective-permute-start.38 = (bf16[128,1280]{1,0:T(8,128)(2,1)S(1)}, bf16[128,1280]{1,0:T(8,128)(2,1)S(1)}, u32[]{:S(2)}, u32[]{:S(2)}) collective-permute-start(bf16[128,1280]{1,0:T(8,128)(2,1)S(1)} %get-tuple-element.85), channel_id=1, source_target_pairs={{0,2},{1,3},{2,0},{3,1},{4,6},{5,7},{6,4},{7,5},{8,10},{9,11},{10,... | collective-permute-start | bytes 983048 | tf_op jit(solution)/shard_map/ppermute | solution.py:360
  70.4 19.5 %collective-permute-start.39 = (bf16[128,1280]{1,0:T(8,128)(2,1)S(1)}, bf16[128,1280]{1,0:T(8,128)(2,1)S(1)}, u32[]{:S(2)}, u32[]{:S(2)}) collective-permute-start(bf16[128,1280]{1,0:T(8,128)(2,1)S(1)} %get-tuple-element.86), channel_id=1, source_target_pairs={{0,3},{1,2},{2,1},{3,0},{4,7},{5,6},{6,5},{7,4},{8,11},{9,10},{10,... | collective-permute-start | bytes 983048 | tf_op jit(solution)/shard_map/ppermute | solution.py:360
  78.8 25.5 %collective-permute-start.35 = (bf16[128,1408]{1,0:T(8,128)(2,1)S(1)}, bf16[128,1408]{1,0:T(8,128)(2,1)S(1)}, u32[]{:S(2)}, u32[]{:S(2)}) collective-permute-start(bf16[128,1408]{1,0:T(8,128)(2,1)S(1)} %get-tuple-element.81), channel_id=1, source_target_pairs={{0,2},{1,3},{2,0},{3,1},{4,6},{5,7},{6,4},{7,5},{8,10},{9,11},{10,... | collective-permute-start | bytes 1081352 | tf_op jit(solution)/shard_map/ppermute | solution.py:360
  79.9 24.4 %collective-permute-start.36 = (bf16[128,1408]{1,0:T(8,128)(2,1)S(1)}, bf16[128,1408]{1,0:T(8,128)(2,1)S(1)}, u32[]{:S(2)}, u32[]{:S(2)}) collective-permute-start(bf16[128,1408]{1,0:T(8,128)(2,1)S(1)} %get-tuple-element.82), channel_id=1, source_target_pairs={{0,3},{1,2},{2,1},{3,0},{4,7},{5,6},{6,5},{7,4},{8,11},{9,10},{10,... | collective-permute-start | bytes 1081352 | tf_op jit(solution)/shard_map/ppermute | solution.py:360
  85.9 22.5 %collective-permute-start.31 = (bf16[128,1536]{1,0:T(8,128)(2,1)S(1)}, bf16[128,1536]{1,0:T(8,128)(2,1)S(1)}, u32[]{:S(2)}, u32[]{:S(2)}) collective-permute-start(bf16[128,1536]{1,0:T(8,128)(2,1)S(1)} %get-tuple-element.76), channel_id=1, source_target_pairs={{0,1},{1,0},{2,3},{3,2},{4,5},{5,4},{6,7},{7,6},{8,9},{9,8},{10,11... | collective-permute-start | bytes 1179656 | tf_op jit(solution)/shard_map/ppermute | solution.py:360
  89.9 30.8 %collective-permute-start.32 = (bf16[128,1536]{1,0:T(8,128)(2,1)S(1)}, bf16[128,1536]{1,0:T(8,128)(2,1)S(1)}, u32[]{:S(2)}, u32[]{:S(2)}) collective-permute-start(bf16[128,1536]{1,0:T(8,128)(2,1)S(1)} %get-tuple-element.77), channel_id=1, source_target_pairs={{0,2},{1,3},{2,0},{3,1},{4,6},{5,7},{6,4},{7,5},{8,10},{9,11},{10,... | collective-permute-start | bytes 1179656 | tf_op jit(solution)/shard_map/ppermute | solution.py:360
  91.3 29.4 %collective-permute-start.33 = (bf16[128,1536]{1,0:T(8,128)(2,1)S(1)}, bf16[128,1536]{1,0:T(8,128)(2,1)S(1)}, u32[]{:S(2)}, u32[]{:S(2)}) collective-permute-start(bf16[128,1536]{1,0:T(8,128)(2,1)S(1)} %get-tuple-element.78), channel_id=1, source_target_pairs={{0,3},{1,2},{2,1},{3,0},{4,7},{5,6},{6,5},{7,4},{8,11},{9,10},{10,... | collective-permute-start | bytes 1179656 | tf_op jit(solution)/shard_map/ppermute | solution.py:360
  143.4 36.0 %collective-permute-start.43 = (bf16[128,1536]{1,0:T(8,128)(2,1)S(1)}, bf16[128,1536]{1,0:T(8,128)(2,1)S(1)}, u32[]{:S(2)}, u32[]{:S(2)}) collective-permute-start(bf16[128,1536]{1,0:T(8,128)(2,1)S(1)} %get-tuple-element.92), channel_id=1, source_target_pairs={{0,1},{1,0},{2,3},{3,2},{4,5},{5,4},{6,7},{7,6},{8,9},{9,8},{10,11... | collective-permute-start | bytes 1179656 | tf_op jit(solution)/shard_map/ppermute | solution.py:360
  144.6 32.7 %collective-permute-start.49 = (bf16[128,1280]{1,0:T(8,128)(2,1)S(1)}, bf16[128,1280]{1,0:T(8,128)(2,1)S(1)}, u32[]{:S(2)}, u32[]{:S(2)}) collective-permute-start(bf16[128,1280]{1,0:T(8,128)(2,1)S(1)} %get-tuple-element.100), channel_id=1, source_target_pairs={{0,1},{1,0},{2,3},{3,2},{4,5},{5,4},{6,7},{7,6},{8,9},{9,8},{10,11... | collective-permute-start | bytes 983048 | tf_op jit(solution)/shard_map/ppermute | solution.py:360
  145.5 35.0 %collective-permute-start.44 = (bf16[128,1536]{1,0:T(8,128)(2,1)S(1)}, bf16[128,1536]{1,0:T(8,128)(2,1)S(1)}, u32[]{:S(2)}, u32[]{:S(2)}) collective-permute-start(bf16[128,1536]{1,0:T(8,128)(2,1)S(1)} %get-tuple-element.93), channel_id=1, source_target_pairs={{0,2},{1,3},{2,0},{3,1},{4,6},{5,7},{6,4},{7,5},{8,10},{9,11},{10,... | collective-permute-start | bytes 1179656 | tf_op jit(solution)/shard_map/ppermute | solution.py:360
  147.5 33.6 %collective-permute-start.45 = (bf16[128,1536]{1,0:T(8,128)(2,1)S(1)}, bf16[128,1536]{1,0:T(8,128)(2,1)S(1)}, u32[]{:S(2)}, u32[]{:S(2)}) collective-permute-start(bf16[128,1536]{1,0:T(8,128)(2,1)S(1)} %get-tuple-element.94), channel_id=1, source_target_pairs={{0,3},{1,2},{2,1},{3,0},{4,7},{5,6},{6,5},{7,4},{8,11},{9,10},{10,... | collective-permute-start | bytes 1179656 | tf_op jit(solution)/shard_map/ppermute | solution.py:360
  148.1 28.8 %collective-permute-start.54 = (bf16[128,1152]{1,0:T(8,128)(2,1)S(1)}, bf16[128,1152]{1,0:T(8,128)(2,1)S(1)}, u32[]{:S(2)}, u32[]{:S(2)}) collective-permute-start(bf16[128,1152]{1,0:T(8,128)(2,1)S(1)} %get-tuple-element.106), channel_id=1, source_target_pairs={{0,3},{1,2},{2,1},{3,0},{4,7},{5,6},{6,5},{7,4},{8,11},{9,10},{10,... | collective-permute-start | bytes 884744 | tf_op jit(solution)/shard_map/ppermute | solution.py:360
  177.3 26.1 %collective-permute-start.47 = (bf16[128,1408]{1,0:T(8,128)(2,1)S(1)}, bf16[128,1408]{1,0:T(8,128)(2,1)S(1)}, u32[]{:S(2)}, u32[]{:S(2)}) collective-permute-start(bf16[128,1408]{1,0:T(8,128)(2,1)S(1)} %get-tuple-element.97), channel_id=1, source_target_pairs={{0,2},{1,3},{2,0},{3,1},{4,6},{5,7},{6,4},{7,5},{8,10},{9,11},{10,... | collective-permute-start | bytes 1081352 | tf_op jit(solution)/shard_map/ppermute | solution.py:360
  179.4 25.2 %collective-permute-start.48 = (bf16[128,1408]{1,0:T(8,128)(2,1)S(1)}, bf16[128,1408]{1,0:T(8,128)(2,1)S(1)}, u32[]{:S(2)}, u32[]{:S(2)}) collective-permute-start(bf16[128,1408]{1,0:T(8,128)(2,1)S(1)} %get-tuple-element.98), channel_id=1, source_target_pairs={{0,3},{1,2},{2,1},{3,0},{4,7},{5,6},{6,5},{7,4},{8,11},{9,10},{10,... | collective-permute-start | bytes 1081352 | tf_op jit(solution)/shard_map/ppermute | solution.py:360
  180.4 27.9 %collective-permute-start.50 = (bf16[128,1280]{1,0:T(8,128)(2,1)S(1)}, bf16[128,1280]{1,0:T(8,128)(2,1)S(1)}, u32[]{:S(2)}, u32[]{:S(2)}) collective-permute-start(bf16[128,1280]{1,0:T(8,128)(2,1)S(1)} %get-tuple-element.101), channel_id=1, source_target_pairs={{0,2},{1,3},{2,0},{3,1},{4,6},{5,7},{6,4},{7,5},{8,10},{9,11},{10,... | collective-permute-start | bytes 983048 | tf_op jit(solution)/shard_map/ppermute | solution.py:360
  181.1 28.5 %collective-permute-start.51 = (bf16[128,1280]{1,0:T(8,128)(2,1)S(1)}, bf16[128,1280]{1,0:T(8,128)(2,1)S(1)}, u32[]{:S(2)}, u32[]{:S(2)}) collective-permute-start(bf16[128,1280]{1,0:T(8,128)(2,1)S(1)} %get-tuple-element.102), channel_id=1, source_target_pairs={{0,3},{1,2},{2,1},{3,0},{4,7},{5,6},{6,5},{7,4},{8,11},{9,10},{10,... | collective-permute-start | bytes 983048 | tf_op jit(solution)/shard_map/ppermute | solution.py:360
  188.2 22.1 %collective-permute-start.76 = (bf16[128,256]{1,0:T(8,128)(2,1)S(1)}, bf16[128,256]{1,0:T(8,128)(2,1)S(1)}, u32[]{:S(2)}, u32[]{:S(2)}) collective-permute-start(bf16[128,256]{1,0:T(8,128)(2,1)S(1)} %get-tuple-element.135), channel_id=1, source_target_pairs={{0,4},{4,0},{8,12},{12,8},{16,20},{20,16},{24,28},{28,24},{1,5},{5... | collective-permute-start | bytes 196616 | tf_op jit(solution)/shard_map/ppermute | solution.py:369
  218.5 11.5 %collective-permute-start.70 = (bf16[128,256]{1,0:T(8,128)(2,1)S(1)}, bf16[128,256]{1,0:T(8,128)(2,1)S(1)}, u32[]{:S(2)}, u32[]{:S(2)}) collective-permute-start(bf16[128,256]{1,0:T(8,128)(2,1)S(1)} %get-tuple-element.128), channel_id=1, source_target_pairs={{0,8},{4,12},{8,0},{12,4},{16,24},{20,28},{24,16},{28,20},{1,9},{5... | collective-permute-start | bytes 196616 | tf_op jit(solution)/shard_map/ppermute | solution.py:369
  219.9 11.6 %collective-permute-start.72 = (bf16[128,256]{1,0:T(8,128)(2,1)S(1)}, bf16[128,256]{1,0:T(8,128)(2,1)S(1)}, u32[]{:S(2)}, u32[]{:S(2)}) collective-permute-start(bf16[128,256]{1,0:T(8,128)(2,1)S(1)} %get-tuple-element.130), channel_id=1, source_target_pairs={{0,16},{4,20},{8,24},{12,28},{16,0},{20,4},{24,8},{28,12},{1,17},{... | collective-permute-start | bytes 196616 | tf_op jit(solution)/shard_map/ppermute | solution.py:369
  242.5 14.1 %collective-permute-start.57 = (bf16[128,256]{1,0:T(8,128)(2,1)S(1)}, bf16[128,256]{1,0:T(8,128)(2,1)S(1)}, u32[]{:S(2)}, u32[]{:S(2)}) collective-permute-start(bf16[128,256]{1,0:T(8,128)(2,1)S(1)} %get-tuple-element.113), channel_id=1, source_target_pairs={{0,12},{4,8},{8,4},{12,0},{16,28},{20,24},{24,20},{28,16},{1,13},{... | collective-permute-start | bytes 196616 | tf_op jit(solution)/shard_map/ppermute | solution.py:369
  242.5 15.8 %collective-permute-start.58 = (bf16[128,256]{1,0:T(8,128)(2,1)S(1)}, bf16[128,256]{1,0:T(8,128)(2,1)S(1)}, u32[]{:S(2)}, u32[]{:S(2)}) collective-permute-start(bf16[128,256]{1,0:T(8,128)(2,1)S(1)} %get-tuple-element.114), channel_id=1, source_target_pairs={{0,16},{4,20},{8,24},{12,28},{16,0},{20,4},{24,8},{28,12},{1,17},{... | collective-permute-start | bytes 196616 | tf_op jit(solution)/shard_map/ppermute | solution.py:369
  (61 other events, 527.5 us)

commit v2 on v1

--- a/solution.py
+++ b/solution.py
@@ -69,7 +69,7 @@
     return dims[3] - k
 
 
-def pack_kernel(dims, k, meta, *refs):
+def pack_kernel(dims, k, pieces, meta, *refs):
     n_mat, n_pts, act, nact = dims
     each = act // n_pts
     arrived, earlier = refs[:n_mat], refs[n_mat : n_mat + k]
@@ -98,15 +98,17 @@
             def _(source=source, o=o):
                 for slot in range(slots_in(dims, k)):
                     b = table[o * (nact + 1) + slot]
-                    packed[o][:, slot * BLOCK : (slot + 1) * BLOCK] = source[:, lanes(b)]
-
-
-def pack(dims, k, meta, arrived, earlier):
+                    for h in range(pieces):
+                        part = source[h * BLOCK // pieces : (h + 1) * BLOCK // pieces, lanes(b)]
+                        packed[h * n_pts + o][:, slot * BLOCK : (slot + 1) * BLOCK] = part
+
+
+def pack(dims, k, pieces, meta, arrived, earlier):
     n_mat, n_pts, act, nact = dims
     shapes = [jax.ShapeDtypeStruct((BLOCK, act * BLOCK), jnp.bfloat16)]
-    shapes += [jax.ShapeDtypeStruct((BLOCK, slots_in(dims, k) * BLOCK), jnp.bfloat16)] * n_pts
+    shapes += [jax.ShapeDtypeStruct((BLOCK // pieces, slots_in(dims, k) * BLOCK), jnp.bfloat16)] * (pieces * n_pts)
     out = pl.pallas_call(
-        functools.partial(pack_kernel, dims, k),
+        functools.partial(pack_kernel, dims, k, pieces),
         out_shape=shapes,
         in_specs=[pl.BlockSpec(memory_space=pltpu.SMEM)] + [VM] * (n_mat + k),
         out_specs=[VM] * len(shapes),
@@ -114,7 +116,7 @@
         compiler_params=GRANT,
         cost_estimate=cost(0, 2 * BLOCK * BLOCK * (act + n_pts * nact)),
     )(meta, *arrived, *earlier)
-    return out[0], out[1:]
+    return out[0], [out[1 + h * n_pts : 1 + (h + 1) * n_pts] for h in range(pieces)]
 
 
 def transpose_kernel(given, out):
@@ -149,8 +151,9 @@
     return half if cases <= 4 and half % BLOCK == 0 else 2 * BLOCK
 
 
-def density_kernel(dims, k, tile, last, meta, *refs):
-    _, n_pts, act, nact = dims
+def density_kernel(dims, k, h, tile, last, meta, *refs):
+    _, n_pts, act, nact = dims
+    height = refs[0].shape[0]
     each = act // n_pts
     parts, flipped, before, after, place, table, left = refs[:n_pts], *refs[n_pts:]
     invert(dims, meta, place)
@@ -164,7 +167,7 @@
         rows.append((jnp.maximum(place[column * each + jnp.maximum(row, 0)], 0), row >= 0))
         for slot in range(slots_in(dims, k)):
             j = table[o * (nact + 1) + slot]
-            left[o * BLOCK : (o + 1) * BLOCK, lanes(j)] = parts[o][:, slot * BLOCK : (slot + 1) * BLOCK]
+            left[o * height : (o + 1) * height, lanes(j)] = parts[o][:, slot * BLOCK : (slot + 1) * BLOCK]
 
     @pl.loop(0, points // tile)
     def _(t):
@@ -172,8 +175,9 @@
         inner = jnp.dot(left[...], flipped[:, at], preferred_element_type=jnp.float32)
         total = before[:, at]
         for o, (spot, valid) in enumerate(rows):
-            own = flipped[rows_at(spot), at].astype(jnp.float32)
-            share = jnp.sum(inner[o * BLOCK : (o + 1) * BLOCK] * own, axis=0, keepdims=True)
+            where = pl.ds(pl.multiple_of(spot * BLOCK + h * height, height), height)
+            own = flipped[where, at].astype(jnp.float32)
+            share = jnp.sum(inner[o * height : (o + 1) * height] * own, axis=0, keepdims=True)
             total = total + jnp.where(valid, share, jnp.zeros_like(share))
         if last:
             point = t * tile + lax.broadcasted_iota(jnp.int32, total.shape, 1)
@@ -181,22 +185,57 @@
         after[:, at] = total
 
 
-def density(dims, k, last, meta, parts, flipped, before):
+def density(dims, k, h, meta, parts, flipped, before):
     _, n_pts, act, nact = dims
     orbitals, points = flipped.shape
+    height = parts[0].shape[0]
     return pl.pallas_call(
-        functools.partial(density_kernel, dims, k, tile_of(points, n_pts), last),
+        functools.partial(density_kernel, dims, k, h, tile_of(points, n_pts), False),
         out_shape=jax.ShapeDtypeStruct((1, points), jnp.float32),
         in_specs=[pl.BlockSpec(memory_space=pltpu.SMEM)] + [VM] * (n_pts + 2),
         out_specs=VM,
         scratch_shapes=[
             pltpu.SMEM((act,), jnp.int32),
             pltpu.SMEM((n_pts * (nact + 1),), jnp.int32),
+            pltpu.VMEM((n_pts * height, orbitals), jnp.bfloat16),
+        ],
+        compiler_params=GRANT,
+        cost_estimate=cost(2 * n_pts * height * orbitals * points, 2 * orbitals * points),
+    )(meta, *parts, flipped, before)
+
+
+def turn_kernel(dims, k, h, tile, meta, *refs):
+    _, n_pts, _, _ = dims
+    parts, (flipped, before, basis, kern, pert, weight) = refs[:n_pts], refs[n_pts : n_pts + 6]
+    out, (n, n_again, place, table, short, left, right) = refs[n_pts + 6 : -7], refs[-7:]
+    density_kernel(dims, k, h, tile, True, meta, *parts, flipped, before, n, place, table, short)
+    n_again[...] = n[...]
+    response_kernel(dims, (0,), tile, meta, flipped, basis, n, kern, pert, weight, *out, place, table, left, right)
+
+
+def turn(dims, k, h, meta, parts, flipped, before, basis, kern, pert, weight):
+    _, n_pts, act, nact = dims
+    orbitals, points = flipped.shape
+    height = parts[0].shape[0]
+    shapes = [jax.ShapeDtypeStruct((BLOCK, slots_out(dims, 0) * BLOCK), jnp.bfloat16)] * n_pts
+    shapes += [jax.ShapeDtypeStruct((1, points), jnp.float32)] * 2
+    out = pl.pallas_call(
+        functools.partial(turn_kernel, dims, k, h, tile_of(points, n_pts)),
+        out_shape=shapes,
+        in_specs=[pl.BlockSpec(memory_space=pltpu.SMEM)] + [VM] * (n_pts + 6),
+        out_specs=[VM] * len(shapes),
+        scratch_shapes=[
+            pltpu.SMEM((act,), jnp.int32),
+            pltpu.SMEM((n_pts * (nact + 1),), jnp.int32),
+            pltpu.VMEM((n_pts * height, orbitals), jnp.bfloat16),
+            pltpu.VMEM((n_pts * BLOCK, points), jnp.bfloat16),
             pltpu.VMEM((n_pts * BLOCK, orbitals), jnp.bfloat16),
         ],
-        compiler_params=GRANT,
-        cost_estimate=cost(2 * n_pts * BLOCK * orbitals * points, 2 * orbitals * points),
-    )(meta, *parts, flipped, before)
+        compiler_params=pltpu.CompilerParams(vmem_limit_bytes=26 << 20),
+        cost_estimate=cost(2 * n_pts * (BLOCK + height) * orbitals * points, 4 * orbitals * points),
+        name="turn",
+    )(meta, *parts, flipped, before, basis, kern, pert, weight)
+    return out[:n_pts], out[-2], out[-1]
 
 
 def response_kernel(dims, ranks, tile, meta, *refs):
@@ -345,8 +384,8 @@
     )(meta, *given, *more)
 
 
-def emissions(row_blocks):
-    return [(0,)] + ([tuple(range(1, row_blocks))] if row_blocks > 1 else [])
+def pieces_of(k, row_blocks):
+    return 2 if k == row_blocks - 1 else 1
 
 
 def body(dens_blocks, basis_values, kernel, perturbation, quad_weight, point_count, active_blocks, block_pattern):
@@ -386,19 +425,24 @@
 
     parts, stages = [], []
     for k in range(row_blocks):
-        held, packed = pack(dims, k, meta, arrived[k], stages)
+        held, packed = pack(dims, k, pieces_of(k, row_blocks), meta, arrived[k], stages)
         stages.append(held)
-        parts.append([packed[0]] + [to_peer(packed[o], o) for o in range(1, n_pts)])
+        for h, piece in enumerate(packed):
+            parts.append((k, h, [piece[0]] + [to_peer(piece[o], o) for o in range(1, n_pts)]))
 
     n = jnp.zeros((1, points), jnp.float32)
+    for k, h, piece in parts[:-1]:
+        n = density(dims, k, h, meta, piece, flipped, n)
+    k, h, piece = parts[-1]
+    sent, n, n_response = turn(dims, k, h, meta, piece, flipped, n, basis, kernel, perturbation, quad_weight)
+    emitted = [sent]
+
+    strips = []
     for k in range(row_blocks):
-        n = density(dims, k, k == row_blocks - 1, meta, parts[k], flipped, n)
-
-    strips = []
-    for ranks in emissions(row_blocks):
-        several = response(dims, ranks, meta, flipped, basis, n, kernel, perturbation, quad_weight)
-        for k, sent in zip(ranks, several):
-            strips.append([sent[0]] + [to_peer(sent[o], o) for o in range(1, n_pts)])
+        if k == 1:
+            later = tuple(range(1, row_blocks))
+            emitted += response(dims, later, meta, flipped, basis, n, kernel, perturbation, quad_weight)
+        strips.append([emitted[k][0]] + [to_peer(emitted[k][o], o) for o in range(1, n_pts)])
 
     inner, result = [], None
     for k in range(row_blocks):
@@ -406,7 +450,7 @@
         inner.append(pairs)
         back = across(cut)
         result = widen(dims, k * BLOCK, BLOCK, dens_blocks.shape[1], meta, back, result)
-    return result, n
+    return result, n_response
 
 
 def solution(mesh):

time: 262 us -> 271 us (1.034)
  waiting for transfers between devices: 97.6 us -> 120 us
  starting transfers between devices: 101 us -> 86.9 us
    ppermute x56, waiting for transfers between devices: 26.2 us -> 44.9 us  [across(): out[d] = lax.ppermute(values[d], 'mat', [(i, i ^ d) for i in range(n_mat)])]
    ppermute x56, starting transfers between devices: 67.5 us -> 53.2 us  [across(): out[d] = lax.ppermute(values[d], 'mat', [(i, i ^ d) for i in range(n_mat)])]
    pallas_call x8 -> x9, Pallas kernels: 24 us -> 29.1 us  [the longest x4 15 us: density(): pl.pallas_call(functools.partial(density_kernel, dims, k, h, tile_of(poin...]
    pallas_call x2 -> x1, Pallas kernels: 15.4 us -> 11.3 us  [response(): pl.pallas_call(functools.partial(response_kernel, dims, ranks, tile_of(or...]
    ppermute x27 -> x30, waiting for transfers between devices: 71.4 us -> 75.2 us  [to_peer(): return lax.ppermute(value, 'pts', [(i, i ^ o) for i in range(n_pts)])]
    ppermute x27 -> x30, starting transfers between devices: 33.5 us -> 33.7 us  [to_peer(): return lax.ppermute(value, 'pts', [(i, i ^ o) for i in range(n_pts)])]
  transfers between devices with their start and end apart: 83 -> 86, of which waited for: 21 -> 34; matrix products, arithmetic and copies ran while one was open for 0% -> 0% of each run, Pallas kernels for 15% -> 14%
where the time goes in v2:
time: 271 us; the launch traced here: 270 us
  waiting for transfers between devices  120 us (44%)
  starting transfers between devices  86.9 us (32%)
  Pallas kernels  57 us (21%)
  local copies, waits for them, and re-layouts  4.33 us (2%)
    ppermute x30, waiting for transfers between devices, to_peer(): return lax.ppermute(value, 'pts', [(i, i ^ o) for i in range(n_pts)])  75.2 us
    ppermute x56, starting transfers between devices, across(): out[d] = lax.ppermute(values[d], 'mat', [(i, i ^ d) for i in range(n_mat)])  53.2 us
    ppermute x56, waiting for transfers between devices, across(): out[d] = lax.ppermute(values[d], 'mat', [(i, i ^ d) for i in range(n_mat)])  44.9 us
    ppermute x30, starting transfers between devices, to_peer(): return lax.ppermute(value, 'pts', [(i, i ^ o) for i in range(n_pts)])  33.7 us
    pallas_call x4, Pallas kernels, density(): pl.pallas_call(functools.partial(density_kernel, dims, k, h, tile_of(poin...  15 us
    pallas_call x1, Pallas kernels, response(): pl.pallas_call(functools.partial(response_kernel, dims, ranks, tile_of(or...  11.3 us
    pallas_call x4, Pallas kernels, combine(): pl.pallas_call(functools.partial(combine_kernel, dims, k), out_shape=shap...  8.34 us
    pallas_call x4, Pallas kernels, pack(): pl.pallas_call(functools.partial(pack_kernel, dims, k, pieces), out_shape...  7.14 us
  transfers between devices with their start and end apart: 86, of which 34 were waited for; matrix products, arithmetic and copies ran while one was open for 0% of the time, Pallas kernels for 14%

profile of v2, /device:TPU:0, one launch (start us, length us, event | category | flops | bytes accessed | tf_op | source)
XLA Modules:
  0.0 270.0 jit_solution(5679183046362737050)
XLA Ops:
  2.5 4.6 %collective-permute-start.30 = (bf16[128,256]{1,0:T(8,128)(2,1)S(1)}, bf16[128,256]{1,0:T(8,128)(2,1)S(1)}, u32[]{:S(2)}, u32[]{:S(2)}) collective-permute-start(bf16[128,256]{1,0:T(8,128)(2,1)S(1)} %get-tuple-element.154), channel_id=1, source_target_pairs={{0,28},{4,24},{8,20},{12,16},{16,12},{20,8},{24,4},{28,0},{1,29},{... | collective-permute-start | bytes 196616 | tf_op jit(solution)/shard_map/ppermute | solution.py:408
  7.1 2.4 collective-permute-start.2
  15.0 2.8 %collective-permute-done.28.refs_5_ = bf16[128,256]{1,0:T(8,128)(2,1)S(1)} collective-permute-done((bf16[128,256]{1,0:T(8,128)(2,1)S(1)}, bf16[128,256]{1,0:T(8,128)(2,1)S(1)}, u32[]{:S(2)}, u32[]{:S(2)}) %collective-permute-start.28) | collective-permute-done | bytes 65568 | tf_op jit(solution)/shard_map/ppermute | solution.py:408
  22.5 2.5 collective-permute-start.15
  27.8 5.9 %collective-permute-done.21.refs_5_ = bf16[128,256]{1,0:T(8,128)(2,1)S(1)} collective-permute-done((bf16[128,256]{1,0:T(8,128)(2,1)S(1)}, bf16[128,256]{1,0:T(8,128)(2,1)S(1)}, u32[]{:S(2)}, u32[]{:S(2)}) %collective-permute-start.21) | collective-permute-done | bytes 65568 | tf_op jit(solution)/shard_map/ppermute | solution.py:408
  35.7 2.3 collective-permute-done.14.refs_5_
  42.4 3.5 %collective-permute-start.9 = (bf16[128,256]{1,0:T(8,128)(2,1)S(1)}, bf16[128,256]{1,0:T(8,128)(2,1)S(1)}, u32[]{:S(2)}, u32[]{:S(2)}) collective-permute-start(bf16[128,256]{1,0:T(8,128)(2,1)S(1)} %get-tuple-element.177), channel_id=1, source_target_pairs={{0,28},{4,24},{8,20},{12,16},{16,12},{20,8},{24,4},{28,0},{1,29},{... | collective-permute-start | bytes 196616 | tf_op jit(solution)/shard_map/ppermute | solution.py:408
  56.8 2.8 %collective-permute-done.7.refs_5_ = bf16[128,256]{1,0:T(8,128)(2,1)S(1)} collective-permute-done((bf16[128,256]{1,0:T(8,128)(2,1)S(1)}, bf16[128,256]{1,0:T(8,128)(2,1)S(1)}, u32[]{:S(2)}, u32[]{:S(2)}) %collective-permute-start.7) | collective-permute-done | bytes 65568 | tf_op jit(solution)/shard_map/ppermute | solution.py:408
  65.9 5.3 %collective-permute-done.29.refs_6_ = bf16[128,256]{1,0:T(8,128)(2,1)S(1)} collective-permute-done((bf16[128,256]{1,0:T(8,128)(2,1)S(1)}, bf16[128,256]{1,0:T(8,128)(2,1)S(1)}, u32[]{:S(2)}, u32[]{:S(2)}) %collective-permute-start.29) | collective-permute-done | bytes 65568 | tf_op jit(solution)/shard_map/ppermute | solution.py:408
  79.0 2.5 shard_map.98
  87.2 4.2 %shard_map.99.refs_5_ = f32[1,1536]{1,0:T(1,128)S(1)} custom-call(s32[307]{0:T(512)S(1)} %concatenate.3.meta, bf16[128,1152]{1,0:T(8,128)(2,1)S(1)} %get-tuple-element.97.refs_0_, bf16[128,1152]{1,0:T(8,128)(2,1)S(1)} %collective-permute-done.43.refs_1_, bf16[128,1152]{1,0:T(8,128)(2,1)S(1)} %collective-permute-done.44.refs_2_, ...), custom_call_target="tpu_custom_call" | custom-call | flops 2415919104 | bytes 4718592 | tf_op jit(solution)/shard_map/pallas_call | solution.py:192
  94.1 4.0 %shard_map.100.refs_5_ = f32[1,1536]{1,0:T(1,128)S(1)} custom-call(s32[307]{0:T(512)S(1)} %concatenate.3.meta, bf16[128,1280]{1,0:T(8,128)(2,1)S(1)} %get-tuple-element.93.refs_0_, bf16[128,1280]{1,0:T(8,128)(2,1)S(1)} %collective-permute-done.40.refs_1_, bf16[128,1280]{1,0:T(8,128)(2,1)S(1)} %collective-permute-done.41.refs_2_, ...), custom_call_target="tpu_custom_call" | custom-call | flops 2415919104 | bytes 4718592 | tf_op jit(solution)/shard_map/pallas_call | solution.py:192
  98.1 9.5 %collective-permute-done.34.refs_1_ = bf16[64,1536]{1,0:T(8,128)(2,1)S(1)} collective-permute-done((bf16[64,1536]{1,0:T(8,128)(2,1)S(1)}, bf16[64,1536]{1,0:T(8,128)(2,1)S(1)}, u32[]{:S(2)}, u32[]{:S(2)}) %collective-permute-start.34) | collective-permute-done | bytes 196640 | tf_op jit(solution)/shard_map/ppermute | solution.py:399
  107.6 2.5 collective-permute-start.32
  113.1 4.0 %shard_map.101.refs_5_ = f32[1,1536]{1,0:T(1,128)S(1)} custom-call(s32[307]{0:T(512)S(1)} %concatenate.3.meta, bf16[128,1408]{1,0:T(8,128)(2,1)S(1)} %get-tuple-element.89.refs_0_, bf16[128,1408]{1,0:T(8,128)(2,1)S(1)} %collective-permute-done.37.refs_1_, bf16[128,1408]{1,0:T(8,128)(2,1)S(1)} %collective-permute-done.38.refs_2_, ...), custom_call_target="tpu_custom_call" | custom-call | flops 2415919104 | bytes 4718592 | tf_op jit(solution)/shard_map/pallas_call | solution.py:192
  117.2 8.2 %collective-permute-done.35.refs_2_ = bf16[64,1536]{1,0:T(8,128)(2,1)S(1)} collective-permute-done((bf16[64,1536]{1,0:T(8,128)(2,1)S(1)}, bf16[64,1536]{1,0:T(8,128)(2,1)S(1)}, u32[]{:S(2)}, u32[]{:S(2)}) %collective-permute-start.35) | collective-permute-done | bytes 196640 | tf_op jit(solution)/shard_map/ppermute | solution.py:399
  125.4 2.8 %shard_map.102.refs_5_ = f32[1,1536]{1,0:T(1,128)S(1)} custom-call(s32[307]{0:T(512)S(1)} %concatenate.3.meta, bf16[64,1536]{1,0:T(8,128)(2,1)S(1)} %get-tuple-element.85.refs_0_, bf16[64,1536]{1,0:T(8,128)(2,1)S(1)} %collective-permute-done.34.refs_1_, bf16[64,1536]{1,0:T(8,128)(2,1)S(1)} %collective-permute-done.35.refs_2_, ...), custom_call_target="tpu_custom_call" | custom-call | flops 1207959552 | bytes 4718592 | tf_op jit(solution)/shard_map/pallas_call | solution.py:192
  128.2 7.0 %turn.1 = (bf16[128,1536]{1,0:T(8,128)(2,1)S(1)}, bf16[128,1536]{1,0:T(8,128)(2,1)S(1)}, bf16[128,1536]{1,0:T(8,128)(2,1)S(1)}, bf16[128,1536]{1,0:T(8,128)(2,1)...) custom-call(s32[307]{0:T(512)S(1)} %concatenate.3.meta, bf16[64,1536]{1,0:T(8,128)(2,1)S(1)} %get-tuple-element.81.refs_0_, ...), custom_call_target="tpu_custom_call" | custom-call | flops 3623878656 | bytes 9437184 | tf_op jit(solution)/shard_map/turn/pallas_call | solution.py:222
  135.2 11.3 %shard_map.103 = (bf16[128,1408]{1,0:T(8,128)(2,1)S(1)}, bf16[128,1408]{1,0:T(8,128)(2,1)S(1)}, bf16[128,1408]{1,0:T(8,128)(2,1)S(1)}, bf16[128,1408]{1,0:T(8,12...) custom-call(s32[307]{0:T(512)S(1)} %concatenate.3.meta, ...), custom_call_target="tpu_custom_call" | custom-call | flops 7247757312 | bytes 9437184 | tf_op jit(solution)/shard_map/pallas_call | solution.py:277
  151.4 5.0 %collective-permute-done.55.refs_13_ = bf16[128,1152]{1,0:T(8,128)(2,1)S(1)} collective-permute-done((bf16[128,1152]{1,0:T(8,128)(2,1)S(1)}, bf16[128,1152]{1,0:T(8,128)(2,1)S(1)}, u32[]{:S(2)}, u32[]{:S(2)}) %collective-permute-start.55) | collective-permute-done | bytes 294944 | tf_op jit(solution)/shard_map/ppermute | solution.py:399
  159.6 27.2 %collective-permute-done.57.refs_15_ = bf16[128,1152]{1,0:T(8,128)(2,1)S(1)} collective-permute-done((bf16[128,1152]{1,0:T(8,128)(2,1)S(1)}, bf16[128,1152]{1,0:T(8,128)(2,1)S(1)}, u32[]{:S(2)}, u32[]{:S(2)}) %collective-permute-start.57) | collective-permute-done | bytes 294944 | tf_op jit(solution)/shard_map/ppermute | solution.py:399
  186.9 3.4 %collective-permute-start.51 = (bf16[128,1408]{1,0:T(8,128)(2,1)S(1)}, bf16[128,1408]{1,0:T(8,128)(2,1)S(1)}, u32[]{:S(2)}, u32[]{:S(2)}) collective-permute-start(bf16[128,1408]{1,0:T(8,128)(2,1)S(1)} %get-tuple-element.109), channel_id=1, source_target_pairs={{0,3},{1,2},{2,1},{3,0},{4,7},{5,6},{6,5},{7,4},{8,11},{9,10},{10,... | collective-permute-start | bytes 1081352 | tf_op jit(solution)/shard_map/ppermute | solution.py:399
  193.5 4.6 %collective-permute-done.49.refs_5_ = bf16[128,1408]{1,0:T(8,128)(2,1)S(1)} collective-permute-done((bf16[128,1408]{1,0:T(8,128)(2,1)S(1)}, bf16[128,1408]{1,0:T(8,128)(2,1)S(1)}, u32[]{:S(2)}, u32[]{:S(2)}) %collective-permute-start.49) | collective-permute-done | bytes 360480 | tf_op jit(solution)/shard_map/ppermute | solution.py:399
  198.1 14.7 %collective-permute-done.50.refs_6_ = bf16[128,1408]{1,0:T(8,128)(2,1)S(1)} collective-permute-done((bf16[128,1408]{1,0:T(8,128)(2,1)S(1)}, bf16[128,1408]{1,0:T(8,128)(2,1)S(1)}, u32[]{:S(2)}, u32[]{:S(2)}) %collective-permute-start.50) | collective-permute-done | bytes 360480 | tf_op jit(solution)/shard_map/ppermute | solution.py:399
  216.4 3.4 %collective-permute-start.83 = (bf16[128,256]{1,0:T(8,128)(2,1)S(1)}, bf16[128,256]{1,0:T(8,128)(2,1)S(1)}, u32[]{:S(2)}, u32[]{:S(2)}) collective-permute-start(bf16[128,256]{1,0:T(8,128)(2,1)S(1)} %get-tuple-element.150), channel_id=1, source_target_pairs={{0,20},{4,16},{8,28},{12,24},{16,4},{20,0},{24,12},{28,8},{1,21},{... | collective-permute-start | bytes 196616 | tf_op jit(solution)/shard_map/ppermute | solution.py:408
  219.8 2.6 collective-permute-start.85
  223.7 3.4 %collective-permute-done.82.refs_4_ = bf16[128,256]{1,0:T(8,128)(2,1)S(1)} collective-permute-done((bf16[128,256]{1,0:T(8,128)(2,1)S(1)}, bf16[128,256]{1,0:T(8,128)(2,1)S(1)}, u32[]{:S(2)}, u32[]{:S(2)}) %collective-permute-start.82) | collective-permute-done | bytes 65568 | tf_op jit(solution)/shard_map/ppermute | solution.py:408
  231.5 2.5 collective-permute-start.77
  236.1 2.5 shard_map.107
  242.0 3.0 %collective-permute-done.78.refs_7_ = bf16[128,256]{1,0:T(8,128)(2,1)S(1)} collective-permute-done((bf16[128,256]{1,0:T(8,128)(2,1)S(1)}, bf16[128,256]{1,0:T(8,128)(2,1)S(1)}, u32[]{:S(2)}, u32[]{:S(2)}) %collective-permute-start.78) | collective-permute-done | bytes 65568 | tf_op jit(solution)/shard_map/ppermute | solution.py:408
  251.2 4.4 %collective-permute-done.68.refs_4_ = bf16[128,256]{1,0:T(8,128)(2,1)S(1)} collective-permute-done((bf16[128,256]{1,0:T(8,128)(2,1)S(1)}, bf16[128,256]{1,0:T(8,128)(2,1)S(1)}, u32[]{:S(2)}, u32[]{:S(2)}) %collective-permute-start.68) | collective-permute-done | bytes 65568 | tf_op jit(solution)/shard_map/ppermute | solution.py:408
  259.4 2.4 collective-permute-start.64
  (181 shorter events, 101.3 us)
Async XLA Ops:
  2.5 12.5 %collective-permute-start.30 = (bf16[128,256]{1,0:T(8,128)(2,1)S(1)}, bf16[128,256]{1,0:T(8,128)(2,1)S(1)}, u32[]{:S(2)}, u32[]{:S(2)}) collective-permute-start(bf16[128,256]{1,0:T(8,128)(2,1)S(1)} %get-tuple-element.154), channel_id=1, source_target_pairs={{0,28},{4,24},{8,20},{12,16},{16,12},{20,8},{24,4},{28,0},{1,29},{... | collective-permute-start | bytes 196616 | tf_op jit(solution)/shard_map/ppermute | solution.py:408
  21.3 12.5 %collective-permute-start.21 = (bf16[128,256]{1,0:T(8,128)(2,1)S(1)}, bf16[128,256]{1,0:T(8,128)(2,1)S(1)}, u32[]{:S(2)}, u32[]{:S(2)}) collective-permute-start(bf16[128,256]{1,0:T(8,128)(2,1)S(1)} %get-tuple-element.163), channel_id=1, source_target_pairs={{0,20},{4,16},{8,28},{12,24},{16,4},{20,0},{24,12},{28,8},{1,21},{... | collective-permute-start | bytes 196616 | tf_op jit(solution)/shard_map/ppermute | solution.py:408
  22.5 13.3 %collective-permute-start.15 = (bf16[128,256]{1,0:T(8,128)(2,1)S(1)}, bf16[128,256]{1,0:T(8,128)(2,1)S(1)}, u32[]{:S(2)}, u32[]{:S(2)}) collective-permute-start(bf16[128,256]{1,0:T(8,128)(2,1)S(1)} %get-tuple-element.170), channel_id=1, source_target_pairs={{0,24},{4,28},{8,16},{12,20},{16,8},{20,12},{24,0},{28,4},{1,25},{... | collective-permute-start | bytes 196616 | tf_op jit(solution)/shard_map/ppermute | solution.py:408
  24.9 13.1 %collective-permute-start.14 = (bf16[128,256]{1,0:T(8,128)(2,1)S(1)}, bf16[128,256]{1,0:T(8,128)(2,1)S(1)}, u32[]{:S(2)}, u32[]{:S(2)}) collective-permute-start(bf16[128,256]{1,0:T(8,128)(2,1)S(1)} %get-tuple-element.171), channel_id=1, source_target_pairs={{0,20},{4,16},{8,28},{12,24},{16,4},{20,0},{24,12},{28,8},{1,21},{... | collective-permute-start | bytes 196616 | tf_op jit(solution)/shard_map/ppermute | solution.py:408
  26.0 13.5 %collective-permute-start.13 = (bf16[128,256]{1,0:T(8,128)(2,1)S(1)}, bf16[128,256]{1,0:T(8,128)(2,1)S(1)}, u32[]{:S(2)}, u32[]{:S(2)}) collective-permute-start(bf16[128,256]{1,0:T(8,128)(2,1)S(1)} %get-tuple-element.172), channel_id=1, source_target_pairs={{0,16},{4,20},{8,24},{12,28},{16,0},{20,4},{24,8},{28,12},{1,17},{... | collective-permute-start | bytes 196616 | tf_op jit(solution)/shard_map/ppermute | solution.py:408
  48.2 24.5 %collective-permute-start.43 = (bf16[128,1152]{1,0:T(8,128)(2,1)S(1)}, bf16[128,1152]{1,0:T(8,128)(2,1)S(1)}, u32[]{:S(2)}, u32[]{:S(2)}) collective-permute-start(bf16[128,1152]{1,0:T(8,128)(2,1)S(1)} %get-tuple-element.98), channel_id=1, source_target_pairs={{0,1},{1,0},{2,3},{3,2},{4,5},{5,4},{6,7},{7,6},{8,9},{9,8},{10,11... | collective-permute-start | bytes 884744 | tf_op jit(solution)/shard_map/ppermute | solution.py:399
  56.2 29.5 %collective-permute-start.40 = (bf16[128,1280]{1,0:T(8,128)(2,1)S(1)}, bf16[128,1280]{1,0:T(8,128)(2,1)S(1)}, u32[]{:S(2)}, u32[]{:S(2)}) collective-permute-start(bf16[128,1280]{1,0:T(8,128)(2,1)S(1)} %get-tuple-element.94), channel_id=1, source_target_pairs={{0,1},{1,0},{2,3},{3,2},{4,5},{5,4},{6,7},{7,6},{8,9},{9,8},{10,11... | collective-permute-start | bytes 983048 | tf_op jit(solution)/shard_map/ppermute | solution.py:399
  60.4 23.2 %collective-permute-start.44 = (bf16[128,1152]{1,0:T(8,128)(2,1)S(1)}, bf16[128,1152]{1,0:T(8,128)(2,1)S(1)}, u32[]{:S(2)}, u32[]{:S(2)}) collective-permute-start(bf16[128,1152]{1,0:T(8,128)(2,1)S(1)} %get-tuple-element.99), channel_id=1, source_target_pairs={{0,2},{1,3},{2,0},{3,1},{4,6},{5,7},{6,4},{7,5},{8,10},{9,11},{10,... | collective-permute-start | bytes 884744 | tf_op jit(solution)/shard_map/ppermute | solution.py:399
  62.0 22.2 %collective-permute-start.45 = (bf16[128,1152]{1,0:T(8,128)(2,1)S(1)}, bf16[128,1152]{1,0:T(8,128)(2,1)S(1)}, u32[]{:S(2)}, u32[]{:S(2)}) collective-permute-start(bf16[128,1152]{1,0:T(8,128)(2,1)S(1)} %get-tuple-element.100), channel_id=1, source_target_pairs={{0,3},{1,2},{2,1},{3,0},{4,7},{5,6},{6,5},{7,4},{8,11},{9,10},{10,... | collective-permute-start | bytes 884744 | tf_op jit(solution)/shard_map/ppermute | solution.py:399
  71.2 20.9 %collective-permute-start.41 = (bf16[128,1280]{1,0:T(8,128)(2,1)S(1)}, bf16[128,1280]{1,0:T(8,128)(2,1)S(1)}, u32[]{:S(2)}, u32[]{:S(2)}) collective-permute-start(bf16[128,1280]{1,0:T(8,128)(2,1)S(1)} %get-tuple-element.95), channel_id=1, source_target_pairs={{0,2},{1,3},{2,0},{3,1},{4,6},{5,7},{6,4},{7,5},{8,10},{9,11},{10,... | collective-permute-start | bytes 983048 | tf_op jit(solution)/shard_map/ppermute | solution.py:399
  72.7 19.9 %collective-permute-start.42 = (bf16[128,1280]{1,0:T(8,128)(2,1)S(1)}, bf16[128,1280]{1,0:T(8,128)(2,1)S(1)}, u32[]{:S(2)}, u32[]{:S(2)}) collective-permute-start(bf16[128,1280]{1,0:T(8,128)(2,1)S(1)} %get-tuple-element.96), channel_id=1, source_target_pairs={{0,3},{1,2},{2,1},{3,0},{4,7},{5,6},{6,5},{7,4},{8,11},{9,10},{10,... | collective-permute-start | bytes 983048 | tf_op jit(solution)/shard_map/ppermute | solution.py:399
  83.7 26.4 %collective-permute-start.37 = (bf16[128,1408]{1,0:T(8,128)(2,1)S(1)}, bf16[128,1408]{1,0:T(8,128)(2,1)S(1)}, u32[]{:S(2)}, u32[]{:S(2)}) collective-permute-start(bf16[128,1408]{1,0:T(8,128)(2,1)S(1)} %get-tuple-element.90), channel_id=1, source_target_pairs={{0,1},{1,0},{2,3},{3,2},{4,5},{5,4},{6,7},{7,6},{8,9},{9,8},{10,11... | collective-permute-start | bytes 1081352 | tf_op jit(solution)/shard_map/ppermute | solution.py:399
  84.2 25.9 %collective-permute-start.38 = (bf16[128,1408]{1,0:T(8,128)(2,1)S(1)}, bf16[128,1408]{1,0:T(8,128)(2,1)S(1)}, u32[]{:S(2)}, u32[]{:S(2)}) collective-permute-start(bf16[128,1408]{1,0:T(8,128)(2,1)S(1)} %get-tuple-element.91), channel_id=1, source_target_pairs={{0,2},{1,3},{2,0},{3,1},{4,6},{5,7},{6,4},{7,5},{8,10},{9,11},{10,... | collective-permute-start | bytes 1081352 | tf_op jit(solution)/shard_map/ppermute | solution.py:399
  85.7 26.4 %collective-permute-start.39 = (bf16[128,1408]{1,0:T(8,128)(2,1)S(1)}, bf16[128,1408]{1,0:T(8,128)(2,1)S(1)}, u32[]{:S(2)}, u32[]{:S(2)}) collective-permute-start(bf16[128,1408]{1,0:T(8,128)(2,1)S(1)} %get-tuple-element.92), channel_id=1, source_target_pairs={{0,3},{1,2},{2,1},{3,0},{4,7},{5,6},{6,5},{7,4},{8,11},{9,10},{10,... | collective-permute-start | bytes 1081352 | tf_op jit(solution)/shard_map/ppermute | solution.py:399
  92.0 36.1 %collective-permute-start.31 = (bf16[64,1536]{1,0:T(8,128)(2,1)S(1)}, bf16[64,1536]{1,0:T(8,128)(2,1)S(1)}, u32[]{:S(2)}, u32[]{:S(2)}) collective-permute-start(bf16[64,1536]{1,0:T(8,128)(2,1)S(1)} %get-tuple-element.82), channel_id=1, source_target_pairs={{0,1},{1,0},{2,3},{3,2},{4,5},{5,4},{6,7},{7,6},{8,9},{9,8},{10,11... | collective-permute-start | bytes 589832 | tf_op jit(solution)/shard_map/ppermute | solution.py:399
  92.6 15.0 %collective-permute-start.34 = (bf16[64,1536]{1,0:T(8,128)(2,1)S(1)}, bf16[64,1536]{1,0:T(8,128)(2,1)S(1)}, u32[]{:S(2)}, u32[]{:S(2)}) collective-permute-start(bf16[64,1536]{1,0:T(8,128)(2,1)S(1)} %get-tuple-element.86), channel_id=1, source_target_pairs={{0,1},{1,0},{2,3},{3,2},{4,5},{5,4},{6,7},{7,6},{8,9},{9,8},{10,11... | collective-permute-start | bytes 589832 | tf_op jit(solution)/shard_map/ppermute | solution.py:399
  107.6 20.6 %collective-permute-start.32 = (bf16[64,1536]{1,0:T(8,128)(2,1)S(1)}, bf16[64,1536]{1,0:T(8,128)(2,1)S(1)}, u32[]{:S(2)}, u32[]{:S(2)}) collective-permute-start(bf16[64,1536]{1,0:T(8,128)(2,1)S(1)} %get-tuple-element.83), channel_id=1, source_target_pairs={{0,2},{1,3},{2,0},{3,1},{4,6},{5,7},{6,4},{7,5},{8,10},{9,11},{10,... | collective-permute-start | bytes 589832 | tf_op jit(solution)/shard_map/ppermute | solution.py:399
  110.1 18.0 %collective-permute-start.33 = (bf16[64,1536]{1,0:T(8,128)(2,1)S(1)}, bf16[64,1536]{1,0:T(8,128)(2,1)S(1)}, u32[]{:S(2)}, u32[]{:S(2)}) collective-permute-start(bf16[64,1536]{1,0:T(8,128)(2,1)S(1)} %get-tuple-element.84), channel_id=1, source_target_pairs={{0,3},{1,2},{2,1},{3,0},{4,7},{5,6},{6,5},{7,4},{8,11},{9,10},{10,... | collective-permute-start | bytes 589832 | tf_op jit(solution)/shard_map/ppermute | solution.py:399
  110.1 15.2 %collective-permute-start.35 = (bf16[64,1536]{1,0:T(8,128)(2,1)S(1)}, bf16[64,1536]{1,0:T(8,128)(2,1)S(1)}, u32[]{:S(2)}, u32[]{:S(2)}) collective-permute-start(bf16[64,1536]{1,0:T(8,128)(2,1)S(1)} %get-tuple-element.87), channel_id=1, source_target_pairs={{0,2},{1,3},{2,0},{3,1},{4,6},{5,7},{6,4},{7,5},{8,10},{9,11},{10,... | collective-permute-start | bytes 589832 | tf_op jit(solution)/shard_map/ppermute | solution.py:399
  112.1 13.3 %collective-permute-start.36 = (bf16[64,1536]{1,0:T(8,128)(2,1)S(1)}, bf16[64,1536]{1,0:T(8,128)(2,1)S(1)}, u32[]{:S(2)}, u32[]{:S(2)}) collective-permute-start(bf16[64,1536]{1,0:T(8,128)(2,1)S(1)} %get-tuple-element.88), channel_id=1, source_target_pairs={{0,3},{1,2},{2,1},{3,0},{4,7},{5,6},{6,5},{7,4},{8,11},{9,10},{10,... | collective-permute-start | bytes 589832 | tf_op jit(solution)/shard_map/ppermute | solution.py:399
  148.8 38.1 %collective-permute-start.46 = (bf16[128,1536]{1,0:T(8,128)(2,1)S(1)}, bf16[128,1536]{1,0:T(8,128)(2,1)S(1)}, u32[]{:S(2)}, u32[]{:S(2)}) collective-permute-start(bf16[128,1536]{1,0:T(8,128)(2,1)S(1)} %get-tuple-element.102), channel_id=1, source_target_pairs={{0,1},{1,0},{2,3},{3,2},{4,5},{5,4},{6,7},{7,6},{8,9},{9,8},{10,11... | collective-permute-start | bytes 1179656 | tf_op jit(solution)/shard_map/ppermute | solution.py:399
  150.3 36.5 %collective-permute-start.52 = (bf16[128,1280]{1,0:T(8,128)(2,1)S(1)}, bf16[128,1280]{1,0:T(8,128)(2,1)S(1)}, u32[]{:S(2)}, u32[]{:S(2)}) collective-permute-start(bf16[128,1280]{1,0:T(8,128)(2,1)S(1)} %get-tuple-element.111), channel_id=1, source_target_pairs={{0,1},{1,0},{2,3},{3,2},{4,5},{5,4},{6,7},{7,6},{8,9},{9,8},{10,11... | collective-permute-start | bytes 983048 | tf_op jit(solution)/shard_map/ppermute | solution.py:399
  150.8 39.5 %collective-permute-start.47 = (bf16[128,1536]{1,0:T(8,128)(2,1)S(1)}, bf16[128,1536]{1,0:T(8,128)(2,1)S(1)}, u32[]{:S(2)}, u32[]{:S(2)}) collective-permute-start(bf16[128,1536]{1,0:T(8,128)(2,1)S(1)} %get-tuple-element.103), channel_id=1, source_target_pairs={{0,2},{1,3},{2,0},{3,1},{4,6},{5,7},{6,4},{7,5},{8,10},{9,11},{10,... | collective-permute-start | bytes 1179656 | tf_op jit(solution)/shard_map/ppermute | solution.py:399
  156.4 34.0 %collective-permute-start.48 = (bf16[128,1536]{1,0:T(8,128)(2,1)S(1)}, bf16[128,1536]{1,0:T(8,128)(2,1)S(1)}, u32[]{:S(2)}, u32[]{:S(2)}) collective-permute-start(bf16[128,1536]{1,0:T(8,128)(2,1)S(1)} %get-tuple-element.104), channel_id=1, source_target_pairs={{0,3},{1,2},{2,1},{3,0},{4,7},{5,6},{6,5},{7,4},{8,11},{9,10},{10,... | collective-permute-start | bytes 1179656 | tf_op jit(solution)/shard_map/ppermute | solution.py:399
  158.1 28.7 %collective-permute-start.57 = (bf16[128,1152]{1,0:T(8,128)(2,1)S(1)}, bf16[128,1152]{1,0:T(8,128)(2,1)S(1)}, u32[]{:S(2)}, u32[]{:S(2)}) collective-permute-start(bf16[128,1152]{1,0:T(8,128)(2,1)S(1)} %get-tuple-element.117), channel_id=1, source_target_pairs={{0,3},{1,2},{2,1},{3,0},{4,7},{5,6},{6,5},{7,4},{8,11},{9,10},{10,... | collective-permute-start | bytes 884744 | tf_op jit(solution)/shard_map/ppermute | solution.py:399
  186.8 25.9 %collective-permute-start.50 = (bf16[128,1408]{1,0:T(8,128)(2,1)S(1)}, bf16[128,1408]{1,0:T(8,128)(2,1)S(1)}, u32[]{:S(2)}, u32[]{:S(2)}) collective-permute-start(bf16[128,1408]{1,0:T(8,128)(2,1)S(1)} %get-tuple-element.108), channel_id=1, source_target_pairs={{0,2},{1,3},{2,0},{3,1},{4,6},{5,7},{6,4},{7,5},{8,10},{9,11},{10,... | collective-permute-start | bytes 1081352 | tf_op jit(solution)/shard_map/ppermute | solution.py:399
  186.9 25.8 %collective-permute-start.51 = (bf16[128,1408]{1,0:T(8,128)(2,1)S(1)}, bf16[128,1408]{1,0:T(8,128)(2,1)S(1)}, u32[]{:S(2)}, u32[]{:S(2)}) collective-permute-start(bf16[128,1408]{1,0:T(8,128)(2,1)S(1)} %get-tuple-element.109), channel_id=1, source_target_pairs={{0,3},{1,2},{2,1},{3,0},{4,7},{5,6},{6,5},{7,4},{8,11},{9,10},{10,... | collective-permute-start | bytes 1081352 | tf_op jit(solution)/shard_map/ppermute | solution.py:399
  190.3 26.0 %collective-permute-start.53 = (bf16[128,1280]{1,0:T(8,128)(2,1)S(1)}, bf16[128,1280]{1,0:T(8,128)(2,1)S(1)}, u32[]{:S(2)}, u32[]{:S(2)}) collective-permute-start(bf16[128,1280]{1,0:T(8,128)(2,1)S(1)} %get-tuple-element.112), channel_id=1, source_target_pairs={{0,2},{1,3},{2,0},{3,1},{4,6},{5,7},{6,4},{7,5},{8,10},{9,11},{10,... | collective-permute-start | bytes 983048 | tf_op jit(solution)/shard_map/ppermute | solution.py:399
  190.4 26.0 %collective-permute-start.54 = (bf16[128,1280]{1,0:T(8,128)(2,1)S(1)}, bf16[128,1280]{1,0:T(8,128)(2,1)S(1)}, u32[]{:S(2)}, u32[]{:S(2)}) collective-permute-start(bf16[128,1280]{1,0:T(8,128)(2,1)S(1)} %get-tuple-element.113), channel_id=1, source_target_pairs={{0,3},{1,2},{2,1},{3,0},{4,7},{5,6},{6,5},{7,4},{8,11},{9,10},{10,... | collective-permute-start | bytes 983048 | tf_op jit(solution)/shard_map/ppermute | solution.py:399
  198.1 21.6 %collective-permute-start.79 = (bf16[128,256]{1,0:T(8,128)(2,1)S(1)}, bf16[128,256]{1,0:T(8,128)(2,1)S(1)}, u32[]{:S(2)}, u32[]{:S(2)}) collective-permute-start(bf16[128,256]{1,0:T(8,128)(2,1)S(1)} %get-tuple-element.146), channel_id=1, source_target_pairs={{0,4},{4,0},{8,12},{12,8},{16,20},{20,16},{24,28},{28,24},{1,5},{5... | collective-permute-start | bytes 196616 | tf_op jit(solution)/shard_map/ppermute | solution.py:408
  216.4 12.2 %collective-permute-start.83 = (bf16[128,256]{1,0:T(8,128)(2,1)S(1)}, bf16[128,256]{1,0:T(8,128)(2,1)S(1)}, u32[]{:S(2)}, u32[]{:S(2)}) collective-permute-start(bf16[128,256]{1,0:T(8,128)(2,1)S(1)} %get-tuple-element.150), channel_id=1, source_target_pairs={{0,20},{4,16},{8,28},{12,24},{16,4},{20,0},{24,12},{28,8},{1,21},{... | collective-permute-start | bytes 196616 | tf_op jit(solution)/shard_map/ppermute | solution.py:408
  251.2 15.4 %collective-permute-start.60 = (bf16[128,256]{1,0:T(8,128)(2,1)S(1)}, bf16[128,256]{1,0:T(8,128)(2,1)S(1)}, u32[]{:S(2)}, u32[]{:S(2)}) collective-permute-start(bf16[128,256]{1,0:T(8,128)(2,1)S(1)} %get-tuple-element.124), channel_id=1, source_target_pairs={{0,12},{4,8},{8,4},{12,0},{16,28},{20,24},{24,20},{28,16},{1,13},{... | collective-permute-start | bytes 196616 | tf_op jit(solution)/shard_map/ppermute | solution.py:408
  (62 other events, 576.0 us)

commit v3 on v2

--- a/solution.py
+++ b/solution.py
@@ -119,19 +119,32 @@
     return out[0], [out[1 + h * n_pts : 1 + (h + 1) * n_pts] for h in range(pieces)]
 
 
-def transpose_kernel(given, out):
-    out[...] = given[...].T
+def transpose_kernel(tile, given, out, held, sem):
+    pieces = given.shape[0] // tile
+
+    def copy(i):
+        at = pl.ds(pl.multiple_of(i * tile, tile), tile)
+        return pltpu.make_async_copy(given.at[at], held.at[at], sem.at[i])
+
+    for i in range(pieces):
+        copy(i).start()
+
+    @pl.loop(0, pieces)
+    def _(i):
+        copy(i).wait()
+        at = pl.ds(pl.multiple_of(i * tile, tile), tile)
+        out[:, at] = held[at, :].T
 
 
 def transposed(basis):
     points, orbitals = basis.shape
-    tile = 256
+    tile = 2 * BLOCK
     return pl.pallas_call(
-        transpose_kernel,
+        functools.partial(transpose_kernel, tile),
         out_shape=jax.ShapeDtypeStruct((orbitals, points), basis.dtype),
-        grid=(points // tile,),
-        in_specs=[pl.BlockSpec((tile, orbitals), lambda i: (i, 0))],
-        out_specs=pl.BlockSpec((orbitals, tile), lambda i: (0, i)),
+        in_specs=[pl.BlockSpec(memory_space=pltpu.HBM)],
+        out_specs=VM,
+        scratch_shapes=[pltpu.VMEM((points, orbitals), basis.dtype), pltpu.SemaphoreType.DMA((points // tile,))],
         compiler_params=GRANT,
         cost_estimate=cost(0, 4 * points * orbitals),
         name="flip",
@@ -421,7 +434,7 @@
     head = jnp.stack([me_mat, me_pts, point_count[0, 0]]).astype(jnp.int32)
     meta = jnp.concatenate([head] + peers + [pattern])
 
-    flipped = transposed(basis)
+    flipped = transposed(pltpu.with_memory_space_constraint(basis, pltpu.HBM))
 
     parts, stages = [], []
     for k in range(row_blocks):

time: 271 us -> 271 us (level)
  no operation moved by 1% of the time
where the time goes in v3:
time: 271 us; the launch traced here: 270 us
  waiting for transfers between devices  122 us (45%)
  starting transfers between devices  86.9 us (32%)
  Pallas kernels  57.8 us (21%)
    ppermute x30, waiting for transfers between devices, to_peer(): return lax.ppermute(value, 'pts', [(i, i ^ o) for i in range(n_pts)])  76.7 us
    ppermute x56, starting transfers between devices, across(): out[d] = lax.ppermute(values[d], 'mat', [(i, i ^ d) for i in range(n_mat)])  53.2 us
    ppermute x56, waiting for transfers between devices, across(): out[d] = lax.ppermute(values[d], 'mat', [(i, i ^ d) for i in range(n_mat)])  44.9 us
    ppermute x30, starting transfers between devices, to_peer(): return lax.ppermute(value, 'pts', [(i, i ^ o) for i in range(n_pts)])  33.7 us
    pallas_call x4, Pallas kernels, density(): pl.pallas_call(functools.partial(density_kernel, dims, k, h, tile_of(poin...  15 us
    pallas_call x1, Pallas kernels, response(): pl.pallas_call(functools.partial(response_kernel, dims, ranks, tile_of(or...  11.3 us
    pallas_call x4, Pallas kernels, combine(): pl.pallas_call(functools.partial(combine_kernel, dims, k), out_shape=shap...  8.34 us
    pallas_call x4, Pallas kernels, pack(): pl.pallas_call(functools.partial(pack_kernel, dims, k, pieces), out_shape...  7.14 us
  transfers between devices with their start and end apart: 86, of which 34 were waited for; matrix products, arithmetic and copies ran while one was open for 0% of the time, Pallas kernels for 14%

profile of v3, /device:TPU:0, one launch (start us, length us, event | category | flops | bytes accessed | tf_op | source)
XLA Modules:
  0.0 270.0 jit_solution(8866432824899995755)
XLA Ops:
  2.5 4.6 %collective-permute-start.30 = (bf16[128,256]{1,0:T(8,128)(2,1)S(1)}, bf16[128,256]{1,0:T(8,128)(2,1)S(1)}, u32[]{:S(2)}, u32[]{:S(2)}) collective-permute-start(bf16[128,256]{1,0:T(8,128)(2,1)S(1)} %get-tuple-element.154), channel_id=1, source_target_pairs={{0,28},{4,24},{8,20},{12,16},{16,12},{20,8},{24,4},{28,0},{1,29},{... | collective-permute-start | bytes 196616 | tf_op jit(solution)/shard_map/ppermute | solution.py:421
  7.1 2.4 collective-permute-start.2
  15.0 2.8 %collective-permute-done.28.refs_5_ = bf16[128,256]{1,0:T(8,128)(2,1)S(1)} collective-permute-done((bf16[128,256]{1,0:T(8,128)(2,1)S(1)}, bf16[128,256]{1,0:T(8,128)(2,1)S(1)}, u32[]{:S(2)}, u32[]{:S(2)}) %collective-permute-start.28) | collective-permute-done | bytes 65568 | tf_op jit(solution)/shard_map/ppermute | solution.py:421
  22.5 2.5 collective-permute-start.15
  27.8 5.9 %collective-permute-done.21.refs_5_ = bf16[128,256]{1,0:T(8,128)(2,1)S(1)} collective-permute-done((bf16[128,256]{1,0:T(8,128)(2,1)S(1)}, bf16[128,256]{1,0:T(8,128)(2,1)S(1)}, u32[]{:S(2)}, u32[]{:S(2)}) %collective-permute-start.21) | collective-permute-done | bytes 65568 | tf_op jit(solution)/shard_map/ppermute | solution.py:421
  42.4 3.5 %collective-permute-start.9 = (bf16[128,256]{1,0:T(8,128)(2,1)S(1)}, bf16[128,256]{1,0:T(8,128)(2,1)S(1)}, u32[]{:S(2)}, u32[]{:S(2)}) collective-permute-start(bf16[128,256]{1,0:T(8,128)(2,1)S(1)} %get-tuple-element.177), channel_id=1, source_target_pairs={{0,28},{4,24},{8,20},{12,16},{16,12},{20,8},{24,4},{28,0},{1,29},{... | collective-permute-start | bytes 196616 | tf_op jit(solution)/shard_map/ppermute | solution.py:421
  56.8 2.8 %collective-permute-done.7.refs_5_ = bf16[128,256]{1,0:T(8,128)(2,1)S(1)} collective-permute-done((bf16[128,256]{1,0:T(8,128)(2,1)S(1)}, bf16[128,256]{1,0:T(8,128)(2,1)S(1)}, u32[]{:S(2)}, u32[]{:S(2)}) %collective-permute-start.7) | collective-permute-done | bytes 65568 | tf_op jit(solution)/shard_map/ppermute | solution.py:421
  65.9 5.3 %collective-permute-done.29.refs_6_ = bf16[128,256]{1,0:T(8,128)(2,1)S(1)} collective-permute-done((bf16[128,256]{1,0:T(8,128)(2,1)S(1)}, bf16[128,256]{1,0:T(8,128)(2,1)S(1)}, u32[]{:S(2)}, u32[]{:S(2)}) %collective-permute-start.29) | collective-permute-done | bytes 65568 | tf_op jit(solution)/shard_map/ppermute | solution.py:421
  73.2 2.7 %flip.1.refs_4_.refs_0_ = bf16[1536,1536]{1,0:T(8,128)(2,1)S(1)} custom-call(bf16[1536,1536]{1,0:T(8,128)(2,1)} %bitcast.70), custom_call_target="tpu_custom_call" | custom-call | bytes 9437184 | tf_op jit(solution)/shard_map/flip/pallas_call | solution.py:142
  77.5 2.5 shard_map.98
  80.0 3.6 %collective-permute-done.44.refs_2_ = bf16[128,1152]{1,0:T(8,128)(2,1)S(1)} collective-permute-done((bf16[128,1152]{1,0:T(8,128)(2,1)S(1)}, bf16[128,1152]{1,0:T(8,128)(2,1)S(1)}, u32[]{:S(2)}, u32[]{:S(2)}) %collective-permute-start.44) | collective-permute-done | bytes 294944 | tf_op jit(solution)/shard_map/ppermute | solution.py:412
  87.2 4.2 %shard_map.99.refs_5_ = f32[1,1536]{1,0:T(1,128)S(1)} custom-call(s32[307]{0:T(512)S(1)} %concatenate.3.meta, bf16[128,1152]{1,0:T(8,128)(2,1)S(1)} %get-tuple-element.97.refs_0_, bf16[128,1152]{1,0:T(8,128)(2,1)S(1)} %collective-permute-done.43.refs_1_, bf16[128,1152]{1,0:T(8,128)(2,1)S(1)} %collective-permute-done.44.refs_2_, ...), custom_call_target="tpu_custom_call" | custom-call | flops 2415919104 | bytes 4718592 | tf_op jit(solution)/shard_map/pallas_call | solution.py:205
  94.1 4.0 %shard_map.100.refs_5_ = f32[1,1536]{1,0:T(1,128)S(1)} custom-call(s32[307]{0:T(512)S(1)} %concatenate.3.meta, bf16[128,1280]{1,0:T(8,128)(2,1)S(1)} %get-tuple-element.93.refs_0_, bf16[128,1280]{1,0:T(8,128)(2,1)S(1)} %collective-permute-done.40.refs_1_, bf16[128,1280]{1,0:T(8,128)(2,1)S(1)} %collective-permute-done.41.refs_2_, ...), custom_call_target="tpu_custom_call" | custom-call | flops 2415919104 | bytes 4718592 | tf_op jit(solution)/shard_map/pallas_call | solution.py:205
  98.1 9.5 %collective-permute-done.34.refs_1_ = bf16[64,1536]{1,0:T(8,128)(2,1)S(1)} collective-permute-done((bf16[64,1536]{1,0:T(8,128)(2,1)S(1)}, bf16[64,1536]{1,0:T(8,128)(2,1)S(1)}, u32[]{:S(2)}, u32[]{:S(2)}) %collective-permute-start.34) | collective-permute-done | bytes 196640 | tf_op jit(solution)/shard_map/ppermute | solution.py:412
  107.6 2.5 collective-permute-start.32
  113.1 4.0 %shard_map.101.refs_5_ = f32[1,1536]{1,0:T(1,128)S(1)} custom-call(s32[307]{0:T(512)S(1)} %concatenate.3.meta, bf16[128,1408]{1,0:T(8,128)(2,1)S(1)} %get-tuple-element.89.refs_0_, bf16[128,1408]{1,0:T(8,128)(2,1)S(1)} %collective-permute-done.37.refs_1_, bf16[128,1408]{1,0:T(8,128)(2,1)S(1)} %collective-permute-done.38.refs_2_, ...), custom_call_target="tpu_custom_call" | custom-call | flops 2415919104 | bytes 4718592 | tf_op jit(solution)/shard_map/pallas_call | solution.py:205
  117.2 8.2 %collective-permute-done.35.refs_2_ = bf16[64,1536]{1,0:T(8,128)(2,1)S(1)} collective-permute-done((bf16[64,1536]{1,0:T(8,128)(2,1)S(1)}, bf16[64,1536]{1,0:T(8,128)(2,1)S(1)}, u32[]{:S(2)}, u32[]{:S(2)}) %collective-permute-start.35) | collective-permute-done | bytes 196640 | tf_op jit(solution)/shard_map/ppermute | solution.py:412
  125.4 2.8 %shard_map.102.refs_5_ = f32[1,1536]{1,0:T(1,128)S(1)} custom-call(s32[307]{0:T(512)S(1)} %concatenate.3.meta, bf16[64,1536]{1,0:T(8,128)(2,1)S(1)} %get-tuple-element.85.refs_0_, bf16[64,1536]{1,0:T(8,128)(2,1)S(1)} %collective-permute-done.34.refs_1_, bf16[64,1536]{1,0:T(8,128)(2,1)S(1)} %collective-permute-done.35.refs_2_, ...), custom_call_target="tpu_custom_call" | custom-call | flops 1207959552 | bytes 4718592 | tf_op jit(solution)/shard_map/pallas_call | solution.py:205
  128.2 7.0 %turn.1 = (bf16[128,1536]{1,0:T(8,128)(2,1)S(1)}, bf16[128,1536]{1,0:T(8,128)(2,1)S(1)}, bf16[128,1536]{1,0:T(8,128)(2,1)S(1)}, bf16[128,1536]{1,0:T(8,128)(2,1)...) custom-call(s32[307]{0:T(512)S(1)} %concatenate.3.meta, bf16[64,1536]{1,0:T(8,128)(2,1)S(1)} %get-tuple-element.81.refs_0_, ...), custom_call_target="tpu_custom_call" | custom-call | flops 3623878656 | bytes 9437184 | tf_op jit(solution)/shard_map/turn/pallas_call | solution.py:235
  135.2 11.3 %shard_map.103 = (bf16[128,1408]{1,0:T(8,128)(2,1)S(1)}, bf16[128,1408]{1,0:T(8,128)(2,1)S(1)}, bf16[128,1408]{1,0:T(8,128)(2,1)S(1)}, bf16[128,1408]{1,0:T(8,12...) custom-call(s32[307]{0:T(512)S(1)} %concatenate.3.meta, ...), custom_call_target="tpu_custom_call" | custom-call | flops 7247757312 | bytes 9437184 | tf_op jit(solution)/shard_map/pallas_call | solution.py:290
  151.4 5.0 %collective-permute-done.55.refs_13_ = bf16[128,1152]{1,0:T(8,128)(2,1)S(1)} collective-permute-done((bf16[128,1152]{1,0:T(8,128)(2,1)S(1)}, bf16[128,1152]{1,0:T(8,128)(2,1)S(1)}, u32[]{:S(2)}, u32[]{:S(2)}) %collective-permute-start.55) | collective-permute-done | bytes 294944 | tf_op jit(solution)/shard_map/ppermute | solution.py:412
  159.6 27.2 %collective-permute-done.57.refs_15_ = bf16[128,1152]{1,0:T(8,128)(2,1)S(1)} collective-permute-done((bf16[128,1152]{1,0:T(8,128)(2,1)S(1)}, bf16[128,1152]{1,0:T(8,128)(2,1)S(1)}, u32[]{:S(2)}, u32[]{:S(2)}) %collective-permute-start.57) | collective-permute-done | bytes 294944 | tf_op jit(solution)/shard_map/ppermute | solution.py:412
  186.9 3.4 %collective-permute-start.51 = (bf16[128,1408]{1,0:T(8,128)(2,1)S(1)}, bf16[128,1408]{1,0:T(8,128)(2,1)S(1)}, u32[]{:S(2)}, u32[]{:S(2)}) collective-permute-start(bf16[128,1408]{1,0:T(8,128)(2,1)S(1)} %get-tuple-element.109), channel_id=1, source_target_pairs={{0,3},{1,2},{2,1},{3,0},{4,7},{5,6},{6,5},{7,4},{8,11},{9,10},{10,... | collective-permute-start | bytes 1081352 | tf_op jit(solution)/shard_map/ppermute | solution.py:412
  193.5 4.6 %collective-permute-done.49.refs_5_ = bf16[128,1408]{1,0:T(8,128)(2,1)S(1)} collective-permute-done((bf16[128,1408]{1,0:T(8,128)(2,1)S(1)}, bf16[128,1408]{1,0:T(8,128)(2,1)S(1)}, u32[]{:S(2)}, u32[]{:S(2)}) %collective-permute-start.49) | collective-permute-done | bytes 360480 | tf_op jit(solution)/shard_map/ppermute | solution.py:412
  198.1 14.7 %collective-permute-done.50.refs_6_ = bf16[128,1408]{1,0:T(8,128)(2,1)S(1)} collective-permute-done((bf16[128,1408]{1,0:T(8,128)(2,1)S(1)}, bf16[128,1408]{1,0:T(8,128)(2,1)S(1)}, u32[]{:S(2)}, u32[]{:S(2)}) %collective-permute-start.50) | collective-permute-done | bytes 360480 | tf_op jit(solution)/shard_map/ppermute | solution.py:412
  216.4 3.4 %collective-permute-start.83 = (bf16[128,256]{1,0:T(8,128)(2,1)S(1)}, bf16[128,256]{1,0:T(8,128)(2,1)S(1)}, u32[]{:S(2)}, u32[]{:S(2)}) collective-permute-start(bf16[128,256]{1,0:T(8,128)(2,1)S(1)} %get-tuple-element.150), channel_id=1, source_target_pairs={{0,20},{4,16},{8,28},{12,24},{16,4},{20,0},{24,12},{28,8},{1,21},{... | collective-permute-start | bytes 196616 | tf_op jit(solution)/shard_map/ppermute | solution.py:421
  219.8 2.6 collective-permute-start.85
  223.7 3.4 %collective-permute-done.82.refs_4_ = bf16[128,256]{1,0:T(8,128)(2,1)S(1)} collective-permute-done((bf16[128,256]{1,0:T(8,128)(2,1)S(1)}, bf16[128,256]{1,0:T(8,128)(2,1)S(1)}, u32[]{:S(2)}, u32[]{:S(2)}) %collective-permute-start.82) | collective-permute-done | bytes 65568 | tf_op jit(solution)/shard_map/ppermute | solution.py:421
  231.5 2.5 collective-permute-start.77
  236.1 2.5 shard_map.107
  242.0 3.0 %collective-permute-done.78.refs_7_ = bf16[128,256]{1,0:T(8,128)(2,1)S(1)} collective-permute-done((bf16[128,256]{1,0:T(8,128)(2,1)S(1)}, bf16[128,256]{1,0:T(8,128)(2,1)S(1)}, u32[]{:S(2)}, u32[]{:S(2)}) %collective-permute-start.78) | collective-permute-done | bytes 65568 | tf_op jit(solution)/shard_map/ppermute | solution.py:421
  251.2 4.4 %collective-permute-done.68.refs_4_ = bf16[128,256]{1,0:T(8,128)(2,1)S(1)} collective-permute-done((bf16[128,256]{1,0:T(8,128)(2,1)S(1)}, bf16[128,256]{1,0:T(8,128)(2,1)S(1)}, u32[]{:S(2)}, u32[]{:S(2)}) %collective-permute-start.68) | collective-permute-done | bytes 65568 | tf_op jit(solution)/shard_map/ppermute | solution.py:421
  (179 shorter events, 99.7 us)
Async XLA Ops:
  2.5 12.5 %collective-permute-start.30 = (bf16[128,256]{1,0:T(8,128)(2,1)S(1)}, bf16[128,256]{1,0:T(8,128)(2,1)S(1)}, u32[]{:S(2)}, u32[]{:S(2)}) collective-permute-start(bf16[128,256]{1,0:T(8,128)(2,1)S(1)} %get-tuple-element.154), channel_id=1, source_target_pairs={{0,28},{4,24},{8,20},{12,16},{16,12},{20,8},{24,4},{28,0},{1,29},{... | collective-permute-start | bytes 196616 | tf_op jit(solution)/shard_map/ppermute | solution.py:421
  21.3 12.5 %collective-permute-start.21 = (bf16[128,256]{1,0:T(8,128)(2,1)S(1)}, bf16[128,256]{1,0:T(8,128)(2,1)S(1)}, u32[]{:S(2)}, u32[]{:S(2)}) collective-permute-start(bf16[128,256]{1,0:T(8,128)(2,1)S(1)} %get-tuple-element.163), channel_id=1, source_target_pairs={{0,20},{4,16},{8,28},{12,24},{16,4},{20,0},{24,12},{28,8},{1,21},{... | collective-permute-start | bytes 196616 | tf_op jit(solution)/shard_map/ppermute | solution.py:421
  22.5 13.3 %collective-permute-start.15 = (bf16[128,256]{1,0:T(8,128)(2,1)S(1)}, bf16[128,256]{1,0:T(8,128)(2,1)S(1)}, u32[]{:S(2)}, u32[]{:S(2)}) collective-permute-start(bf16[128,256]{1,0:T(8,128)(2,1)S(1)} %get-tuple-element.170), channel_id=1, source_target_pairs={{0,24},{4,28},{8,16},{12,20},{16,8},{20,12},{24,0},{28,4},{1,25},{... | collective-permute-start | bytes 196616 | tf_op jit(solution)/shard_map/ppermute | solution.py:421
  24.9 13.1 %collective-permute-start.14 = (bf16[128,256]{1,0:T(8,128)(2,1)S(1)}, bf16[128,256]{1,0:T(8,128)(2,1)S(1)}, u32[]{:S(2)}, u32[]{:S(2)}) collective-permute-start(bf16[128,256]{1,0:T(8,128)(2,1)S(1)} %get-tuple-element.171), channel_id=1, source_target_pairs={{0,20},{4,16},{8,28},{12,24},{16,4},{20,0},{24,12},{28,8},{1,21},{... | collective-permute-start | bytes 196616 | tf_op jit(solution)/shard_map/ppermute | solution.py:421
  26.0 13.5 %collective-permute-start.13 = (bf16[128,256]{1,0:T(8,128)(2,1)S(1)}, bf16[128,256]{1,0:T(8,128)(2,1)S(1)}, u32[]{:S(2)}, u32[]{:S(2)}) collective-permute-start(bf16[128,256]{1,0:T(8,128)(2,1)S(1)} %get-tuple-element.172), channel_id=1, source_target_pairs={{0,16},{4,20},{8,24},{12,28},{16,0},{20,4},{24,8},{28,12},{1,17},{... | collective-permute-start | bytes 196616 | tf_op jit(solution)/shard_map/ppermute | solution.py:421
  48.2 24.5 %collective-permute-start.43 = (bf16[128,1152]{1,0:T(8,128)(2,1)S(1)}, bf16[128,1152]{1,0:T(8,128)(2,1)S(1)}, u32[]{:S(2)}, u32[]{:S(2)}) collective-permute-start(bf16[128,1152]{1,0:T(8,128)(2,1)S(1)} %get-tuple-element.98), channel_id=1, source_target_pairs={{0,1},{1,0},{2,3},{3,2},{4,5},{5,4},{6,7},{7,6},{8,9},{9,8},{10,11... | collective-permute-start | bytes 884744 | tf_op jit(solution)/shard_map/ppermute | solution.py:412
  56.2 29.5 %collective-permute-start.40 = (bf16[128,1280]{1,0:T(8,128)(2,1)S(1)}, bf16[128,1280]{1,0:T(8,128)(2,1)S(1)}, u32[]{:S(2)}, u32[]{:S(2)}) collective-permute-start(bf16[128,1280]{1,0:T(8,128)(2,1)S(1)} %get-tuple-element.94), channel_id=1, source_target_pairs={{0,1},{1,0},{2,3},{3,2},{4,5},{5,4},{6,7},{7,6},{8,9},{9,8},{10,11... | collective-permute-start | bytes 983048 | tf_op jit(solution)/shard_map/ppermute | solution.py:412
  60.4 23.2 %collective-permute-start.44 = (bf16[128,1152]{1,0:T(8,128)(2,1)S(1)}, bf16[128,1152]{1,0:T(8,128)(2,1)S(1)}, u32[]{:S(2)}, u32[]{:S(2)}) collective-permute-start(bf16[128,1152]{1,0:T(8,128)(2,1)S(1)} %get-tuple-element.99), channel_id=1, source_target_pairs={{0,2},{1,3},{2,0},{3,1},{4,6},{5,7},{6,4},{7,5},{8,10},{9,11},{10,... | collective-permute-start | bytes 884744 | tf_op jit(solution)/shard_map/ppermute | solution.py:412
  62.0 22.2 %collective-permute-start.45 = (bf16[128,1152]{1,0:T(8,128)(2,1)S(1)}, bf16[128,1152]{1,0:T(8,128)(2,1)S(1)}, u32[]{:S(2)}, u32[]{:S(2)}) collective-permute-start(bf16[128,1152]{1,0:T(8,128)(2,1)S(1)} %get-tuple-element.100), channel_id=1, source_target_pairs={{0,3},{1,2},{2,1},{3,0},{4,7},{5,6},{6,5},{7,4},{8,11},{9,10},{10,... | collective-permute-start | bytes 884744 | tf_op jit(solution)/shard_map/ppermute | solution.py:412
  71.2 20.9 %collective-permute-start.41 = (bf16[128,1280]{1,0:T(8,128)(2,1)S(1)}, bf16[128,1280]{1,0:T(8,128)(2,1)S(1)}, u32[]{:S(2)}, u32[]{:S(2)}) collective-permute-start(bf16[128,1280]{1,0:T(8,128)(2,1)S(1)} %get-tuple-element.95), channel_id=1, source_target_pairs={{0,2},{1,3},{2,0},{3,1},{4,6},{5,7},{6,4},{7,5},{8,10},{9,11},{10,... | collective-permute-start | bytes 983048 | tf_op jit(solution)/shard_map/ppermute | solution.py:412
  72.7 19.9 %collective-permute-start.42 = (bf16[128,1280]{1,0:T(8,128)(2,1)S(1)}, bf16[128,1280]{1,0:T(8,128)(2,1)S(1)}, u32[]{:S(2)}, u32[]{:S(2)}) collective-permute-start(bf16[128,1280]{1,0:T(8,128)(2,1)S(1)} %get-tuple-element.96), channel_id=1, source_target_pairs={{0,3},{1,2},{2,1},{3,0},{4,7},{5,6},{6,5},{7,4},{8,11},{9,10},{10,... | collective-permute-start | bytes 983048 | tf_op jit(solution)/shard_map/ppermute | solution.py:412
  83.7 26.4 %collective-permute-start.37 = (bf16[128,1408]{1,0:T(8,128)(2,1)S(1)}, bf16[128,1408]{1,0:T(8,128)(2,1)S(1)}, u32[]{:S(2)}, u32[]{:S(2)}) collective-permute-start(bf16[128,1408]{1,0:T(8,128)(2,1)S(1)} %get-tuple-element.90), channel_id=1, source_target_pairs={{0,1},{1,0},{2,3},{3,2},{4,5},{5,4},{6,7},{7,6},{8,9},{9,8},{10,11... | collective-permute-start | bytes 1081352 | tf_op jit(solution)/shard_map/ppermute | solution.py:412
  84.2 25.9 %collective-permute-start.38 = (bf16[128,1408]{1,0:T(8,128)(2,1)S(1)}, bf16[128,1408]{1,0:T(8,128)(2,1)S(1)}, u32[]{:S(2)}, u32[]{:S(2)}) collective-permute-start(bf16[128,1408]{1,0:T(8,128)(2,1)S(1)} %get-tuple-element.91), channel_id=1, source_target_pairs={{0,2},{1,3},{2,0},{3,1},{4,6},{5,7},{6,4},{7,5},{8,10},{9,11},{10,... | collective-permute-start | bytes 1081352 | tf_op jit(solution)/shard_map/ppermute | solution.py:412
  85.7 26.4 %collective-permute-start.39 = (bf16[128,1408]{1,0:T(8,128)(2,1)S(1)}, bf16[128,1408]{1,0:T(8,128)(2,1)S(1)}, u32[]{:S(2)}, u32[]{:S(2)}) collective-permute-start(bf16[128,1408]{1,0:T(8,128)(2,1)S(1)} %get-tuple-element.92), channel_id=1, source_target_pairs={{0,3},{1,2},{2,1},{3,0},{4,7},{5,6},{6,5},{7,4},{8,11},{9,10},{10,... | collective-permute-start | bytes 1081352 | tf_op jit(solution)/shard_map/ppermute | solution.py:412
  92.0 36.1 %collective-permute-start.31 = (bf16[64,1536]{1,0:T(8,128)(2,1)S(1)}, bf16[64,1536]{1,0:T(8,128)(2,1)S(1)}, u32[]{:S(2)}, u32[]{:S(2)}) collective-permute-start(bf16[64,1536]{1,0:T(8,128)(2,1)S(1)} %get-tuple-element.82), channel_id=1, source_target_pairs={{0,1},{1,0},{2,3},{3,2},{4,5},{5,4},{6,7},{7,6},{8,9},{9,8},{10,11... | collective-permute-start | bytes 589832 | tf_op jit(solution)/shard_map/ppermute | solution.py:412
  92.6 15.0 %collective-permute-start.34 = (bf16[64,1536]{1,0:T(8,128)(2,1)S(1)}, bf16[64,1536]{1,0:T(8,128)(2,1)S(1)}, u32[]{:S(2)}, u32[]{:S(2)}) collective-permute-start(bf16[64,1536]{1,0:T(8,128)(2,1)S(1)} %get-tuple-element.86), channel_id=1, source_target_pairs={{0,1},{1,0},{2,3},{3,2},{4,5},{5,4},{6,7},{7,6},{8,9},{9,8},{10,11... | collective-permute-start | bytes 589832 | tf_op jit(solution)/shard_map/ppermute | solution.py:412
  107.6 20.6 %collective-permute-start.32 = (bf16[64,1536]{1,0:T(8,128)(2,1)S(1)}, bf16[64,1536]{1,0:T(8,128)(2,1)S(1)}, u32[]{:S(2)}, u32[]{:S(2)}) collective-permute-start(bf16[64,1536]{1,0:T(8,128)(2,1)S(1)} %get-tuple-element.83), channel_id=1, source_target_pairs={{0,2},{1,3},{2,0},{3,1},{4,6},{5,7},{6,4},{7,5},{8,10},{9,11},{10,... | collective-permute-start | bytes 589832 | tf_op jit(solution)/shard_map/ppermute | solution.py:412
  110.1 18.0 %collective-permute-start.33 = (bf16[64,1536]{1,0:T(8,128)(2,1)S(1)}, bf16[64,1536]{1,0:T(8,128)(2,1)S(1)}, u32[]{:S(2)}, u32[]{:S(2)}) collective-permute-start(bf16[64,1536]{1,0:T(8,128)(2,1)S(1)} %get-tuple-element.84), channel_id=1, source_target_pairs={{0,3},{1,2},{2,1},{3,0},{4,7},{5,6},{6,5},{7,4},{8,11},{9,10},{10,... | collective-permute-start | bytes 589832 | tf_op jit(solution)/shard_map/ppermute | solution.py:412
  110.1 15.2 %collective-permute-start.35 = (bf16[64,1536]{1,0:T(8,128)(2,1)S(1)}, bf16[64,1536]{1,0:T(8,128)(2,1)S(1)}, u32[]{:S(2)}, u32[]{:S(2)}) collective-permute-start(bf16[64,1536]{1,0:T(8,128)(2,1)S(1)} %get-tuple-element.87), channel_id=1, source_target_pairs={{0,2},{1,3},{2,0},{3,1},{4,6},{5,7},{6,4},{7,5},{8,10},{9,11},{10,... | collective-permute-start | bytes 589832 | tf_op jit(solution)/shard_map/ppermute | solution.py:412
  112.1 13.3 %collective-permute-start.36 = (bf16[64,1536]{1,0:T(8,128)(2,1)S(1)}, bf16[64,1536]{1,0:T(8,128)(2,1)S(1)}, u32[]{:S(2)}, u32[]{:S(2)}) collective-permute-start(bf16[64,1536]{1,0:T(8,128)(2,1)S(1)} %get-tuple-element.88), channel_id=1, source_target_pairs={{0,3},{1,2},{2,1},{3,0},{4,7},{5,6},{6,5},{7,4},{8,11},{9,10},{10,... | collective-permute-start | bytes 589832 | tf_op jit(solution)/shard_map/ppermute | solution.py:412
  148.8 38.1 %collective-permute-start.46 = (bf16[128,1536]{1,0:T(8,128)(2,1)S(1)}, bf16[128,1536]{1,0:T(8,128)(2,1)S(1)}, u32[]{:S(2)}, u32[]{:S(2)}) collective-permute-start(bf16[128,1536]{1,0:T(8,128)(2,1)S(1)} %get-tuple-element.102), channel_id=1, source_target_pairs={{0,1},{1,0},{2,3},{3,2},{4,5},{5,4},{6,7},{7,6},{8,9},{9,8},{10,11... | collective-permute-start | bytes 1179656 | tf_op jit(solution)/shard_map/ppermute | solution.py:412
  150.3 36.5 %collective-permute-start.52 = (bf16[128,1280]{1,0:T(8,128)(2,1)S(1)}, bf16[128,1280]{1,0:T(8,128)(2,1)S(1)}, u32[]{:S(2)}, u32[]{:S(2)}) collective-permute-start(bf16[128,1280]{1,0:T(8,128)(2,1)S(1)} %get-tuple-element.111), channel_id=1, source_target_pairs={{0,1},{1,0},{2,3},{3,2},{4,5},{5,4},{6,7},{7,6},{8,9},{9,8},{10,11... | collective-permute-start | bytes 983048 | tf_op jit(solution)/shard_map/ppermute | solution.py:412
  150.8 39.5 %collective-permute-start.47 = (bf16[128,1536]{1,0:T(8,128)(2,1)S(1)}, bf16[128,1536]{1,0:T(8,128)(2,1)S(1)}, u32[]{:S(2)}, u32[]{:S(2)}) collective-permute-start(bf16[128,1536]{1,0:T(8,128)(2,1)S(1)} %get-tuple-element.103), channel_id=1, source_target_pairs={{0,2},{1,3},{2,0},{3,1},{4,6},{5,7},{6,4},{7,5},{8,10},{9,11},{10,... | collective-permute-start | bytes 1179656 | tf_op jit(solution)/shard_map/ppermute | solution.py:412
  156.4 34.0 %collective-permute-start.48 = (bf16[128,1536]{1,0:T(8,128)(2,1)S(1)}, bf16[128,1536]{1,0:T(8,128)(2,1)S(1)}, u32[]{:S(2)}, u32[]{:S(2)}) collective-permute-start(bf16[128,1536]{1,0:T(8,128)(2,1)S(1)} %get-tuple-element.104), channel_id=1, source_target_pairs={{0,3},{1,2},{2,1},{3,0},{4,7},{5,6},{6,5},{7,4},{8,11},{9,10},{10,... | collective-permute-start | bytes 1179656 | tf_op jit(solution)/shard_map/ppermute | solution.py:412
  158.1 28.7 %collective-permute-start.57 = (bf16[128,1152]{1,0:T(8,128)(2,1)S(1)}, bf16[128,1152]{1,0:T(8,128)(2,1)S(1)}, u32[]{:S(2)}, u32[]{:S(2)}) collective-permute-start(bf16[128,1152]{1,0:T(8,128)(2,1)S(1)} %get-tuple-element.117), channel_id=1, source_target_pairs={{0,3},{1,2},{2,1},{3,0},{4,7},{5,6},{6,5},{7,4},{8,11},{9,10},{10,... | collective-permute-start | bytes 884744 | tf_op jit(solution)/shard_map/ppermute | solution.py:412
  186.8 25.9 %collective-permute-start.50 = (bf16[128,1408]{1,0:T(8,128)(2,1)S(1)}, bf16[128,1408]{1,0:T(8,128)(2,1)S(1)}, u32[]{:S(2)}, u32[]{:S(2)}) collective-permute-start(bf16[128,1408]{1,0:T(8,128)(2,1)S(1)} %get-tuple-element.108), channel_id=1, source_target_pairs={{0,2},{1,3},{2,0},{3,1},{4,6},{5,7},{6,4},{7,5},{8,10},{9,11},{10,... | collective-permute-start | bytes 1081352 | tf_op jit(solution)/shard_map/ppermute | solution.py:412
  186.9 25.8 %collective-permute-start.51 = (bf16[128,1408]{1,0:T(8,128)(2,1)S(1)}, bf16[128,1408]{1,0:T(8,128)(2,1)S(1)}, u32[]{:S(2)}, u32[]{:S(2)}) collective-permute-start(bf16[128,1408]{1,0:T(8,128)(2,1)S(1)} %get-tuple-element.109), channel_id=1, source_target_pairs={{0,3},{1,2},{2,1},{3,0},{4,7},{5,6},{6,5},{7,4},{8,11},{9,10},{10,... | collective-permute-start | bytes 1081352 | tf_op jit(solution)/shard_map/ppermute | solution.py:412
  190.3 26.0 %collective-permute-start.53 = (bf16[128,1280]{1,0:T(8,128)(2,1)S(1)}, bf16[128,1280]{1,0:T(8,128)(2,1)S(1)}, u32[]{:S(2)}, u32[]{:S(2)}) collective-permute-start(bf16[128,1280]{1,0:T(8,128)(2,1)S(1)} %get-tuple-element.112), channel_id=1, source_target_pairs={{0,2},{1,3},{2,0},{3,1},{4,6},{5,7},{6,4},{7,5},{8,10},{9,11},{10,... | collective-permute-start | bytes 983048 | tf_op jit(solution)/shard_map/ppermute | solution.py:412
  190.4 26.0 %collective-permute-start.54 = (bf16[128,1280]{1,0:T(8,128)(2,1)S(1)}, bf16[128,1280]{1,0:T(8,128)(2,1)S(1)}, u32[]{:S(2)}, u32[]{:S(2)}) collective-permute-start(bf16[128,1280]{1,0:T(8,128)(2,1)S(1)} %get-tuple-element.113), channel_id=1, source_target_pairs={{0,3},{1,2},{2,1},{3,0},{4,7},{5,6},{6,5},{7,4},{8,11},{9,10},{10,... | collective-permute-start | bytes 983048 | tf_op jit(solution)/shard_map/ppermute | solution.py:412
  198.1 21.6 %collective-permute-start.79 = (bf16[128,256]{1,0:T(8,128)(2,1)S(1)}, bf16[128,256]{1,0:T(8,128)(2,1)S(1)}, u32[]{:S(2)}, u32[]{:S(2)}) collective-permute-start(bf16[128,256]{1,0:T(8,128)(2,1)S(1)} %get-tuple-element.146), channel_id=1, source_target_pairs={{0,4},{4,0},{8,12},{12,8},{16,20},{20,16},{24,28},{28,24},{1,5},{5... | collective-permute-start | bytes 196616 | tf_op jit(solution)/shard_map/ppermute | solution.py:421
  216.4 12.2 %collective-permute-start.83 = (bf16[128,256]{1,0:T(8,128)(2,1)S(1)}, bf16[128,256]{1,0:T(8,128)(2,1)S(1)}, u32[]{:S(2)}, u32[]{:S(2)}) collective-permute-start(bf16[128,256]{1,0:T(8,128)(2,1)S(1)} %get-tuple-element.150), channel_id=1, source_target_pairs={{0,20},{4,16},{8,28},{12,24},{16,4},{20,0},{24,12},{28,8},{1,21},{... | collective-permute-start | bytes 196616 | tf_op jit(solution)/shard_map/ppermute | solution.py:421
  251.2 15.4 %collective-permute-start.60 = (bf16[128,256]{1,0:T(8,128)(2,1)S(1)}, bf16[128,256]{1,0:T(8,128)(2,1)S(1)}, u32[]{:S(2)}, u32[]{:S(2)}) collective-permute-start(bf16[128,256]{1,0:T(8,128)(2,1)S(1)} %get-tuple-element.124), channel_id=1, source_target_pairs={{0,12},{4,8},{8,4},{12,0},{16,28},{20,24},{24,20},{28,16},{1,13},{... | collective-permute-start | bytes 196616 | tf_op jit(solution)/shard_map/ppermute | solution.py:421
  (61 other events, 573.7 us)

commit v4 on v3

--- a/solution.py
+++ b/solution.py
@@ -308,7 +308,9 @@
     n_mat, n_pts, act, nact = dims
     each = act // n_pts
     strips, before = refs[: (k + 1) * n_pts], refs[(k + 1) * n_pts : (k + 1) * n_pts + k]
-    out, (inner, total, table, held, sem) = refs[(k + 1) * n_pts + k : -5], refs[-5:]
+    final = k == each - 1
+    out, (total, table, held, sem) = refs[(k + 1) * n_pts + k : -4], refs[-4:]
+    inner = None if final else out[-1]
     me_pts = meta[1]
     first = me_pts * each
     ranks = []
@@ -338,7 +340,7 @@
 
     for r in range(k):
         total[:, lanes(first + r)] = before[r][:, k * BLOCK : (k + 1) * BLOCK].T
-    for r in range(each):
+    for r in range(k + 1, each):
         inner[:, r * BLOCK : (r + 1) * BLOCK] = total[:, lanes(first + r)]
     width = act // n_mat
     pattern_at = HEAD + n_pts * nact + (first + k) * act
@@ -353,7 +355,8 @@
 def combine(dims, k, meta, strips, before):
     n_mat, n_pts, act, nact = dims
     shapes = [jax.ShapeDtypeStruct((BLOCK, act // n_mat * BLOCK), jnp.bfloat16)] * n_mat
-    shapes += [jax.ShapeDtypeStruct((BLOCK, act // n_pts * BLOCK), jnp.float32)]
+    if k < act // n_pts - 1:
+        shapes += [jax.ShapeDtypeStruct((BLOCK, act // n_pts * BLOCK), jnp.float32)]
     given = sum(strips, [])
     out = pl.pallas_call(
         functools.partial(combine_kernel, dims, k),
@@ -369,7 +372,7 @@
         compiler_params=GRANT,
         cost_estimate=cost(0, 2 * BLOCK * BLOCK * (act + n_pts * nact)),
     )(meta, *given, *before)
-    return out[:-1], out[-1]
+    return out[:n_mat], out[n_mat:]
 
 
 def widen_kernel(n_mat, meta, *refs):
@@ -460,7 +463,7 @@
     inner, result = [], None
     for k in range(row_blocks):
         cut, pairs = combine(dims, k, meta, strips[: k + 1], inner)
-        inner.append(pairs)
+        inner += pairs
         back = across(cut)
         result = widen(dims, k * BLOCK, BLOCK, dens_blocks.shape[1], meta, back, result)
     return result, n_response

time: 271 us -> 270 us (level)
  transfers between devices with their start and end apart: 86 -> 86, of which waited for: 34 -> 35; matrix products, arithmetic and copies ran while one was open for 0% -> 0% of each run, Pallas kernels for 14% -> 14%
where the time goes in v4:
time: 270 us; the launch traced here: 269 us
  waiting for transfers between devices  121 us (45%)
  starting transfers between devices  87.3 us (32%)
  Pallas kernels  57.1 us (21%)
    ppermute x30, waiting for transfers between devices, to_peer(): return lax.ppermute(value, 'pts', [(i, i ^ o) for i in range(n_pts)])  76.7 us
    ppermute x56, starting transfers between devices, across(): out[d] = lax.ppermute(values[d], 'mat', [(i, i ^ d) for i in range(n_mat)])  53.6 us
    ppermute x56, waiting for transfers between devices, across(): out[d] = lax.ppermute(values[d], 'mat', [(i, i ^ d) for i in range(n_mat)])  44.6 us
    ppermute x30, starting transfers between devices, to_peer(): return lax.ppermute(value, 'pts', [(i, i ^ o) for i in range(n_pts)])  33.7 us
    pallas_call x4, Pallas kernels, density(): pl.pallas_call(functools.partial(density_kernel, dims, k, h, tile_of(poin...  15 us
    pallas_call x1, Pallas kernels, response(): pl.pallas_call(functools.partial(response_kernel, dims, ranks, tile_of(or...  11.3 us
    pallas_call x4, Pallas kernels, combine(): pl.pallas_call(functools.partial(combine_kernel, dims, k), out_shape=shap...  7.59 us
    pallas_call x4, Pallas kernels, pack(): pl.pallas_call(functools.partial(pack_kernel, dims, k, pieces), out_shape...  7.14 us
  transfers between devices with their start and end apart: 86, of which 35 were waited for; matrix products, arithmetic and copies ran while one was open for 0% of the time, Pallas kernels for 14%

profile of v4, /device:TPU:0, one launch (start us, length us, event | category | flops | bytes accessed | tf_op | source)
XLA Modules:
  0.0 269.3 jit_solution(12895940393953470768)
XLA Ops:
  2.5 4.6 %collective-permute-start.30 = (bf16[128,256]{1,0:T(8,128)(2,1)S(1)}, bf16[128,256]{1,0:T(8,128)(2,1)S(1)}, u32[]{:S(2)}, u32[]{:S(2)}) collective-permute-start(bf16[128,256]{1,0:T(8,128)(2,1)S(1)} %get-tuple-element.154), channel_id=1, source_target_pairs={{0,28},{4,24},{8,20},{12,16},{16,12},{20,8},{24,4},{28,0},{1,29},{... | collective-permute-start | bytes 196616 | tf_op jit(solution)/shard_map/ppermute | solution.py:424
  7.1 2.4 collective-permute-start.2
  15.0 2.8 %collective-permute-done.28.refs_5_ = bf16[128,256]{1,0:T(8,128)(2,1)S(1)} collective-permute-done((bf16[128,256]{1,0:T(8,128)(2,1)S(1)}, bf16[128,256]{1,0:T(8,128)(2,1)S(1)}, u32[]{:S(2)}, u32[]{:S(2)}) %collective-permute-start.28) | collective-permute-done | bytes 65568 | tf_op jit(solution)/shard_map/ppermute | solution.py:424
  22.5 2.5 collective-permute-start.15
  27.8 5.9 %collective-permute-done.21.refs_5_ = bf16[128,256]{1,0:T(8,128)(2,1)S(1)} collective-permute-done((bf16[128,256]{1,0:T(8,128)(2,1)S(1)}, bf16[128,256]{1,0:T(8,128)(2,1)S(1)}, u32[]{:S(2)}, u32[]{:S(2)}) %collective-permute-start.21) | collective-permute-done | bytes 65568 | tf_op jit(solution)/shard_map/ppermute | solution.py:424
  35.7 2.3 collective-permute-done.14.refs_5_
  42.4 3.5 %collective-permute-start.9 = (bf16[128,256]{1,0:T(8,128)(2,1)S(1)}, bf16[128,256]{1,0:T(8,128)(2,1)S(1)}, u32[]{:S(2)}, u32[]{:S(2)}) collective-permute-start(bf16[128,256]{1,0:T(8,128)(2,1)S(1)} %get-tuple-element.177), channel_id=1, source_target_pairs={{0,28},{4,24},{8,20},{12,16},{16,12},{20,8},{24,4},{28,0},{1,29},{... | collective-permute-start | bytes 196616 | tf_op jit(solution)/shard_map/ppermute | solution.py:424
  56.8 2.8 %collective-permute-done.7.refs_5_ = bf16[128,256]{1,0:T(8,128)(2,1)S(1)} collective-permute-done((bf16[128,256]{1,0:T(8,128)(2,1)S(1)}, bf16[128,256]{1,0:T(8,128)(2,1)S(1)}, u32[]{:S(2)}, u32[]{:S(2)}) %collective-permute-start.7) | collective-permute-done | bytes 65568 | tf_op jit(solution)/shard_map/ppermute | solution.py:424
  65.9 5.3 %collective-permute-done.29.refs_6_ = bf16[128,256]{1,0:T(8,128)(2,1)S(1)} collective-permute-done((bf16[128,256]{1,0:T(8,128)(2,1)S(1)}, bf16[128,256]{1,0:T(8,128)(2,1)S(1)}, u32[]{:S(2)}, u32[]{:S(2)}) %collective-permute-start.29) | collective-permute-done | bytes 65568 | tf_op jit(solution)/shard_map/ppermute | solution.py:424
  73.2 2.7 %flip.1.refs_4_.refs_0_ = bf16[1536,1536]{1,0:T(8,128)(2,1)S(1)} custom-call(bf16[1536,1536]{1,0:T(8,128)(2,1)} %bitcast.70), custom_call_target="tpu_custom_call" | custom-call | bytes 9437184 | tf_op jit(solution)/shard_map/flip/pallas_call | solution.py:142
  77.5 2.5 shard_map.98
  80.0 3.6 %collective-permute-done.44.refs_2_ = bf16[128,1152]{1,0:T(8,128)(2,1)S(1)} collective-permute-done((bf16[128,1152]{1,0:T(8,128)(2,1)S(1)}, bf16[128,1152]{1,0:T(8,128)(2,1)S(1)}, u32[]{:S(2)}, u32[]{:S(2)}) %collective-permute-start.44) | collective-permute-done | bytes 294944 | tf_op jit(solution)/shard_map/ppermute | solution.py:415
  87.2 4.2 %shard_map.99.refs_5_ = f32[1,1536]{1,0:T(1,128)S(1)} custom-call(s32[307]{0:T(512)S(1)} %concatenate.3.meta, bf16[128,1152]{1,0:T(8,128)(2,1)S(1)} %get-tuple-element.97.refs_0_, bf16[128,1152]{1,0:T(8,128)(2,1)S(1)} %collective-permute-done.43.refs_1_, bf16[128,1152]{1,0:T(8,128)(2,1)S(1)} %collective-permute-done.44.refs_2_, ...), custom_call_target="tpu_custom_call" | custom-call | flops 2415919104 | bytes 4718592 | tf_op jit(solution)/shard_map/pallas_call | solution.py:205
  94.1 4.0 %shard_map.100.refs_5_ = f32[1,1536]{1,0:T(1,128)S(1)} custom-call(s32[307]{0:T(512)S(1)} %concatenate.3.meta, bf16[128,1280]{1,0:T(8,128)(2,1)S(1)} %get-tuple-element.93.refs_0_, bf16[128,1280]{1,0:T(8,128)(2,1)S(1)} %collective-permute-done.40.refs_1_, bf16[128,1280]{1,0:T(8,128)(2,1)S(1)} %collective-permute-done.41.refs_2_, ...), custom_call_target="tpu_custom_call" | custom-call | flops 2415919104 | bytes 4718592 | tf_op jit(solution)/shard_map/pallas_call | solution.py:205
  98.1 9.5 %collective-permute-done.34.refs_1_ = bf16[64,1536]{1,0:T(8,128)(2,1)S(1)} collective-permute-done((bf16[64,1536]{1,0:T(8,128)(2,1)S(1)}, bf16[64,1536]{1,0:T(8,128)(2,1)S(1)}, u32[]{:S(2)}, u32[]{:S(2)}) %collective-permute-start.34) | collective-permute-done | bytes 196640 | tf_op jit(solution)/shard_map/ppermute | solution.py:415
  107.6 2.5 collective-permute-start.32
  113.1 4.0 %shard_map.101.refs_5_ = f32[1,1536]{1,0:T(1,128)S(1)} custom-call(s32[307]{0:T(512)S(1)} %concatenate.3.meta, bf16[128,1408]{1,0:T(8,128)(2,1)S(1)} %get-tuple-element.89.refs_0_, bf16[128,1408]{1,0:T(8,128)(2,1)S(1)} %collective-permute-done.37.refs_1_, bf16[128,1408]{1,0:T(8,128)(2,1)S(1)} %collective-permute-done.38.refs_2_, ...), custom_call_target="tpu_custom_call" | custom-call | flops 2415919104 | bytes 4718592 | tf_op jit(solution)/shard_map/pallas_call | solution.py:205
  117.2 8.2 %collective-permute-done.35.refs_2_ = bf16[64,1536]{1,0:T(8,128)(2,1)S(1)} collective-permute-done((bf16[64,1536]{1,0:T(8,128)(2,1)S(1)}, bf16[64,1536]{1,0:T(8,128)(2,1)S(1)}, u32[]{:S(2)}, u32[]{:S(2)}) %collective-permute-start.35) | collective-permute-done | bytes 196640 | tf_op jit(solution)/shard_map/ppermute | solution.py:415
  125.4 2.8 %shard_map.102.refs_5_ = f32[1,1536]{1,0:T(1,128)S(1)} custom-call(s32[307]{0:T(512)S(1)} %concatenate.3.meta, bf16[64,1536]{1,0:T(8,128)(2,1)S(1)} %get-tuple-element.85.refs_0_, bf16[64,1536]{1,0:T(8,128)(2,1)S(1)} %collective-permute-done.34.refs_1_, bf16[64,1536]{1,0:T(8,128)(2,1)S(1)} %collective-permute-done.35.refs_2_, ...), custom_call_target="tpu_custom_call" | custom-call | flops 1207959552 | bytes 4718592 | tf_op jit(solution)/shard_map/pallas_call | solution.py:205
  128.2 7.0 %turn.1 = (bf16[128,1536]{1,0:T(8,128)(2,1)S(1)}, bf16[128,1536]{1,0:T(8,128)(2,1)S(1)}, bf16[128,1536]{1,0:T(8,128)(2,1)S(1)}, bf16[128,1536]{1,0:T(8,128)(2,1)...) custom-call(s32[307]{0:T(512)S(1)} %concatenate.3.meta, bf16[64,1536]{1,0:T(8,128)(2,1)S(1)} %get-tuple-element.81.refs_0_, ...), custom_call_target="tpu_custom_call" | custom-call | flops 3623878656 | bytes 9437184 | tf_op jit(solution)/shard_map/turn/pallas_call | solution.py:235
  135.2 11.3 %shard_map.103 = (bf16[128,1408]{1,0:T(8,128)(2,1)S(1)}, bf16[128,1408]{1,0:T(8,128)(2,1)S(1)}, bf16[128,1408]{1,0:T(8,128)(2,1)S(1)}, bf16[128,1408]{1,0:T(8,12...) custom-call(s32[307]{0:T(512)S(1)} %concatenate.3.meta, ...), custom_call_target="tpu_custom_call" | custom-call | flops 7247757312 | bytes 9437184 | tf_op jit(solution)/shard_map/pallas_call | solution.py:290
  151.4 5.0 %collective-permute-done.55.refs_13_ = bf16[128,1152]{1,0:T(8,128)(2,1)S(1)} collective-permute-done((bf16[128,1152]{1,0:T(8,128)(2,1)S(1)}, bf16[128,1152]{1,0:T(8,128)(2,1)S(1)}, u32[]{:S(2)}, u32[]{:S(2)}) %collective-permute-start.55) | collective-permute-done | bytes 294944 | tf_op jit(solution)/shard_map/ppermute | solution.py:415
  159.6 27.2 %collective-permute-done.57.refs_15_ = bf16[128,1152]{1,0:T(8,128)(2,1)S(1)} collective-permute-done((bf16[128,1152]{1,0:T(8,128)(2,1)S(1)}, bf16[128,1152]{1,0:T(8,128)(2,1)S(1)}, u32[]{:S(2)}, u32[]{:S(2)}) %collective-permute-start.57) | collective-permute-done | bytes 294944 | tf_op jit(solution)/shard_map/ppermute | solution.py:415
  186.9 3.4 %collective-permute-start.51 = (bf16[128,1408]{1,0:T(8,128)(2,1)S(1)}, bf16[128,1408]{1,0:T(8,128)(2,1)S(1)}, u32[]{:S(2)}, u32[]{:S(2)}) collective-permute-start(bf16[128,1408]{1,0:T(8,128)(2,1)S(1)} %get-tuple-element.109), channel_id=1, source_target_pairs={{0,3},{1,2},{2,1},{3,0},{4,7},{5,6},{6,5},{7,4},{8,11},{9,10},{10,... | collective-permute-start | bytes 1081352 | tf_op jit(solution)/shard_map/ppermute | solution.py:415
  193.5 4.6 %collective-permute-done.49.refs_5_ = bf16[128,1408]{1,0:T(8,128)(2,1)S(1)} collective-permute-done((bf16[128,1408]{1,0:T(8,128)(2,1)S(1)}, bf16[128,1408]{1,0:T(8,128)(2,1)S(1)}, u32[]{:S(2)}, u32[]{:S(2)}) %collective-permute-start.49) | collective-permute-done | bytes 360480 | tf_op jit(solution)/shard_map/ppermute | solution.py:415
  198.1 14.7 %collective-permute-done.50.refs_6_ = bf16[128,1408]{1,0:T(8,128)(2,1)S(1)} collective-permute-done((bf16[128,1408]{1,0:T(8,128)(2,1)S(1)}, bf16[128,1408]{1,0:T(8,128)(2,1)S(1)}, u32[]{:S(2)}, u32[]{:S(2)}) %collective-permute-start.50) | collective-permute-done | bytes 360480 | tf_op jit(solution)/shard_map/ppermute | solution.py:415
  216.3 3.4 %collective-permute-start.83 = (bf16[128,256]{1,0:T(8,128)(2,1)S(1)}, bf16[128,256]{1,0:T(8,128)(2,1)S(1)}, u32[]{:S(2)}, u32[]{:S(2)}) collective-permute-start(bf16[128,256]{1,0:T(8,128)(2,1)S(1)} %get-tuple-element.150), channel_id=1, source_target_pairs={{0,20},{4,16},{8,28},{12,24},{16,4},{20,0},{24,12},{28,8},{1,21},{... | collective-permute-start | bytes 196616 | tf_op jit(solution)/shard_map/ppermute | solution.py:424
  219.8 2.6 collective-permute-start.85
  223.7 3.4 %collective-permute-done.82.refs_4_ = bf16[128,256]{1,0:T(8,128)(2,1)S(1)} collective-permute-done((bf16[128,256]{1,0:T(8,128)(2,1)S(1)}, bf16[128,256]{1,0:T(8,128)(2,1)S(1)}, u32[]{:S(2)}, u32[]{:S(2)}) %collective-permute-start.82) | collective-permute-done | bytes 65568 | tf_op jit(solution)/shard_map/ppermute | solution.py:424
  231.5 2.5 collective-permute-start.77
  250.4 4.4 %collective-permute-done.68.refs_4_ = bf16[128,256]{1,0:T(8,128)(2,1)S(1)} collective-permute-done((bf16[128,256]{1,0:T(8,128)(2,1)S(1)}, bf16[128,256]{1,0:T(8,128)(2,1)S(1)}, u32[]{:S(2)}, u32[]{:S(2)}) %collective-permute-start.68) | collective-permute-done | bytes 65568 | tf_op jit(solution)/shard_map/ppermute | solution.py:424
  258.6 2.4 collective-permute-start.64
  (179 shorter events, 99.7 us)
Async XLA Ops:
  2.5 12.5 %collective-permute-start.30 = (bf16[128,256]{1,0:T(8,128)(2,1)S(1)}, bf16[128,256]{1,0:T(8,128)(2,1)S(1)}, u32[]{:S(2)}, u32[]{:S(2)}) collective-permute-start(bf16[128,256]{1,0:T(8,128)(2,1)S(1)} %get-tuple-element.154), channel_id=1, source_target_pairs={{0,28},{4,24},{8,20},{12,16},{16,12},{20,8},{24,4},{28,0},{1,29},{... | collective-permute-start | bytes 196616 | tf_op jit(solution)/shard_map/ppermute | solution.py:424
  21.3 12.5 %collective-permute-start.21 = (bf16[128,256]{1,0:T(8,128)(2,1)S(1)}, bf16[128,256]{1,0:T(8,128)(2,1)S(1)}, u32[]{:S(2)}, u32[]{:S(2)}) collective-permute-start(bf16[128,256]{1,0:T(8,128)(2,1)S(1)} %get-tuple-element.163), channel_id=1, source_target_pairs={{0,20},{4,16},{8,28},{12,24},{16,4},{20,0},{24,12},{28,8},{1,21},{... | collective-permute-start | bytes 196616 | tf_op jit(solution)/shard_map/ppermute | solution.py:424
  22.5 13.3 %collective-permute-start.15 = (bf16[128,256]{1,0:T(8,128)(2,1)S(1)}, bf16[128,256]{1,0:T(8,128)(2,1)S(1)}, u32[]{:S(2)}, u32[]{:S(2)}) collective-permute-start(bf16[128,256]{1,0:T(8,128)(2,1)S(1)} %get-tuple-element.170), channel_id=1, source_target_pairs={{0,24},{4,28},{8,16},{12,20},{16,8},{20,12},{24,0},{28,4},{1,25},{... | collective-permute-start | bytes 196616 | tf_op jit(solution)/shard_map/ppermute | solution.py:424
  24.9 13.1 %collective-permute-start.14 = (bf16[128,256]{1,0:T(8,128)(2,1)S(1)}, bf16[128,256]{1,0:T(8,128)(2,1)S(1)}, u32[]{:S(2)}, u32[]{:S(2)}) collective-permute-start(bf16[128,256]{1,0:T(8,128)(2,1)S(1)} %get-tuple-element.171), channel_id=1, source_target_pairs={{0,20},{4,16},{8,28},{12,24},{16,4},{20,0},{24,12},{28,8},{1,21},{... | collective-permute-start | bytes 196616 | tf_op jit(solution)/shard_map/ppermute | solution.py:424
  26.0 13.5 %collective-permute-start.13 = (bf16[128,256]{1,0:T(8,128)(2,1)S(1)}, bf16[128,256]{1,0:T(8,128)(2,1)S(1)}, u32[]{:S(2)}, u32[]{:S(2)}) collective-permute-start(bf16[128,256]{1,0:T(8,128)(2,1)S(1)} %get-tuple-element.172), channel_id=1, source_target_pairs={{0,16},{4,20},{8,24},{12,28},{16,0},{20,4},{24,8},{28,12},{1,17},{... | collective-permute-start | bytes 196616 | tf_op jit(solution)/shard_map/ppermute | solution.py:424
  48.2 24.5 %collective-permute-start.43 = (bf16[128,1152]{1,0:T(8,128)(2,1)S(1)}, bf16[128,1152]{1,0:T(8,128)(2,1)S(1)}, u32[]{:S(2)}, u32[]{:S(2)}) collective-permute-start(bf16[128,1152]{1,0:T(8,128)(2,1)S(1)} %get-tuple-element.98), channel_id=1, source_target_pairs={{0,1},{1,0},{2,3},{3,2},{4,5},{5,4},{6,7},{7,6},{8,9},{9,8},{10,11... | collective-permute-start | bytes 884744 | tf_op jit(solution)/shard_map/ppermute | solution.py:415
  56.2 29.5 %collective-permute-start.40 = (bf16[128,1280]{1,0:T(8,128)(2,1)S(1)}, bf16[128,1280]{1,0:T(8,128)(2,1)S(1)}, u32[]{:S(2)}, u32[]{:S(2)}) collective-permute-start(bf16[128,1280]{1,0:T(8,128)(2,1)S(1)} %get-tuple-element.94), channel_id=1, source_target_pairs={{0,1},{1,0},{2,3},{3,2},{4,5},{5,4},{6,7},{7,6},{8,9},{9,8},{10,11... | collective-permute-start | bytes 983048 | tf_op jit(solution)/shard_map/ppermute | solution.py:415
  60.4 23.2 %collective-permute-start.44 = (bf16[128,1152]{1,0:T(8,128)(2,1)S(1)}, bf16[128,1152]{1,0:T(8,128)(2,1)S(1)}, u32[]{:S(2)}, u32[]{:S(2)}) collective-permute-start(bf16[128,1152]{1,0:T(8,128)(2,1)S(1)} %get-tuple-element.99), channel_id=1, source_target_pairs={{0,2},{1,3},{2,0},{3,1},{4,6},{5,7},{6,4},{7,5},{8,10},{9,11},{10,... | collective-permute-start | bytes 884744 | tf_op jit(solution)/shard_map/ppermute | solution.py:415
  62.0 22.2 %collective-permute-start.45 = (bf16[128,1152]{1,0:T(8,128)(2,1)S(1)}, bf16[128,1152]{1,0:T(8,128)(2,1)S(1)}, u32[]{:S(2)}, u32[]{:S(2)}) collective-permute-start(bf16[128,1152]{1,0:T(8,128)(2,1)S(1)} %get-tuple-element.100), channel_id=1, source_target_pairs={{0,3},{1,2},{2,1},{3,0},{4,7},{5,6},{6,5},{7,4},{8,11},{9,10},{10,... | collective-permute-start | bytes 884744 | tf_op jit(solution)/shard_map/ppermute | solution.py:415
  71.2 20.9 %collective-permute-start.41 = (bf16[128,1280]{1,0:T(8,128)(2,1)S(1)}, bf16[128,1280]{1,0:T(8,128)(2,1)S(1)}, u32[]{:S(2)}, u32[]{:S(2)}) collective-permute-start(bf16[128,1280]{1,0:T(8,128)(2,1)S(1)} %get-tuple-element.95), channel_id=1, source_target_pairs={{0,2},{1,3},{2,0},{3,1},{4,6},{5,7},{6,4},{7,5},{8,10},{9,11},{10,... | collective-permute-start | bytes 983048 | tf_op jit(solution)/shard_map/ppermute | solution.py:415
  72.7 19.9 %collective-permute-start.42 = (bf16[128,1280]{1,0:T(8,128)(2,1)S(1)}, bf16[128,1280]{1,0:T(8,128)(2,1)S(1)}, u32[]{:S(2)}, u32[]{:S(2)}) collective-permute-start(bf16[128,1280]{1,0:T(8,128)(2,1)S(1)} %get-tuple-element.96), channel_id=1, source_target_pairs={{0,3},{1,2},{2,1},{3,0},{4,7},{5,6},{6,5},{7,4},{8,11},{9,10},{10,... | collective-permute-start | bytes 983048 | tf_op jit(solution)/shard_map/ppermute | solution.py:415
  83.7 26.4 %collective-permute-start.37 = (bf16[128,1408]{1,0:T(8,128)(2,1)S(1)}, bf16[128,1408]{1,0:T(8,128)(2,1)S(1)}, u32[]{:S(2)}, u32[]{:S(2)}) collective-permute-start(bf16[128,1408]{1,0:T(8,128)(2,1)S(1)} %get-tuple-element.90), channel_id=1, source_target_pairs={{0,1},{1,0},{2,3},{3,2},{4,5},{5,4},{6,7},{7,6},{8,9},{9,8},{10,11... | collective-permute-start | bytes 1081352 | tf_op jit(solution)/shard_map/ppermute | solution.py:415
  84.2 25.9 %collective-permute-start.38 = (bf16[128,1408]{1,0:T(8,128)(2,1)S(1)}, bf16[128,1408]{1,0:T(8,128)(2,1)S(1)}, u32[]{:S(2)}, u32[]{:S(2)}) collective-permute-start(bf16[128,1408]{1,0:T(8,128)(2,1)S(1)} %get-tuple-element.91), channel_id=1, source_target_pairs={{0,2},{1,3},{2,0},{3,1},{4,6},{5,7},{6,4},{7,5},{8,10},{9,11},{10,... | collective-permute-start | bytes 1081352 | tf_op jit(solution)/shard_map/ppermute | solution.py:415
  85.7 26.4 %collective-permute-start.39 = (bf16[128,1408]{1,0:T(8,128)(2,1)S(1)}, bf16[128,1408]{1,0:T(8,128)(2,1)S(1)}, u32[]{:S(2)}, u32[]{:S(2)}) collective-permute-start(bf16[128,1408]{1,0:T(8,128)(2,1)S(1)} %get-tuple-element.92), channel_id=1, source_target_pairs={{0,3},{1,2},{2,1},{3,0},{4,7},{5,6},{6,5},{7,4},{8,11},{9,10},{10,... | collective-permute-start | bytes 1081352 | tf_op jit(solution)/shard_map/ppermute | solution.py:415
  92.0 36.1 %collective-permute-start.31 = (bf16[64,1536]{1,0:T(8,128)(2,1)S(1)}, bf16[64,1536]{1,0:T(8,128)(2,1)S(1)}, u32[]{:S(2)}, u32[]{:S(2)}) collective-permute-start(bf16[64,1536]{1,0:T(8,128)(2,1)S(1)} %get-tuple-element.82), channel_id=1, source_target_pairs={{0,1},{1,0},{2,3},{3,2},{4,5},{5,4},{6,7},{7,6},{8,9},{9,8},{10,11... | collective-permute-start | bytes 589832 | tf_op jit(solution)/shard_map/ppermute | solution.py:415
  92.6 15.0 %collective-permute-start.34 = (bf16[64,1536]{1,0:T(8,128)(2,1)S(1)}, bf16[64,1536]{1,0:T(8,128)(2,1)S(1)}, u32[]{:S(2)}, u32[]{:S(2)}) collective-permute-start(bf16[64,1536]{1,0:T(8,128)(2,1)S(1)} %get-tuple-element.86), channel_id=1, source_target_pairs={{0,1},{1,0},{2,3},{3,2},{4,5},{5,4},{6,7},{7,6},{8,9},{9,8},{10,11... | collective-permute-start | bytes 589832 | tf_op jit(solution)/shard_map/ppermute | solution.py:415
  107.6 20.6 %collective-permute-start.32 = (bf16[64,1536]{1,0:T(8,128)(2,1)S(1)}, bf16[64,1536]{1,0:T(8,128)(2,1)S(1)}, u32[]{:S(2)}, u32[]{:S(2)}) collective-permute-start(bf16[64,1536]{1,0:T(8,128)(2,1)S(1)} %get-tuple-element.83), channel_id=1, source_target_pairs={{0,2},{1,3},{2,0},{3,1},{4,6},{5,7},{6,4},{7,5},{8,10},{9,11},{10,... | collective-permute-start | bytes 589832 | tf_op jit(solution)/shard_map/ppermute | solution.py:415
  110.1 18.0 %collective-permute-start.33 = (bf16[64,1536]{1,0:T(8,128)(2,1)S(1)}, bf16[64,1536]{1,0:T(8,128)(2,1)S(1)}, u32[]{:S(2)}, u32[]{:S(2)}) collective-permute-start(bf16[64,1536]{1,0:T(8,128)(2,1)S(1)} %get-tuple-element.84), channel_id=1, source_target_pairs={{0,3},{1,2},{2,1},{3,0},{4,7},{5,6},{6,5},{7,4},{8,11},{9,10},{10,... | collective-permute-start | bytes 589832 | tf_op jit(solution)/shard_map/ppermute | solution.py:415
  110.1 15.2 %collective-permute-start.35 = (bf16[64,1536]{1,0:T(8,128)(2,1)S(1)}, bf16[64,1536]{1,0:T(8,128)(2,1)S(1)}, u32[]{:S(2)}, u32[]{:S(2)}) collective-permute-start(bf16[64,1536]{1,0:T(8,128)(2,1)S(1)} %get-tuple-element.87), channel_id=1, source_target_pairs={{0,2},{1,3},{2,0},{3,1},{4,6},{5,7},{6,4},{7,5},{8,10},{9,11},{10,... | collective-permute-start | bytes 589832 | tf_op jit(solution)/shard_map/ppermute | solution.py:415
  112.1 13.3 %collective-permute-start.36 = (bf16[64,1536]{1,0:T(8,128)(2,1)S(1)}, bf16[64,1536]{1,0:T(8,128)(2,1)S(1)}, u32[]{:S(2)}, u32[]{:S(2)}) collective-permute-start(bf16[64,1536]{1,0:T(8,128)(2,1)S(1)} %get-tuple-element.88), channel_id=1, source_target_pairs={{0,3},{1,2},{2,1},{3,0},{4,7},{5,6},{6,5},{7,4},{8,11},{9,10},{10,... | collective-permute-start | bytes 589832 | tf_op jit(solution)/shard_map/ppermute | solution.py:415
  148.8 38.1 %collective-permute-start.46 = (bf16[128,1536]{1,0:T(8,128)(2,1)S(1)}, bf16[128,1536]{1,0:T(8,128)(2,1)S(1)}, u32[]{:S(2)}, u32[]{:S(2)}) collective-permute-start(bf16[128,1536]{1,0:T(8,128)(2,1)S(1)} %get-tuple-element.102), channel_id=1, source_target_pairs={{0,1},{1,0},{2,3},{3,2},{4,5},{5,4},{6,7},{7,6},{8,9},{9,8},{10,11... | collective-permute-start | bytes 1179656 | tf_op jit(solution)/shard_map/ppermute | solution.py:415
  150.3 36.5 %collective-permute-start.52 = (bf16[128,1280]{1,0:T(8,128)(2,1)S(1)}, bf16[128,1280]{1,0:T(8,128)(2,1)S(1)}, u32[]{:S(2)}, u32[]{:S(2)}) collective-permute-start(bf16[128,1280]{1,0:T(8,128)(2,1)S(1)} %get-tuple-element.111), channel_id=1, source_target_pairs={{0,1},{1,0},{2,3},{3,2},{4,5},{5,4},{6,7},{7,6},{8,9},{9,8},{10,11... | collective-permute-start | bytes 983048 | tf_op jit(solution)/shard_map/ppermute | solution.py:415
  150.8 39.5 %collective-permute-start.47 = (bf16[128,1536]{1,0:T(8,128)(2,1)S(1)}, bf16[128,1536]{1,0:T(8,128)(2,1)S(1)}, u32[]{:S(2)}, u32[]{:S(2)}) collective-permute-start(bf16[128,1536]{1,0:T(8,128)(2,1)S(1)} %get-tuple-element.103), channel_id=1, source_target_pairs={{0,2},{1,3},{2,0},{3,1},{4,6},{5,7},{6,4},{7,5},{8,10},{9,11},{10,... | collective-permute-start | bytes 1179656 | tf_op jit(solution)/shard_map/ppermute | solution.py:415
  156.4 34.0 %collective-permute-start.48 = (bf16[128,1536]{1,0:T(8,128)(2,1)S(1)}, bf16[128,1536]{1,0:T(8,128)(2,1)S(1)}, u32[]{:S(2)}, u32[]{:S(2)}) collective-permute-start(bf16[128,1536]{1,0:T(8,128)(2,1)S(1)} %get-tuple-element.104), channel_id=1, source_target_pairs={{0,3},{1,2},{2,1},{3,0},{4,7},{5,6},{6,5},{7,4},{8,11},{9,10},{10,... | collective-permute-start | bytes 1179656 | tf_op jit(solution)/shard_map/ppermute | solution.py:415
  158.1 28.7 %collective-permute-start.57 = (bf16[128,1152]{1,0:T(8,128)(2,1)S(1)}, bf16[128,1152]{1,0:T(8,128)(2,1)S(1)}, u32[]{:S(2)}, u32[]{:S(2)}) collective-permute-start(bf16[128,1152]{1,0:T(8,128)(2,1)S(1)} %get-tuple-element.117), channel_id=1, source_target_pairs={{0,3},{1,2},{2,1},{3,0},{4,7},{5,6},{6,5},{7,4},{8,11},{9,10},{10,... | collective-permute-start | bytes 884744 | tf_op jit(solution)/shard_map/ppermute | solution.py:415
  186.8 25.9 %collective-permute-start.50 = (bf16[128,1408]{1,0:T(8,128)(2,1)S(1)}, bf16[128,1408]{1,0:T(8,128)(2,1)S(1)}, u32[]{:S(2)}, u32[]{:S(2)}) collective-permute-start(bf16[128,1408]{1,0:T(8,128)(2,1)S(1)} %get-tuple-element.108), channel_id=1, source_target_pairs={{0,2},{1,3},{2,0},{3,1},{4,6},{5,7},{6,4},{7,5},{8,10},{9,11},{10,... | collective-permute-start | bytes 1081352 | tf_op jit(solution)/shard_map/ppermute | solution.py:415
  186.9 25.8 %collective-permute-start.51 = (bf16[128,1408]{1,0:T(8,128)(2,1)S(1)}, bf16[128,1408]{1,0:T(8,128)(2,1)S(1)}, u32[]{:S(2)}, u32[]{:S(2)}) collective-permute-start(bf16[128,1408]{1,0:T(8,128)(2,1)S(1)} %get-tuple-element.109), channel_id=1, source_target_pairs={{0,3},{1,2},{2,1},{3,0},{4,7},{5,6},{6,5},{7,4},{8,11},{9,10},{10,... | collective-permute-start | bytes 1081352 | tf_op jit(solution)/shard_map/ppermute | solution.py:415
  190.3 26.0 %collective-permute-start.53 = (bf16[128,1280]{1,0:T(8,128)(2,1)S(1)}, bf16[128,1280]{1,0:T(8,128)(2,1)S(1)}, u32[]{:S(2)}, u32[]{:S(2)}) collective-permute-start(bf16[128,1280]{1,0:T(8,128)(2,1)S(1)} %get-tuple-element.112), channel_id=1, source_target_pairs={{0,2},{1,3},{2,0},{3,1},{4,6},{5,7},{6,4},{7,5},{8,10},{9,11},{10,... | collective-permute-start | bytes 983048 | tf_op jit(solution)/shard_map/ppermute | solution.py:415
  190.4 26.0 %collective-permute-start.54 = (bf16[128,1280]{1,0:T(8,128)(2,1)S(1)}, bf16[128,1280]{1,0:T(8,128)(2,1)S(1)}, u32[]{:S(2)}, u32[]{:S(2)}) collective-permute-start(bf16[128,1280]{1,0:T(8,128)(2,1)S(1)} %get-tuple-element.113), channel_id=1, source_target_pairs={{0,3},{1,2},{2,1},{3,0},{4,7},{5,6},{6,5},{7,4},{8,11},{9,10},{10,... | collective-permute-start | bytes 983048 | tf_op jit(solution)/shard_map/ppermute | solution.py:415
  198.1 21.6 %collective-permute-start.79 = (bf16[128,256]{1,0:T(8,128)(2,1)S(1)}, bf16[128,256]{1,0:T(8,128)(2,1)S(1)}, u32[]{:S(2)}, u32[]{:S(2)}) collective-permute-start(bf16[128,256]{1,0:T(8,128)(2,1)S(1)} %get-tuple-element.146), channel_id=1, source_target_pairs={{0,4},{4,0},{8,12},{12,8},{16,20},{20,16},{24,28},{28,24},{1,5},{5... | collective-permute-start | bytes 196616 | tf_op jit(solution)/shard_map/ppermute | solution.py:424
  216.3 12.2 %collective-permute-start.83 = (bf16[128,256]{1,0:T(8,128)(2,1)S(1)}, bf16[128,256]{1,0:T(8,128)(2,1)S(1)}, u32[]{:S(2)}, u32[]{:S(2)}) collective-permute-start(bf16[128,256]{1,0:T(8,128)(2,1)S(1)} %get-tuple-element.150), channel_id=1, source_target_pairs={{0,20},{4,16},{8,28},{12,24},{16,4},{20,0},{24,12},{28,8},{1,21},{... | collective-permute-start | bytes 196616 | tf_op jit(solution)/shard_map/ppermute | solution.py:424
  250.4 15.4 %collective-permute-start.60 = (bf16[128,256]{1,0:T(8,128)(2,1)S(1)}, bf16[128,256]{1,0:T(8,128)(2,1)S(1)}, u32[]{:S(2)}, u32[]{:S(2)}) collective-permute-start(bf16[128,256]{1,0:T(8,128)(2,1)S(1)} %get-tuple-element.124), channel_id=1, source_target_pairs={{0,12},{4,8},{8,4},{12,0},{16,28},{20,24},{24,20},{28,16},{1,13},{... | collective-permute-start | bytes 196616 | tf_op jit(solution)/shard_map/ppermute | solution.py:424
  (61 other events, 570.0 us)
